TPU v7x, 32 devices: a whole 2x2x4 slice. The times are simulated.
32 devices in a mesh: dp: 8 (over z, x), tensor: 4 (over y, core).
Axes of the slice: x: 2, y: 2, z: 4, core: 2. Of those that a mesh axis runs over, the one named last changes fastest.
Arguments:
- text_embed: bfloat16 [32, 384, 768], P('dp'), may hold values from -6 to 6
- region_feats: bfloat16 [3072, 2048], P('dp', 'tensor'), may hold values from -6 to 6
- box_coords: int32 [3072, 4], P('dp'), may hold values from 0 to 127
- seg_ids: int32 [32, 512], P('dp'), may hold values from 0 to 5, never falling along the last dimension, each value on 1 to 256 neighbouring positions
- region_counts: int32 [32], P('dp'), may hold values from 1 to 128, as said below
- send_index: int32 [8, 8, 96], P('dp'), may hold values from -1 to 383, as said below
- recv_pos: int32 [8, 8, 96], P('dp'), may hold values from -1 to 2047, as said below
- w_proj: bfloat16 [2048, 768], P('tensor'), may hold values from -0.125 to 0.125
- box_table: bfloat16 [4, 128, 768], replicated, may hold values from -1.75 to 1.75
- type_embed: bfloat16 [2, 768], replicated, may hold values from -3 to 3
- pos_embed: bfloat16 [512, 768], replicated, may hold values from -3 to 3
- gain_embed: float32 [768], replicated, may hold values from 0.5 to 1.5
- bias_embed: float32 [768], replicated, may hold values from -1.75 to 1.75
- w_qkv: bfloat16 [3, 768, 768], P(None, None, 'tensor'), may hold values from -0.21875 to 0.21875
- w_mix: bfloat16 [768, 768], P('tensor'), may hold values from -1.75 to 1.75
- gain_mid: float32 [768], replicated, may hold values from 0.5 to 1.5
- bias_mid: float32 [768], replicated, may hold values from -1.75 to 1.75
- w_up: bfloat16 [768, 3072], P(None, 'tensor'), may hold values from -0.21875 to 0.21875
- w_down: bfloat16 [3072, 768], P('tensor'), may hold values from -0.15625 to 0.15625
- gain_final: float32 [768], replicated, may hold values from 0.5 to 1.5
- bias_final: float32 [768], replicated, may hold values from -1.75 to 1.75
- cotangent: bfloat16 [32, 512, 768], P('dp'), may hold values from -8 to 8
Outputs:
- layer_output: bfloat16 [32, 512, 768], P('dp')
- text_grad: float32 [32, 384, 768], P('dp')
- feat_grad: float32 [3072, 2048], P('dp', 'tensor')
- grad_proj: float32 [2048, 768], P('tensor', 'dp')
- grad_box: float32 [4, 128, 768], P(None, 'dp')
- grad_type: float32 [2, 768], P(None, 'dp')
- grad_pos: float32 [512, 768], P('dp')
- grad_gain_embed: float32 [768], P('dp')
- grad_bias_embed: float32 [768], P('dp')
- grad_qkv: float32 [3, 768, 768], P(None, 'dp', 'tensor')
- grad_mix: float32 [768, 768], P('tensor', 'dp')
- grad_gain_mid: float32 [768], P('dp')
- grad_bias_mid: float32 [768], P('dp')
- grad_up: float32 [768, 3072], P('dp', 'tensor')
- grad_down: float32 [3072, 768], P('tensor', 'dp')
- grad_gain_final: float32 [768], P('dp')
- grad_bias_final: float32 [768], P('dp')
Inputs may be any that keep to these rules, and one draw needn't show every extreme that they name: `seg_ids`: each row holds 6 documents; ids never fall along a row. `region_counts`: the 4 rows of each device hold 384 regions in all, and one of them holds 128. `send_index`: entry [s, d, c] is the index, among device s's 384 stored regions, of the c-th region that device s sends to device d, or -1; every stored region is named once; for each pair the named entries come first and are even in number, at most 96, and every device sends exactly 96 to some device. `recv_pos`: entry [d, s, c] is the token, among device d's 4 * 512 tokens numbered row by row, that receives the region named by send_index[s, d, c], and -1 exactly where that entry is -1; the tokens named are the region tokens of device d's rows, position 384 + q of a row with q below its region count, each once.
All inputs are finite; a program needn't handle non-finite values.
Results may differ from a plain program's by a relative error of at most 0.03.
Values may be sent and summed in bfloat16 or wider, within the bound.
No kernel may reach another device: no remote copies, remote signals or barrier semaphores. Data moves between devices by JAX's collectives and lax.ppermute only.
A program may use at most 192 MiB of HBM per device.

v0:
```python
import jax
import jax.numpy as jnp
from jax import lax
from jax.sharding import PartitionSpec as P

HD = 64
LT = 384


EPSILON = 1e-06
NEGATIVE = -1000000000.0


def layer_norm(values, gain, bias):
    mean = jnp.mean(values, axis=-1, keepdims=True)
    centred = values - mean
    variance = jnp.mean(centred * centred, axis=-1, keepdims=True)
    inverse = lax.rsqrt(variance + EPSILON)
    normed = centred * inverse
    return (normed * gain + bias, normed, inverse)


def norm_back(grad, normed, inverse, gain):
    scaled = grad * gain
    mean_grad = jnp.mean(scaled, axis=-1, keepdims=True)
    mean_proj = jnp.mean(scaled * normed, axis=-1, keepdims=True)
    grad_in = inverse * (scaled - mean_grad - normed * mean_proj)
    return (grad_in, jnp.sum(grad * normed, axis=0), jnp.sum(grad, axis=0))


def key_mask(seg_row, count):
    length = seg_row.shape[0]
    places = jnp.arange(length, dtype=jnp.int32)
    usable = places < LT + count
    same = seg_row[:, None] == seg_row[None, :]
    return same & (usable[None, :] | (places[:, None] == places[None, :]))


def masked_scores(queries, keys, seg_row, count):
    scale = queries.shape[-1] ** (-0.5)
    scores = jnp.einsum("qhd,khd->hqk", queries, keys, preferred_element_type=jnp.float32) * scale
    return jnp.where(key_mask(seg_row, count)[None], scores, NEGATIVE)


def attend_item(item):
    queries, keys, values, seg_row, count = item
    scores = masked_scores(queries, keys, seg_row, count)
    top = jnp.max(scores, axis=-1, keepdims=True)
    total = jnp.sum(jnp.exp(scores - top), axis=-1, keepdims=True)
    logsum = top + jnp.log(total)
    probs = jnp.exp(scores - logsum)
    context = jnp.einsum(
        "hqk,khd->qhd", probs.astype(jnp.bfloat16), values, preferred_element_type=jnp.float32
    )
    return (context.astype(jnp.bfloat16), logsum[..., 0])


def back_item(item):
    queries, keys, values, grad_context, logsum, seg_row, count = item
    scale = queries.shape[-1] ** (-0.5)
    scores = masked_scores(queries, keys, seg_row, count)
    probs = jnp.exp(scores - logsum[..., None])
    grad_probs = jnp.einsum(
        "qhd,khd->hqk", grad_context, values, preferred_element_type=jnp.float32
    )
    inner = jnp.sum(probs * grad_probs, axis=-1, keepdims=True)
    grad_scores = (probs * (grad_probs - inner)).astype(jnp.bfloat16)
    grad_queries = (
        jnp.einsum("hqk,khd->qhd", grad_scores, keys, preferred_element_type=jnp.float32) * scale
    ).astype(jnp.bfloat16)
    grad_keys = (
        jnp.einsum("hqk,qhd->khd", grad_scores, queries, preferred_element_type=jnp.float32) * scale
    ).astype(jnp.bfloat16)
    grad_values = jnp.einsum(
        "hqk,qhd->khd", probs.astype(jnp.bfloat16), grad_context, preferred_element_type=jnp.float32
    ).astype(jnp.bfloat16)
    return (grad_queries, grad_keys, grad_values)


def local(
    text_embed,
    region_feats,
    box_coords,
    seg_ids,
    region_counts,
    send_index,
    recv_pos,
    w_proj,
    box_table,
    type_embed,
    pos_embed,
    gain_embed,
    bias_embed,
    w_qkv,
    w_mix,
    gain_mid,
    bias_mid,
    w_up,
    w_down,
    gain_final,
    bias_final,
    cotangent,
):
    row_count, text_len, width = text_embed.shape
    length = seg_ids.shape[1]
    tokens = row_count * length
    stored = region_feats.shape[0]
    peers = send_index.shape[1]
    capacity = send_index.shape[2]
    bins = box_table.shape[1]
    heads_here = w_qkv.shape[2] // HD
    partial_value = jnp.dot(region_feats, w_proj, preferred_element_type=jnp.float32)
    corners = (box_coords.T[:, :, None] == jnp.arange(bins, dtype=jnp.int32)[None, None, :]).astype(
        jnp.bfloat16
    )
    boxed = jnp.einsum("csb,cbd->sd", corners, box_table, preferred_element_type=jnp.float32)
    sources = send_index[0]
    filled = sources >= 0
    picks = jnp.maximum(sources, 0)
    projected = lax.psum(partial_value.astype(jnp.bfloat16), "tensor").astype(jnp.float32)
    rows_low = (projected + boxed).astype(jnp.bfloat16)
    outgoing = jnp.where(filled[:, :, None], rows_low[picks], jnp.zeros((), jnp.bfloat16))
    incoming = lax.all_to_all(outgoing, "dp", split_axis=0, concat_axis=0, tiled=True)
    targets = recv_pos[0].reshape(-1)
    spots = jnp.where(targets >= 0, targets, tokens)
    placed = (
        jnp.zeros((tokens, width), jnp.bfloat16)
        .at[spots]
        .set(incoming.reshape(-1, width), mode="drop")
    )
    text_part = text_embed.astype(jnp.float32) + type_embed[0].astype(jnp.float32)
    region_part = placed.reshape(row_count, length, width)[:, text_len:].astype(
        jnp.float32
    ) + type_embed[1].astype(jnp.float32)
    embedded = (
        jnp.concatenate([text_part, region_part], axis=1) + pos_embed.astype(jnp.float32)[None]
    )
    hidden0, normed0, inverse0 = layer_norm(embedded.reshape(tokens, width), gain_embed, bias_embed)
    inputs0 = hidden0.astype(jnp.bfloat16)
    mixed = jnp.einsum("td,cde->cte", inputs0, w_qkv, preferred_element_type=jnp.float32).astype(
        jnp.bfloat16
    )
    heads_view = mixed.reshape(3, row_count, length, heads_here, HD)
    context, logsum = lax.map(
        attend_item, (heads_view[0], heads_view[1], heads_view[2], seg_ids, region_counts)
    )
    context = context.reshape(tokens, heads_here * HD)
    attn = lax.psum(
        jnp.dot(context, w_mix, preferred_element_type=jnp.float32).astype(jnp.bfloat16), "tensor"
    ).astype(jnp.float32)
    hidden1, normed1, inverse1 = layer_norm(hidden0 + attn, gain_mid, bias_mid)
    inputs1 = hidden1.astype(jnp.bfloat16)
    before = jnp.dot(inputs1, w_up, preferred_element_type=jnp.float32)
    active = jax.nn.gelu(before, approximate=False).astype(jnp.bfloat16)
    ffn = lax.psum(
        jnp.dot(active, w_down, preferred_element_type=jnp.float32).astype(jnp.bfloat16), "tensor"
    ).astype(jnp.float32)
    final, normed2, inverse2 = layer_norm(hidden1 + ffn, gain_final, bias_final)
    layer_output = final.astype(jnp.bfloat16).reshape(row_count, length, width)
    grad_final = cotangent.astype(jnp.float32).reshape(tokens, width)
    grad_x2, grad_gain_final, grad_bias_final = norm_back(grad_final, normed2, inverse2, gain_final)
    grad_ffn = grad_x2.astype(jnp.bfloat16)
    grad_down = jnp.einsum("tf,td->fd", active, grad_ffn, preferred_element_type=jnp.float32)
    grad_active = jnp.einsum("td,fd->tf", grad_ffn, w_down, preferred_element_type=jnp.float32)
    slope = jax.vjp(lambda value: jax.nn.gelu(value, approximate=False), before)[1]
    grad_before = slope(grad_active)[0].astype(jnp.bfloat16)
    grad_up = jnp.einsum("td,tf->df", inputs1, grad_before, preferred_element_type=jnp.float32)
    back_one = lax.psum(
        jnp.einsum("tf,df->td", grad_before, w_up, preferred_element_type=jnp.float32).astype(
            jnp.bfloat16
        ),
        "tensor",
    ).astype(jnp.float32)
    grad_x1, grad_gain_mid, grad_bias_mid = norm_back(
        grad_x2 + back_one, normed1, inverse1, gain_mid
    )
    grad_attn = grad_x1.astype(jnp.bfloat16)
    grad_mix = jnp.einsum("te,td->ed", context, grad_attn, preferred_element_type=jnp.float32)
    grad_context = jnp.einsum(
        "td,ed->te", grad_attn, w_mix, preferred_element_type=jnp.float32
    ).astype(jnp.bfloat16)
    grad_context = grad_context.reshape(row_count, length, heads_here, HD)
    grad_heads = lax.map(
        back_item,
        (heads_view[0], heads_view[1], heads_view[2], grad_context, logsum, seg_ids, region_counts),
    )
    grad_mixed = jnp.stack(grad_heads).reshape(3, tokens, heads_here * HD)
    grad_qkv = jnp.einsum("td,cte->cde", inputs0, grad_mixed, preferred_element_type=jnp.float32)
    back_zero = lax.psum(
        jnp.einsum("cte,cde->td", grad_mixed, w_qkv, preferred_element_type=jnp.float32).astype(
            jnp.bfloat16
        ),
        "tensor",
    ).astype(jnp.float32)
    grad_embedded, grad_gain_embed, grad_bias_embed = norm_back(
        grad_x1 + back_zero, normed0, inverse0, gain_embed
    )
    grad_rows = grad_embedded.reshape(row_count, length, width)
    text_grad = grad_rows[:, :text_len]
    grad_type = jnp.stack(
        [jnp.sum(text_grad, axis=(0, 1)), jnp.sum(grad_rows[:, text_len:], axis=(0, 1))]
    )
    grad_pos = jnp.sum(grad_rows, axis=0)
    returning = jnp.where((targets >= 0)[:, None], grad_embedded[jnp.maximum(targets, 0)], 0.0)
    returning = returning.astype(jnp.bfloat16).reshape(peers, capacity, width)
    returned = lax.all_to_all(returning, "dp", split_axis=0, concat_axis=0, tiled=True)
    landing = jnp.where(filled, sources, stored).reshape(-1)
    grad_regions = (
        jnp.zeros((stored, width), jnp.bfloat16)
        .at[landing]
        .set(returned.reshape(-1, width), mode="drop")
    )
    grad_proj = jnp.einsum(
        "sf,sd->fd", region_feats, grad_regions, preferred_element_type=jnp.float32
    )
    feat_grad = jnp.einsum("sd,fd->sf", grad_regions, w_proj, preferred_element_type=jnp.float32)
    grad_box = jnp.einsum("csb,sd->cbd", corners, grad_regions, preferred_element_type=jnp.float32)
    sums = (
        lax.psum_scatter(grad_proj, "dp", scatter_dimension=1, tiled=True),
        lax.psum_scatter(grad_box, "dp", scatter_dimension=1, tiled=True),
        lax.psum_scatter(grad_type, "dp", scatter_dimension=1, tiled=True),
        lax.psum_scatter(grad_pos, "dp", scatter_dimension=0, tiled=True),
        lax.psum_scatter(grad_gain_embed, "dp", scatter_dimension=0, tiled=True),
        lax.psum_scatter(grad_bias_embed, "dp", scatter_dimension=0, tiled=True),
        lax.psum_scatter(grad_qkv, "dp", scatter_dimension=1, tiled=True),
        lax.psum_scatter(grad_mix, "dp", scatter_dimension=1, tiled=True),
        lax.psum_scatter(grad_gain_mid, "dp", scatter_dimension=0, tiled=True),
        lax.psum_scatter(grad_bias_mid, "dp", scatter_dimension=0, tiled=True),
        lax.psum_scatter(grad_up, "dp", scatter_dimension=0, tiled=True),
        lax.psum_scatter(grad_down, "dp", scatter_dimension=1, tiled=True),
        lax.psum_scatter(grad_gain_final, "dp", scatter_dimension=0, tiled=True),
        lax.psum_scatter(grad_bias_final, "dp", scatter_dimension=0, tiled=True),
    )
    sum_box = sums[1]
    sum_pos = sums[3]
    return (
        layer_output,
        text_grad,
        feat_grad,
        sums[0],
        sum_box,
        sums[2],
        sum_pos,
        sums[4],
        sums[5],
        sums[6],
        sums[7],
        sums[8],
        sums[9],
        sums[10],
        sums[11],
        sums[12],
        sums[13],
    )


def solution(mesh):
    return jax.shard_map(
        local,
        mesh=mesh,
        in_specs=(
            P("dp", None, None),
            P("dp", "tensor"),
            P("dp", None),
            P("dp", None),
            P("dp"),
            P("dp", None, None),
            P("dp", None, None),
            P("tensor", None),
            P(),
            P(),
            P(),
            P(),
            P(),
            P(None, None, "tensor"),
            P("tensor", None),
            P(),
            P(),
            P(None, "tensor"),
            P("tensor", None),
            P(),
            P(),
            P("dp", None, None),
        ),
        out_specs=(
            P("dp", None, None),
            P("dp", None, None),
            P("dp", "tensor"),
            P("tensor", "dp"),
            P(None, "dp", None),
            P(None, "dp"),
            P("dp", None),
            P("dp"),
            P("dp"),
            P(None, "dp", "tensor"),
            P("tensor", "dp"),
            P("dp"),
            P("dp"),
            P("dp", "tensor"),
            P("tensor", "dp"),
            P("dp"),
            P("dp"),
        ),
        check_vma=False,
    )
```

profile of v0, /device:TPU:0, one launch (start us, length us, event | category | flops | bytes accessed | tf_op | source)
XLA Modules:
  0.0 1116.4 jit_solution(7481657063689769484)
XLA Ops:
  11.4 35.8 %all-reduce.13.cloned.1.call-done = bf16[384,768]{1,0:T(8,128)(2,1)} async-done(((bf16[384,768]{1,0:T(8,128)(2,1)}), bf16[384,768]{1,0:T(8,128)(2,1)}) %all-reduce.13.cloned.1.call-update) | async-done | bytes 589840 | tf_op jit(solution)/shard_map/psum | solution.py:120
  64.8 21.7 %all-to-all-done = bf16[8,96,768]{2,1,0:T(8,128)(2,1)} async-done(((bf16[8,96,768]{2,1,0:T(8,128)(2,1)}), bf16[8,96,768]{2,1,0:T(8,128)(2,1)}, u32[]{:S(2)}, u32[]{:S(2)}) %all-to-all-start) | async-done | bytes 1179680 | tf_op jit(solution)/shard_map/all_to_all | solution.py:123
  86.5 8.5 scatter_custom_fusion
  113.8 26.5 %while.26 = (s32[]{:T(128)}, bf16[4,512,3,64]{1,3,2,0:T(8,128)(2,1)}, f32[4,3,512]{2,1,0:T(4,128)}, bf16[4,512,3,64]{1,3,2,0:T(8,128)(2,1)S(1)}, s32[4,512]{1,0:...) while((s32[]{:T(128)}, ...), condition=%wide.region_7.8_spmd, body=%wide.region_4.7_spmd.sunk | while | flops 211123200 | bytes 11335301 | solution.py:144
  147.3 66.0 %all-reduce.15.cloned.1.call-done = bf16[2048,768]{1,0:T(8,128)(2,1)} async-done(((bf16[2048,768]{1,0:T(8,128)(2,1)}), bf16[2048,768]{1,0:T(8,128)(2,1)}) %all-reduce.15.cloned.1.call-update) | async-done | bytes 3145744 | tf_op jit(solution)/shard_map/psum | solution.py:148
  220.8 18.1 %multiply_convert_fusion.1 = (bf16[2048,768]{1,0:T(8,128)(2,1)S(1)}, f32[2048,768]{1,0:T(8,128)}, f32[2048,768]{1,0:T(8,128)}) fusion(bf16[2048,768]{1,0:T(8,128)(2,1)S(1)} %fusion.73, bf16[768,768]{1,0:T(8,128)(2,1)S(1)} %copy-done), kind=kOutput, calls=%fused_computation.102 | convolution fusion | flops 2518155264 | bytes 20054016 | tf_op jit(solution)/shard_map/dot_general | solution.py:153
  249.2 64.0 %all-reduce.17.cloned.1.call-done = bf16[2048,768]{1,0:T(8,128)(2,1)} async-done(((bf16[2048,768]{1,0:T(8,128)(2,1)}), bf16[2048,768]{1,0:T(8,128)(2,1)}) %all-reduce.17.cloned.1.call-update) | async-done | bytes 3145744 | tf_op jit(solution)/shard_map/psum | solution.py:155
  326.8 8.6 add_convert_fusion
  341.4 68.5 %all-reduce.19.cloned.1.call-done = bf16[2048,768]{1,0:T(8,128)(2,1)} async-done(((bf16[2048,768]{1,0:T(8,128)(2,1)}), bf16[2048,768]{1,0:T(8,128)(2,1)}) %all-reduce.19.cloned.1.call-update) | async-done | bytes 3145744 | tf_op jit(solution)/shard_map/psum | solution.py:168
  409.9 8.6 multiply_reduce_fusion.1
  434.1 37.0 %while.27 = (s32[]{:T(128)}, bf16[4,512,3,64]{1,3,2,0:T(8,128)(2,1)}, bf16[4,512,3,64]{1,3,2,0:T(8,128)(2,1)}, bf16[4,512,3,64]{1,3,2,0:T(8,128)(2,1)}, bf16[4,5...) while((s32[]{:T(128)}, ...), condition=%wide.region_21.22_spmd, body=%wide.region_19.21_spmd.sunk | while | flops 511933440 | bytes 26128544 | solution.py:183
  492.4 63.6 %all-reduce.21.cloned.1.call-done = bf16[2048,768]{1,0:T(8,128)(2,1)} async-done(((bf16[2048,768]{1,0:T(8,128)(2,1)}), bf16[2048,768]{1,0:T(8,128)(2,1)}) %all-reduce.21.cloned.1.call-update) | async-done | bytes 3145744 | tf_op jit(solution)/shard_map/psum | solution.py:189
  556.0 7.1 multiply_reduce_fusion.2
  587.1 7.9 fusion.79
  595.0 7.0 fusion.114
  620.3 29.6 %all-to-all-done.1 = bf16[8,96,768]{2,1,0:T(8,128)(2,1)} async-done(((bf16[8,96,768]{2,1,0:T(8,128)(2,1)}), bf16[8,96,768]{2,1,0:T(8,128)(2,1)}, u32[]{:S(2)}, u32[]{:S(2)}) %all-to-all-start.1) | async-done | bytes 1179680 | tf_op jit(solution)/shard_map/all_to_all | solution.py:206
  649.9 6.4 scatter_custom_fusion.1
  662.9 35.4 %all-reduce.6 = (f32[768]{0:T(1024)S(1)}, f32[768]{0:T(1024)S(1)}, f32[768]{0:T(1024)S(1)}, f32[768]{0:T(1024)S(1)}, f32[768]{0:T(1024)S(1)}, /*index=5*/f32[768]{0:T(1024)S(1)}) all-reduce(f32[768]{0:T(1024)S(1)} %get-tuple-element.234, f32[768]{0:T(1024)S(1)} %get-tuple-element.241, ...), channel_id=6, replica_groups=mesh['dp'=8,'tensor'=4] {'dp'}, use_global_device_ids=true, to_apply=%region_34.35.clone | all-reduce | flops 4608 | bytes 36864
  703.3 58.2 %reduce-scatter.27.cloned.1.call-done = f32[96,576]{1,0:T(8,128)} async-done(((f32[768,576]{1,0:T(8,128)}), f32[96,576]{1,0:T(8,128)}) %reduce-scatter.27.cloned.1.call-update) | async-done | bytes 221200
  764.7 68.8 %reduce-scatter.23.cloned.1.call-done = f32[768,96]{0,1:T(8,128)} async-done(((f32[768,768]{0,1:T(8,128)}), f32[768,96]{0,1:T(8,128)}) %reduce-scatter.23.cloned.1.call-update) | async-done | bytes 294928 | tf_op jit(solution)/shard_map/reduce_scatter | solution.py:230
  833.5 72.0 %reduce-scatter.21.cloned.1.call-done = f32[96,768]{1,0:T(8,128)} async-done(((f32[768,768]{1,0:T(8,128)}), f32[96,768]{1,0:T(8,128)}) %reduce-scatter.21.cloned.1.call-update) | async-done | bytes 294928 | tf_op jit(solution)/shard_map/reduce_scatter | solution.py:229
  905.5 67.9 %reduce-scatter.19.cloned.1.call-done = f32[64,768]{1,0:T(8,128)} async-done(((f32[512,768]{1,0:T(8,128)}), f32[64,768]{1,0:T(8,128)}) %reduce-scatter.19.cloned.1.call-update) | async-done | bytes 196624 | tf_op jit(solution)/shard_map/reduce_scatter | solution.py:222
  973.4 68.1 %reduce-scatter.15.cloned.1.call-done = f32[512,96]{0,1:T(8,128)} async-done(((f32[512,768]{0,1:T(8,128)}), f32[512,96]{0,1:T(8,128)}) %reduce-scatter.15.cloned.1.call-update) | async-done | bytes 196624 | tf_op jit(solution)/shard_map/reduce_scatter | solution.py:219
  1041.5 67.9 %reduce-scatter.17.cloned.1.call-done = f32[4,16,768]{2,1,0:T(8,128)} async-done(((f32[4,128,768]{2,1,0:T(8,128)}), f32[4,16,768]{2,1,0:T(8,128)}) %reduce-scatter.17.cloned.1.call-update) | async-done | bytes 196624 | tf_op jit(solution)/shard_map/reduce_scatter | solution.py:220
  (309 shorter events, 235.2 us)
Async XLA Ops:
  7.2 213.6 %copy-start = (bf16[768,768]{1,0:T(8,128)(2,1)S(1)}, bf16[768,768]{1,0:T(8,128)(2,1)}, u32[]{:S(2)}) copy-start(bf16[768,768]{1,0:T(8,128)(2,1)} %param.43) | copy-start | bytes 3538948
  7.2 40.0 %all-reduce.13.cloned.1.call-start = ((), (), s32[]{:S(2)}) async-start(), calls=%async_computation.10 | async-start | bytes 1179648 | tf_op jit(solution)/shard_map/psum | solution.py:120
  53.0 33.5 %all-to-all-start = ((bf16[8,96,768]{2,1,0:T(8,128)(2,1)}), bf16[8,96,768]{2,1,0:T(8,128)(2,1)}, u32[]{:S(2)}, u32[]{:S(2)}) async-start(bf16[8,96,768]{2,1,0:T(8,128)(2,1)} %broadcast_select_fusion), calls=%async_computation | async-start | bytes 2359296 | tf_op jit(solution)/shard_map/all_to_all | solution.py:123
  58.5 154.8 %all-reduce.15.cloned.1.call-start = ((), (), s32[]{:S(2)}) async-start(), calls=%async_computation.11 | async-start | bytes 6291456 | tf_op jit(solution)/shard_map/psum | solution.py:148
  100.3 113.1 %copy-start.17 = (f32[1,4,4,128]{3,1,2,0:T(4,128)}, f32[1,4,4,128]{3,1,2,0:T(4,128)S(1)}, u32[]{:S(2)}) copy-start(f32[1,4,4,128]{3,1,2,0:T(4,128)S(1)} %copy.102) | copy-start | bytes 24580
  100.3 113.1 %copy-start.19 = (f32[1,4,4,128]{3,1,2,0:T(4,128)}, f32[1,4,4,128]{3,1,2,0:T(4,128)S(1)}, u32[]{:S(2)}) copy-start(f32[1,4,4,128]{3,1,2,0:T(4,128)S(1)} %copy.101) | copy-start | bytes 24580
  146.9 166.3 %all-reduce.17.cloned.1.call-start = ((), (), s32[]{:S(2)}) async-start(), calls=%async_computation.12 | async-start | bytes 6291456 | tf_op jit(solution)/shard_map/psum | solution.py:155
  244.5 165.3 %all-reduce.19.cloned.1.call-start = ((), (), s32[]{:S(2)}) async-start(), calls=%async_computation.13 | async-start | bytes 6291456 | tf_op jit(solution)/shard_map/psum | solution.py:168
  341.2 77.3 %copy-start.22 = (f32[768]{0:T(1024)S(1)}, f32[768]{0:T(1024)}, u32[]{:S(2)}) copy-start(f32[768]{0:T(1024)} %param.41) | copy-start | bytes 9220
  341.2 214.8 %all-reduce.21.cloned.1.call-start = ((), (), s32[]{:S(2)}) async-start(), calls=%async_computation.14 | async-start | bytes 6291456 | tf_op jit(solution)/shard_map/psum | solution.py:189
  487.3 68.7 %copy-start.18 = (f32[1,4,4,128]{3,1,2,0:T(4,128)S(1)}, f32[1,4,4,128]{3,1,2,0:T(4,128)}, u32[]{:S(2)}) copy-start(f32[1,4,4,128]{3,1,2,0:T(4,128)} %copy-done.17) | copy-start | bytes 24580
  487.3 68.7 %copy-start.20 = (f32[1,4,4,128]{3,1,2,0:T(4,128)S(1)}, f32[1,4,4,128]{3,1,2,0:T(4,128)}, u32[]{:S(2)}) copy-start(f32[1,4,4,128]{3,1,2,0:T(4,128)} %copy-done.19) | copy-start | bytes 24580
  487.3 68.7 %copy-start.24 = (f32[768]{0:T(1024)S(1)}, f32[768]{0:T(1024)}, u32[]{:S(2)}) copy-start(f32[768]{0:T(1024)} %param.37) | copy-start | bytes 9220
  487.3 174.0 %reduce-scatter.29.cloned.1.call-start = ((), (), s32[]{:S(2)}) async-start(), calls=%async_computation.22 | async-start | bytes 884736
  492.4 209.5 %reduce-scatter.25.cloned.1.call-start = ((), (), s32[]{:S(2)}) async-start(), calls=%async_computation.20 | async-start | bytes 442368
  574.5 186.9 %reduce-scatter.27.cloned.1.call-start = ((), (), s32[]{:S(2)}) async-start(), calls=%async_computation.21 | async-start | bytes 2211840
  587.0 246.5 %reduce-scatter.23.cloned.1.call-start = ((), (), s32[]{:S(2)}) async-start(), calls=%async_computation.19 | async-start | bytes 2654208 | tf_op jit(solution)/shard_map/reduce_scatter | solution.py:230
  595.0 310.5 %reduce-scatter.21.cloned.1.call-start = ((), (), s32[]{:S(2)}) async-start(), calls=%async_computation.18 | async-start | bytes 2654208 | tf_op jit(solution)/shard_map/reduce_scatter | solution.py:229
  602.0 371.3 %reduce-scatter.19.cloned.1.call-start = ((), (), s32[]{:S(2)}) async-start(), calls=%async_computation.17 | async-start | bytes 1769472 | tf_op jit(solution)/shard_map/reduce_scatter | solution.py:222
  614.2 149.1 %copy-start.12 = (bf16[512,768]{1,0:T(8,128)(2,1)S(1)}, bf16[512,768]{1,0:T(8,128)(2,1)}, u32[]{:S(2)}) copy-start(bf16[512,768]{1,0:T(8,128)(2,1)} %param.33) | copy-start | bytes 2359300
  614.2 35.7 %all-to-all-start.1 = ((bf16[8,96,768]{2,1,0:T(8,128)(2,1)}), bf16[8,96,768]{2,1,0:T(8,128)(2,1)}, u32[]{:S(2)}, u32[]{:S(2)}) async-start(bf16[8,96,768]{2,1,0:T(8,128)(2,1)} %select_convert_fusion), calls=%async_computation.1 | async-start | bytes 2359296 | tf_op jit(solution)/shard_map/all_to_all | solution.py:206
  619.9 489.5 %copy-start.1 = (bf16[768,768]{1,0:T(8,128)(2,1)S(1)}, bf16[768,768]{1,0:T(8,128)(2,1)}, u32[]{:S(2)}) copy-start(bf16[768,768]{1,0:T(8,128)(2,1)} %param.43) | copy-start | bytes 3538948
  619.9 421.6 %reduce-scatter.15.cloned.1.call-start = ((), (), s32[]{:S(2)}) async-start(), calls=%async_computation.15 | async-start | bytes 1769472 | tf_op jit(solution)/shard_map/reduce_scatter | solution.py:219
  658.2 451.2 %reduce-scatter.17.cloned.1.call-start = ((), (), s32[]{:S(2)}) async-start(), calls=%async_computation.16 | async-start | bytes 1769472 | tf_op jit(solution)/shard_map/reduce_scatter | solution.py:220
  (40 other events, 520.2 us)
Sparse Core Ops, SparseCore 0:
  11.0 36.1 all-reduce.12
  147.0 66.2 all-reduce.14
  244.6 68.5 all-reduce.16
  341.3 68.5 all-reduce.18
  487.4 68.5 all-reduce.20
  559.7 62.5 reduce-scatter.28
  625.9 65.5 reduce-scatter.24
  695.3 66.0 reduce-scatter.26
  765.5 67.9 reduce-scatter.22
  837.4 67.9 reduce-scatter.20
  909.5 63.8 reduce-scatter.18
  977.6 63.8 reduce-scatter.14
  1045.5 63.8 reduce-scatter.16
where the time goes:
time: 1120 us
  waiting for transfers between devices  752 us (67%)
  matrix products  113 us (10%)
  local copies, waits for them, and re-layouts  94.3 us (8%)
  other arithmetic  87 us (8%)
  blocking collectives  35.4 us (3%)
  between operations  15.9 us (1%)
  starting transfers between devices  12.8 us (1%)
    reduce_scatter x1, waiting for transfers between devices, local(): lax.psum_scatter(grad_up, 'dp', scatter_dimension=0, tiled=True)  72 us
    reduce_scatter x1, waiting for transfers between devices, local(): lax.psum_scatter(grad_down, 'dp', scatter_dimension=1, tiled=True)  68.8 us
    psum x1, waiting for transfers between devices, local(): lax.psum(jnp.einsum('tf,df->td', grad_before, w_up, preferred_element_typ...  68.5 us
    reduce_scatter x1, waiting for transfers between devices, local(): lax.psum_scatter(grad_proj, 'dp', scatter_dimension=1, tiled=True)  68.1 us
    reduce_scatter x1, waiting for transfers between devices, local(): lax.psum_scatter(grad_box, 'dp', scatter_dimension=1, tiled=True)  67.9 us
    reduce_scatter x1, waiting for transfers between devices, local(): lax.psum_scatter(grad_pos, 'dp', scatter_dimension=0, tiled=True)  67.9 us
    psum x1, waiting for transfers between devices, local(): lax.psum(jnp.dot(context, w_mix, preferred_element_type=jnp.float32).asty...  66 us
    psum x1, waiting for transfers between devices, local(): lax.psum(jnp.dot(active, w_down, preferred_element_type=jnp.float32).asty...  64 us
  transfers between devices with their start and end apart: 15, of which 13 were waited for; matrix products, arithmetic and copies ran while one was open for 8% of the time, Pallas kernels for 0%

commit v1 on v0

v1 whole, which is shorter than its diff:
```python
import jax
import jax.numpy as jnp
from jax import lax
from jax.sharding import PartitionSpec as P

HD = 64
LT = 384
EPSILON = 1e-06
NEGATIVE = -1000000000.0
BF = jnp.bfloat16
F32 = jnp.float32


def layer_norm(values, gain, bias):
    mean = jnp.mean(values, axis=-1, keepdims=True)
    centred = values - mean
    variance = jnp.mean(centred * centred, axis=-1, keepdims=True)
    inverse = lax.rsqrt(variance + EPSILON)
    normed = centred * inverse
    return (normed * gain + bias, normed, inverse)


def norm_back(grad, normed, inverse, gain):
    scaled = grad * gain
    mean_grad = jnp.mean(scaled, axis=-1, keepdims=True)
    mean_proj = jnp.mean(scaled * normed, axis=-1, keepdims=True)
    grad_in = inverse * (scaled - mean_grad - normed * mean_proj)
    return (grad_in, jnp.sum(grad * normed, axis=0), jnp.sum(grad, axis=0))


def key_mask(seg_row, count):
    length = seg_row.shape[0]
    places = jnp.arange(length, dtype=jnp.int32)
    usable = places < LT + count
    same = seg_row[:, None] == seg_row[None, :]
    return same & (usable[None, :] | (places[:, None] == places[None, :]))


def masked_scores(queries, keys, allowed):
    scale = queries.shape[-1] ** (-0.5)
    scores = jnp.einsum("qhd,khd->hqk", queries, keys, preferred_element_type=F32) * scale
    return jnp.where(allowed[None], scores, NEGATIVE)


def attend(queries, keys, values, allowed):
    scores = masked_scores(queries, keys, allowed)
    top = jnp.max(scores, axis=-1, keepdims=True)
    total = jnp.sum(jnp.exp(scores - top), axis=-1, keepdims=True)
    logsum = top + jnp.log(total)
    probs = jnp.exp(scores - logsum)
    context = jnp.einsum("hqk,khd->qhd", probs.astype(BF), values, preferred_element_type=F32)
    return (context.astype(BF), logsum)


def attend_back(queries, keys, values, grad_context, logsum, allowed):
    scale = queries.shape[-1] ** (-0.5)
    scores = masked_scores(queries, keys, allowed)
    probs = jnp.exp(scores - logsum)
    grad_probs = jnp.einsum("qhd,khd->hqk", grad_context, values, preferred_element_type=F32)
    inner = jnp.sum(probs * grad_probs, axis=-1, keepdims=True)
    grad_scores = (probs * (grad_probs - inner)).astype(BF)
    grad_queries = (
        jnp.einsum("hqk,khd->qhd", grad_scores, keys, preferred_element_type=F32) * scale
    ).astype(BF)
    grad_keys = (
        jnp.einsum("hqk,qhd->khd", grad_scores, queries, preferred_element_type=F32) * scale
    ).astype(BF)
    grad_values = jnp.einsum(
        "hqk,qhd->khd", probs.astype(BF), grad_context, preferred_element_type=F32
    ).astype(BF)
    return (grad_queries, grad_keys, grad_values)


def swap(value, axis, bit):
    count = lax.axis_size(axis)
    return lax.ppermute(value, axis, [(i, i ^ bit) for i in range(count)])


def bits_of(axis):
    count = lax.axis_size(axis)
    return [1 << i for i in range(count.bit_length() - 1)]


def gather_shards(shard):
    held = {0: shard}
    for bit in reversed(bits_of("tensor")):
        held.update({k | bit: swap(v, "tensor", bit) for k, v in list(held.items())})
    return [held[k] for k in sorted(held)]


def reduce_shards(parts):
    held = dict(enumerate(parts))
    for bit in bits_of("tensor"):
        moved = {k: swap(v.astype(BF), "tensor", bit) for k, v in held.items() if k & bit}
        held = {
            k: v + moved[k | bit].astype(F32) for k, v in held.items() if not k & bit
        }
    return held[0]


def sum_over_dp(terms):
    return jnp.sum(
        lax.all_to_all(terms.astype(BF), "dp", 0, 0, tiled=True).astype(F32), axis=0
    )


def local(
    text_embed,
    region_feats,
    box_coords,
    seg_ids,
    region_counts,
    send_index,
    recv_pos,
    w_proj,
    box_table,
    type_embed,
    pos_embed,
    gain_embed,
    bias_embed,
    w_qkv,
    w_mix,
    gain_mid,
    bias_mid,
    w_up,
    w_down,
    gain_final,
    bias_final,
    cotangent,
):
    parts = lax.axis_size("tensor")
    peers = lax.axis_size("dp")
    mine = lax.axis_index("tensor")
    row_count, text_len, width = text_embed.shape
    assert row_count == parts
    length = seg_ids.shape[1]
    slots = length - text_len
    stored = region_feats.shape[0]
    capacity = send_index.shape[2]
    bins = box_table.shape[1]
    group = w_qkv.shape[2]
    heads_here = group // HD
    chunk = width // parts
    share = width // peers

    def own(array):
        return lax.dynamic_index_in_dim(array, mine, 0, keepdims=False)

    def own_columns(array, k=0):
        return lax.dynamic_slice_in_dim(array, (mine ^ k) * chunk, chunk, array.ndim - 1)

    partial = reduce_shards(
        [
            jnp.dot(region_feats, own_columns(w_proj, k), preferred_element_type=F32)
            for k in range(parts)
        ]
    )
    corners = (
        (box_coords[:, :, None] == jnp.arange(bins, dtype=jnp.int32)[None, None, :])
        .astype(BF)
        .reshape(stored, -1)
    )
    boxed = jnp.dot(
        corners, own_columns(box_table).reshape(-1, chunk), preferred_element_type=F32
    )
    rows_low = (partial + boxed).astype(BF)
    send_flat = send_index.reshape(-1)
    send_pick = (send_flat[:, None] == jnp.arange(stored, dtype=jnp.int32)[None, :]).astype(BF)
    outgoing = jnp.dot(send_pick, rows_low, preferred_element_type=F32).astype(BF)
    incoming = lax.all_to_all(
        outgoing.reshape(peers, capacity, chunk), "dp", 0, 0, tiled=True
    ).reshape(peers * capacity, chunk)
    recv_flat = recv_pos.reshape(-1)
    recv_slot = jnp.where(
        recv_flat >= 0,
        (recv_flat // length) * slots + recv_flat % length - text_len,
        -1,
    )
    recv_pick = (
        jnp.arange(row_count * slots, dtype=jnp.int32)[:, None] == recv_slot[None, :]
    ).astype(BF)
    placed = jnp.dot(recv_pick, incoming, preferred_element_type=F32).astype(BF)
    placed = lax.all_to_all(placed.reshape(parts, slots, chunk), "tensor", 0, 0, tiled=True)
    placed = placed.transpose(1, 0, 2).reshape(slots, width)

    qkv_shards = gather_shards(w_qkv)
    mix_shards = gather_shards(w_mix)
    up_shards = gather_shards(w_up)
    down_shards = gather_shards(w_down)

    text_part = own(text_embed).astype(F32) + type_embed[0].astype(F32)
    region_part = placed.astype(F32) + type_embed[1].astype(F32)
    embedded = jnp.concatenate([text_part, region_part], axis=0) + pos_embed.astype(F32)
    hidden0, normed0, inverse0 = layer_norm(embedded, gain_embed, bias_embed)
    inputs0 = hidden0.astype(BF)
    allowed = key_mask(own(seg_ids), own(region_counts))
    heads, contexts, logsums = [], [], []
    attn = 0.0
    for k in range(parts):
        mixed = jnp.einsum("td,cde->cte", inputs0, qkv_shards[k], preferred_element_type=F32)
        mixed = mixed.astype(BF).reshape(3, length, heads_here, HD)
        context, logsum = attend(mixed[0], mixed[1], mixed[2], allowed)
        context = context.reshape(length, group)
        attn = attn + jnp.dot(context, mix_shards[k], preferred_element_type=F32)
        heads.append(mixed)
        contexts.append(context)
        logsums.append(logsum)
    hidden1, normed1, inverse1 = layer_norm(hidden0 + attn, gain_mid, bias_mid)
    inputs1 = hidden1.astype(BF)
    befores, actives = [], []
    ffn = 0.0
    for k in range(parts):
        before = jnp.dot(inputs1, up_shards[k], preferred_element_type=F32)
        active = jax.nn.gelu(before, approximate=False).astype(BF)
        ffn = ffn + jnp.dot(active, down_shards[k], preferred_element_type=F32)
        befores.append(before)
        actives.append(active)
    final, normed2, inverse2 = layer_norm(hidden1 + ffn, gain_final, bias_final)
    layer_output = lax.all_gather(final.astype(BF), "tensor", axis=0, tiled=False)

    grad_final = own(cotangent).astype(F32)
    grad_x2, grad_gain_final, grad_bias_final = norm_back(grad_final, normed2, inverse2, gain_final)
    grad_ffn = grad_x2.astype(BF)
    down_terms, up_terms = [], []
    back_one = 0.0
    for k in range(parts):
        down_terms.append(
            jnp.einsum("td,tf->df", grad_ffn, actives[k], preferred_element_type=F32)
        )
        grad_active = jnp.einsum("td,fd->tf", grad_ffn, down_shards[k], preferred_element_type=F32)
        slope = jax.vjp(lambda value: jax.nn.gelu(value, approximate=False), befores[k])[1]
        grad_before = slope(grad_active)[0].astype(BF)
        up_terms.append(
            jnp.einsum("td,tf->df", inputs1, grad_before, preferred_element_type=F32)
        )
        back_one = back_one + jnp.einsum(
            "tf,df->td", grad_before, up_shards[k], preferred_element_type=F32
        )
    sum_down = reduce_shards(down_terms)
    sum_up = reduce_shards(up_terms)
    grad_x1, grad_gain_mid, grad_bias_mid = norm_back(
        grad_x2 + back_one, normed1, inverse1, gain_mid
    )
    grad_attn = grad_x1.astype(BF)
    mix_terms, qkv_terms = [], []
    back_zero = 0.0
    for k in range(parts):
        mix_terms.append(
            jnp.einsum("td,te->de", grad_attn, contexts[k], preferred_element_type=F32)
        )
        grad_context = jnp.einsum(
            "td,ed->te", grad_attn, mix_shards[k], preferred_element_type=F32
        ).astype(BF)
        grad_mixed = jnp.stack(
            attend_back(
                heads[k][0],
                heads[k][1],
                heads[k][2],
                grad_context.reshape(length, heads_here, HD),
                logsums[k],
                allowed,
            )
        ).reshape(3, length, group)
        qkv_terms.append(
            jnp.einsum("td,cte->cde", inputs0, grad_mixed, preferred_element_type=F32)
        )
        back_zero = back_zero + jnp.einsum(
            "cte,cde->td", grad_mixed, qkv_shards[k], preferred_element_type=F32
        )
    sum_mix = reduce_shards(mix_terms)
    sum_qkv = reduce_shards(qkv_terms)
    grad_embedded, grad_gain_embed, grad_bias_embed = norm_back(
        grad_x1 + back_zero, normed0, inverse0, gain_embed
    )
    text_own = grad_embedded[:text_len]
    region_own = grad_embedded[text_len:]
    text_grad = lax.all_gather(text_own.astype(BF), "tensor", axis=0, tiled=False).astype(F32)

    vectors = jnp.stack(
        [
            jnp.sum(text_own, axis=0),
            jnp.sum(region_own, axis=0),
            grad_gain_embed,
            grad_bias_embed,
            grad_gain_mid,
            grad_bias_mid,
            grad_gain_final,
            grad_bias_final,
        ]
    )
    vector_count = vectors.shape[0]
    outward = jnp.concatenate([region_own, text_own, vectors], axis=0).astype(BF)
    outward = outward.reshape(-1, parts, chunk).transpose(1, 0, 2)
    inward = lax.all_to_all(outward, "tensor", 0, 0, tiled=True)
    returning = jnp.einsum(
        "js,jc->sc",
        recv_pick,
        inward[:, :slots].reshape(row_count * slots, chunk),
        preferred_element_type=F32,
    ).astype(BF)
    returned = lax.all_to_all(
        returning.reshape(peers, capacity, chunk), "dp", 0, 0, tiled=True
    ).reshape(peers * capacity, chunk)
    region_chunk = jnp.einsum(
        "sr,sc->rc", send_pick, returned, preferred_element_type=F32
    ).astype(BF)
    grad_regions = lax.all_gather(region_chunk, "tensor", axis=1, tiled=True)
    proj_term = jnp.einsum("sd,sf->df", grad_regions, region_feats, preferred_element_type=F32)
    feat_grad = jnp.einsum("sd,fd->sf", grad_regions, w_proj, preferred_element_type=F32)
    box_term = jnp.einsum("sb,sc->bc", corners, region_chunk, preferred_element_type=F32)

    summed = jnp.sum(inward.astype(F32), axis=0)
    pos_term = jnp.concatenate([summed[slots:length], summed[:slots]], axis=0)
    bin_share = bins // peers
    pos_share = length // peers
    bundle = jnp.concatenate(
        [
            pos_term.reshape(peers, pos_share, chunk),
            box_term.reshape(-1, peers, bin_share, chunk)
            .transpose(1, 0, 2, 3)
            .reshape(peers, -1, chunk),
            jnp.broadcast_to(summed[length:], (peers, vector_count, chunk)),
        ],
        axis=1,
    )
    bundle = lax.all_gather(sum_over_dp(bundle), "tensor", axis=1, tiled=True)
    grad_pos = bundle[:pos_share]
    grad_box = bundle[pos_share:-vector_count].reshape(-1, bin_share, width)
    vectors = lax.dynamic_slice_in_dim(
        bundle[-vector_count:], lax.axis_index("dp") * share, share, 1
    )

    grad_down = sum_over_dp(sum_down.reshape(peers, share, -1)).T
    grad_up = sum_over_dp(sum_up.reshape(peers, share, -1))
    grad_mix = sum_over_dp(sum_mix.reshape(peers, share, -1)).T
    grad_qkv = sum_over_dp(sum_qkv.reshape(3, peers, share, group).transpose(1, 0, 2, 3))
    grad_proj = sum_over_dp(proj_term.reshape(peers, share, -1)).T
    return (
        layer_output,
        text_grad,
        feat_grad,
        grad_proj,
        grad_box,
        vectors[:2],
        grad_pos,
        vectors[2],
        vectors[3],
        grad_qkv,
        grad_mix,
        vectors[4],
        vectors[5],
        grad_up,
        grad_down,
        vectors[6],
        vectors[7],
    )


def solution(mesh):
    return jax.shard_map(
        local,
        mesh=mesh,
        in_specs=(
            P("dp", None, None),
            P("dp", "tensor"),
            P("dp", None),
            P("dp", None),
            P("dp"),
            P("dp", None, None),
            P("dp", None, None),
            P("tensor", None),
            P(),
            P(),
            P(),
            P(),
            P(),
            P(None, None, "tensor"),
            P("tensor", None),
            P(),
            P(),
            P(None, "tensor"),
            P("tensor", None),
            P(),
            P(),
            P("dp", None, None),
        ),
        out_specs=(
            P("dp", None, None),
            P("dp", None, None),
            P("dp", "tensor"),
            P("tensor", "dp"),
            P(None, "dp", None),
            P(None, "dp"),
            P("dp", None),
            P("dp"),
            P("dp"),
            P(None, "dp", "tensor"),
            P("tensor", "dp"),
            P("dp"),
            P("dp"),
            P("dp", "tensor"),
            P("tensor", "dp"),
            P("dp"),
            P("dp"),
        ),
        check_vma=False,
    )
```

time: 1120 us -> 453 us (0.40)
  waiting for transfers between devices: 752 us -> 131 us
  starting transfers between devices: 12.8 us -> 60.8 us
  local copies, waits for them, and re-layouts: 94.3 us -> 49.1 us
  other arithmetic: 87 us -> 44.3 us
  blocking collectives: 35.4 us -> 14.4 us
  matrix products: 113 us -> 130 us
    reduce_scatter x5 -> x0, waiting for transfers between devices: 345 us -> none  [the longest x1 72 us: local(): lax.psum_scatter(grad_up, 'dp', scatter_dimension=0, tiled=True)]
    psum x5 -> x0, waiting for transfers between devices: 298 us -> none  [the longest x1 68.5 us: local(): lax.psum(jnp.einsum('tf,df->td', grad_before, w_up, preferred_element_typ...]
    ppermute x0 -> x27, waiting for transfers between devices: none -> 81.5 us  [swap(): return lax.ppermute(value, axis, [(i, i ^ bit) for i in range(count)])]
    unnamed x16 -> x2, waiting for transfers between devices: 58.4 us -> 0.03 us
    unnamed x1 -> x0, blocking collectives: 35.4 us -> none
    all_to_all x2 -> x10, starting transfers between devices: 11.1 us -> 45.9 us  [the longest x6 28 us: sum_over_dp(): lax.all_to_all(terms.astype(BF), 'dp', 0, 0, tiled=True).astype(F32)]
    reduce_sum x4 -> x2, other arithmetic: 22.8 us -> 2.08 us  [norm_back(): return (grad_in, jnp.sum(grad * normed, axis=0), jnp.sum(grad, axis=0))]
    dot_general x43 -> x79, matrix products: 106 us -> 124 us  [the longest x4 26.8 us: local(): before = jnp.dot(inputs1, up_shards[k], preferred_element_type=F32)]
  transfers between devices with their start and end apart: 15 -> 39, of which waited for: 13 -> 15; matrix products, arithmetic and copies ran while one was open for 8% -> 37% of each run, Pallas kernels for 0% -> 0%
where the time goes in v1:
time: 453 us; the launch traced here: 446 us
  waiting for transfers between devices  131 us (29%)
  matrix products  130 us (29%)
  starting transfers between devices  60.8 us (13%)
  local copies, waits for them, and re-layouts  49.1 us (11%)
  other arithmetic  44.3 us (10%)
  between operations  16.7 us (4%)
  blocking collectives  14.4 us (3%)
    ppermute x27, waiting for transfers between devices, swap(): return lax.ppermute(value, axis, [(i, i ^ bit) for i in range(count)])  81.5 us
    all_to_all x6, starting transfers between devices, sum_over_dp(): lax.all_to_all(terms.astype(BF), 'dp', 0, 0, tiled=True).astype(F32)  28 us
    all_to_all x6, waiting for transfers between devices, sum_over_dp(): lax.all_to_all(terms.astype(BF), 'dp', 0, 0, tiled=True).astype(F32)  27.7 us
    dot_general x4, matrix products, local(): before = jnp.dot(inputs1, up_shards[k], preferred_element_type=F32)  26.8 us
    ppermute x27, starting transfers between devices, swap(): return lax.ppermute(value, axis, [(i, i ^ bit) for i in range(count)])  14.8 us
    concatenate x9, local copies, waits for them, and re-layouts, local(): jnp.concatenate([region_own, text_own, vectors], axis=0).astype(BF)  12 us
    unnamed x190, local copies, waits for them, and re-layouts  11.8 us
  transfers between devices with their start and end apart: 39, of which 15 were waited for; matrix products, arithmetic and copies ran while one was open for 37% of the time, Pallas kernels for 0%

profile of v1, /device:TPU:0, one launch (start us, length us, event | category | flops | bytes accessed | tf_op | source)
XLA Modules:
  0.0 446.2 jit_solution(14704864233762571165)
XLA Ops:
  23.4 6.0 %all-to-all-start = ((bf16[8,96,192]{1,2,0:T(8,128)(2,1)}), bf16[8,96,192]{1,2,0:T(8,128)(2,1)S(1)}, u32[]{:S(2)}, u32[]{:S(2)}) async-start(bf16[8,96,192]{1,2,0:T(8,128)(2,1)} %copy.226), calls=%async_computation | async-start | bytes 786432 | tf_op jit(solution)/shard_map/all_to_all | solution.py:170
  33.8 7.9 %all-to-all-done = bf16[8,96,192]{1,2,0:T(8,128)(2,1)S(1)} async-done(((bf16[8,96,192]{1,2,0:T(8,128)(2,1)}), bf16[8,96,192]{1,2,0:T(8,128)(2,1)S(1)}, u32[]{:S(2)}, u32[]{:S(2)}) %all-to-all-start) | async-done | bytes 294944 | tf_op jit(solution)/shard_map/all_to_all | solution.py:170
  47.5 5.0 %all-to-all-done.1 = bf16[4,128,192]{1,2,0:T(8,128)(2,1)S(1)} async-done(((bf16[4,128,192]{1,2,0:T(8,128)(2,1)}), bf16[4,128,192]{1,2,0:T(8,128)(2,1)S(1)}, u32[]{:S(2)}, u32[]{:S(2)}) %all-to-all-start.1) | async-done | bytes 196640 | tf_op jit(solution)/shard_map/all_to_all | solution.py:183
  77.7 6.9 %collective-permute-done.11 = bf16[768,768]{1,0:T(8,128)(2,1)S(1)} collective-permute-done((bf16[768,768]{1,0:T(8,128)(2,1)S(1)}, bf16[768,768]{1,0:T(8,128)(2,1)S(1)}, u32[]{:S(2)}, u32[]{:S(2)}) %collective-permute-start.11) | collective-permute-done | bytes 1179680 | tf_op jit(solution)/shard_map/ppermute | solution.py:76
  84.6 23.9 %collective-permute-done.12 = bf16[768,768]{1,0:T(8,128)(2,1)S(1)} collective-permute-done((bf16[768,768]{1,0:T(8,128)(2,1)S(1)}, bf16[768,768]{1,0:T(8,128)(2,1)S(1)}, u32[]{:S(2)}, u32[]{:S(2)}) %collective-permute-start.12) | collective-permute-done | bytes 1179680 | tf_op jit(solution)/shard_map/ppermute | solution.py:76
  111.8 5.4 %multiply_convert_fusion.7 = (bf16[512,768]{1,0:T(8,128)(2,1)S(1)}, f32[512,768]{1,0:T(8,128)}, f32[512,768]{1,0:T(8,128)}) fusion(bf16[512,768]{1,0:T(8,128)(2,1)S(1)} %fusion.46, bf16[768,768]{1,0:T(8,128)(2,1)S(1)} %copy-done.74), kind=kOutput, calls=%fused_computation.117 | convolution fusion | flops 629538816 | bytes 5898240 | tf_op jit(solution)/shard_map/dot_general | solution.py:213
  118.0 9.6 %multiply_convert_fusion.5 = (bf16[512,768]{1,0:T(8,128)(2,1)S(1)}, f32[512,768]{1,0:T(8,128)S(1)}, f32[512,768]{1,0:T(8,128)S(1)}) fusion(bf16[512,768]{1,0:T(8,128)(2,1)S(1)} %fusion.46, bf16[768,768]{1,0:T(8,128)(2,1)S(1)} %collective-permute-done.11), kind=kOutput, calls=%fused_computation.91 | convolution fusion | flops 629538816 | bytes 5898240 | tf_op jit(solution)/shard_map/dot_general | solution.py:213
  128.6 6.3 %multiply_convert_fusion.6 = (bf16[512,768]{1,0:T(8,128)(2,1)S(1)}, f32[512,768]{1,0:T(8,128)}, f32[512,768]{1,0:T(8,128)}) fusion(bf16[512,768]{1,0:T(8,128)(2,1)S(1)} %fusion.46, bf16[768,768]{1,0:T(8,128)(2,1)} %collective-permute-done.9), kind=kOutput, calls=%fused_computation.104 | convolution fusion | flops 629538816 | bytes 5898240 | tf_op jit(solution)/shard_map/dot_general | solution.py:213
  135.8 5.5 %multiply_convert_fusion.4 = (bf16[512,768]{1,0:T(8,128)(2,1)S(1)}, f32[512,768]{1,0:T(8,128)}, f32[512,768]{1,0:T(8,128)}) fusion(bf16[512,768]{1,0:T(8,128)(2,1)S(1)} %fusion.46, bf16[768,768]{1,0:T(8,128)(2,1)S(1)} %collective-permute-done.13), kind=kOutput, calls=%fused_computation.78 | convolution fusion | flops 629538816 | bytes 5898240 | tf_op jit(solution)/shard_map/dot_general | solution.py:213
  174.8 4.8 %multiply_reduce_fusion = (f32[3,512]{1,0:T(4,128)S(1)}, f32[3,512]{1,0:T(4,128)S(1)}, f32[3,512]{1,0:T(4,128)S(1)}, f32[3,512]{1,0:T(4,128)S(1)}, f32[3,512,512]{1,2,0:T(8,128)}) fusion(f32[3,512,512]{1,2,0:T(8,128)S(1)} %get-tuple-element.131, f32[3,512]{1,0:T(4,128)S(1)} %get-tuple-element.144, pred[512,512]{0,1:T(8,128)(4,1)S(1)} %fusion.66, ...), kind=kOutput, calls=%fused_computation.1 | convolution fusion | flops 116385792 | bytes 25870336 | tf_op jit(solution)/shard_map/qhd,khd->hqk/dot_general | solution.py:59
  179.6 7.5 %multiply_convert_fusion = (bf16[3,512,512]{1,2,0:T(8,128)(2,1)}, bf16[3,512,512]{1,2,0:T(8,128)(2,1)}, bf16[3,512,512]{1,2,0:T(8,128)(2,1)}, bf16[3,512,512]{1,2,0:T(8,128)(2,1)S(1)}) fusion(f32[3,512,512]{1,2,0:T(8,128)} %get-tuple-element.142, f32[3,512,512]{1,2,0:T(8,128)S(1)} %get-tuple-element.131, f32[3,512]{1,0:T(4,128)S(1)} %get-tuple-element.79, ...), kind=kLoop, calls=%fused_computation | loop fusion | flops 18874368 | bytes 31768576 | tf_op jit(solution)/shard_map/convert_element_type | solution.py:61
  220.5 4.4 all-to-all-start.2
  232.8 6.4 %all-to-all-done.2 = bf16[4,520,192]{1,2,0:T(8,128)(2,1)} async-done(((bf16[4,520,192]{1,2,0:T(8,128)(2,1)}), bf16[4,520,192]{1,2,0:T(8,128)(2,1)}, u32[]{:S(2)}, u32[]{:S(2)}) %all-to-all-start.2) | async-done | bytes 798752 | tf_op jit(solution)/shard_map/all_to_all | solution.py:294
  267.2 6.2 %all-to-all-done.7 = bf16[8,96,192]{1,2,0:T(8,128)(2,1)S(1)} async-done(((bf16[8,96,192]{1,2,0:T(8,128)(2,1)}), bf16[8,96,192]{1,2,0:T(8,128)(2,1)S(1)}, u32[]{:S(2)}, u32[]{:S(2)}) %all-to-all-start.7) | async-done | bytes 294944 | tf_op jit(solution)/shard_map/all_to_all | solution.py:103
  280.3 7.8 %all_gather.22 = bf16[384,768]{0,1:T(8,128)(2,1)S(1)} all-gather(bf16[384,192]{0,1:T(8,128)(2,1)S(1)} %fusion.61), channel_id=1, replica_groups=mesh['dp'=8,'tensor'=4] {'tensor'}, dimensions={1}, use_global_device_ids=true | all-gather | bytes 737280 | tf_op jit(solution)/shard_map/all_gather | solution.py:307
  306.4 14.3 %collective-permute-done.17 = bf16[3,768,192]{1,2,0:T(8,128)(2,1)S(1)} collective-permute-done((bf16[3,768,192]{1,2,0:T(8,128)(2,1)S(1)}, bf16[3,768,192]{1,2,0:T(8,128)(2,1)S(1)}, u32[]{:S(2)}, u32[]{:S(2)}) %collective-permute-start.17) | collective-permute-done | bytes 884768 | tf_op jit(solution)/shard_map/ppermute | solution.py:76
  328.9 6.0 %all-to-all-start.6 = ((bf16[8,3,96,192]{2,3,1,0:T(8,128)(2,1)}), bf16[8,3,96,192]{2,3,1,0:T(8,128)(2,1)}, u32[]{:S(2)}, u32[]{:S(2)}) async-start(bf16[8,3,96,192]{2,3,1,0:T(8,128)(2,1)} %bitcast.368), calls=%async_computation.6 | async-start | bytes 2359296 | tf_op jit(solution)/shard_map/all_to_all | solution.py:103
  338.8 5.9 %collective-permute-done.26 = bf16[768,768]{1,0:T(8,128)(2,1)} collective-permute-done((bf16[768,768]{1,0:T(8,128)(2,1)}, bf16[768,768]{1,0:T(8,128)(2,1)}, u32[]{:S(2)}, u32[]{:S(2)}) %collective-permute-start.26) | collective-permute-done | bytes 1179680 | tf_op jit(solution)/shard_map/ppermute | solution.py:76
  348.0 12.8 %all-to-all-done.6 = bf16[8,3,96,192]{2,3,1,0:T(8,128)(2,1)} async-done(((bf16[8,3,96,192]{2,3,1,0:T(8,128)(2,1)}), bf16[8,3,96,192]{2,3,1,0:T(8,128)(2,1)}, u32[]{:S(2)}, u32[]{:S(2)}) %all-to-all-start.6) | async-done | bytes 884768 | tf_op jit(solution)/shard_map/all_to_all | solution.py:103
  370.3 26.9 %collective-permute-done.23 = bf16[768,768]{1,0:T(8,128)(2,1)S(1)} collective-permute-done((bf16[768,768]{1,0:T(8,128)(2,1)S(1)}, bf16[768,768]{1,0:T(8,128)(2,1)S(1)}, u32[]{:S(2)}, u32[]{:S(2)}) %collective-permute-start.23) | collective-permute-done | bytes 1179680 | tf_op jit(solution)/shard_map/ppermute | solution.py:76
  398.6 6.1 %all-to-all-start.8 = ((bf16[8,96,768]{2,1,0:T(8,128)(2,1)}), bf16[8,96,768]{2,1,0:T(8,128)(2,1)}, u32[]{:S(2)}, u32[]{:S(2)}) async-start(bf16[8,96,768]{2,1,0:T(8,128)(2,1)} %bitcast.369), calls=%async_computation.8 | async-start | bytes 2359296 | tf_op jit(solution)/shard_map/all_to_all | solution.py:103
  408.0 6.6 %all-gather.2 = f32[4,192,136]{1,2,0:T(8,128)S(1)} all-gather(f32[1,192,136]{1,2,0:T(8,128)S(1)} %bitcast.431), channel_id=1, replica_groups=mesh['dp'=8,'tensor'=4] {'tensor'}, dimensions={0}, use_global_device_ids=true | all-gather | bytes 522240 | tf_op jit(solution)/shard_map/all_gather | solution.py:326
  421.5 4.3 convert.75
  426.6 6.6 %all-to-all-done.8 = bf16[8,96,768]{2,1,0:T(8,128)(2,1)} async-done(((bf16[8,96,768]{2,1,0:T(8,128)(2,1)}), bf16[8,96,768]{2,1,0:T(8,128)(2,1)}, u32[]{:S(2)}, u32[]{:S(2)}) %all-to-all-start.8) | async-done | bytes 1179680 | tf_op jit(solution)/shard_map/all_to_all | solution.py:103
  (434 shorter events, 226.5 us)
Async XLA Ops:
  7.3 70.0 %collective-permute-start.4 = (bf16[192,768]{1,0:T(8,128)(2,1)}, bf16[192,768]{1,0:T(8,128)(2,1)}, u32[]{:S(2)}, u32[]{:S(2)}) collective-permute-start(bf16[192,768]{1,0:T(8,128)(2,1)} %param.36), channel_id=1, source_target_pairs={{0,1},{1,0},{2,3},{3,2},{4,5},{5,4},{6,7},{7,6},{8,9},{9,8},{10,11... | collective-permute-start | bytes 884744 | tf_op jit(solution)/shard_map/ppermute | solution.py:76
  7.8 55.8 %collective-permute-start.6 = (bf16[192,768]{1,0:T(8,128)(2,1)}, bf16[192,768]{1,0:T(8,128)(2,1)S(1)}, u32[]{:S(2)}, u32[]{:S(2)}) collective-permute-start(bf16[192,768]{1,0:T(8,128)(2,1)} %param.36), channel_id=1, source_target_pairs={{0,2},{1,3},{2,0},{3,1},{4,6},{5,7},{6,4},{7,5},{8,10},{9,11},{10,... | collective-permute-start | bytes 884744 | tf_op jit(solution)/shard_map/ppermute | solution.py:76
  13.9 44.1 %collective-permute-start.3 = (bf16[3,768,192]{1,2,0:T(8,128)(2,1)}, bf16[3,768,192]{1,2,0:T(8,128)(2,1)}, u32[]{:S(2)}, u32[]{:S(2)}) collective-permute-start(bf16[3,768,192]{1,2,0:T(8,128)(2,1)} %param.35), channel_id=1, source_target_pairs={{0,1},{1,0},{2,3},{3,2},{4,5},{5,4},{6,7},{7,6},{8,9},{9,8},{10,11... | collective-permute-start | bytes 2654216 | tf_op jit(solution)/shard_map/ppermute | solution.py:76
  19.1 36.0 %collective-permute-start.5 = (bf16[3,768,192]{1,2,0:T(8,128)(2,1)}, bf16[3,768,192]{1,2,0:T(8,128)(2,1)}, u32[]{:S(2)}, u32[]{:S(2)}) collective-permute-start(bf16[3,768,192]{1,2,0:T(8,128)(2,1)} %param.35), channel_id=1, source_target_pairs={{0,2},{1,3},{2,0},{3,1},{4,6},{5,7},{6,4},{7,5},{8,10},{9,11},{10,... | collective-permute-start | bytes 2654216 | tf_op jit(solution)/shard_map/ppermute | solution.py:76
  21.3 107.3 %collective-permute-start.9 = (bf16[768,768]{1,0:T(8,128)(2,1)}, bf16[768,768]{1,0:T(8,128)(2,1)}, u32[]{:S(2)}, u32[]{:S(2)}) collective-permute-start(bf16[768,768]{1,0:T(8,128)(2,1)} %param.39), channel_id=1, source_target_pairs={{0,1},{1,0},{2,3},{3,2},{4,5},{5,4},{6,7},{7,6},{8,9},{9,8},{10,11... | collective-permute-start | bytes 3538952 | tf_op jit(solution)/shard_map/ppermute | solution.py:76
  55.7 28.9 %collective-permute-start.11 = (bf16[768,768]{1,0:T(8,128)(2,1)S(1)}, bf16[768,768]{1,0:T(8,128)(2,1)S(1)}, u32[]{:S(2)}, u32[]{:S(2)}) collective-permute-start(bf16[768,768]{1,0:T(8,128)(2,1)S(1)} %copy-done.74), channel_id=1, source_target_pairs={{0,2},{1,3},{2,0},{3,1},{4,6},{5,7},{6,4},{7,5},{8,10},{9,11},{10,... | collective-permute-start | bytes 3538952 | tf_op jit(solution)/shard_map/ppermute | solution.py:76
  64.2 44.3 %collective-permute-start.12 = (bf16[768,768]{1,0:T(8,128)(2,1)S(1)}, bf16[768,768]{1,0:T(8,128)(2,1)S(1)}, u32[]{:S(2)}, u32[]{:S(2)}) collective-permute-start(bf16[768,768]{1,0:T(8,128)(2,1)S(1)} %copy-done.73), channel_id=1, source_target_pairs={{0,2},{1,3},{2,0},{3,1},{4,6},{5,7},{6,4},{7,5},{8,10},{9,11},{10,... | collective-permute-start | bytes 3538952 | tf_op jit(solution)/shard_map/ppermute | solution.py:76
  65.9 44.0 %collective-permute-start.8 = (bf16[192,768]{1,0:T(8,128)(2,1)S(1)}, bf16[192,768]{1,0:T(8,128)(2,1)S(1)}, u32[]{:S(2)}, u32[]{:S(2)}) collective-permute-start(bf16[192,768]{1,0:T(8,128)(2,1)S(1)} %collective-permute-done.6), channel_id=1, source_target_pairs={{0,1},{1,0},{2,3},{3,2},{4,5},{5,4},{6,7},{7,6},{8,9},{9,8},{10,11... | collective-permute-start | bytes 884744 | tf_op jit(solution)/shard_map/ppermute | solution.py:76
  77.3 57.6 %collective-permute-start.10 = (bf16[768,768]{1,0:T(8,128)(2,1)S(1)}, bf16[768,768]{1,0:T(8,128)(2,1)S(1)}, u32[]{:S(2)}, u32[]{:S(2)}) collective-permute-start(bf16[768,768]{1,0:T(8,128)(2,1)S(1)} %copy-done.73), channel_id=1, source_target_pairs={{0,1},{1,0},{2,3},{3,2},{4,5},{5,4},{6,7},{7,6},{8,9},{9,8},{10,11... | collective-permute-start | bytes 3538952 | tf_op jit(solution)/shard_map/ppermute | solution.py:76
  84.6 51.2 %collective-permute-start.13 = (bf16[768,768]{1,0:T(8,128)(2,1)S(1)}, bf16[768,768]{1,0:T(8,128)(2,1)S(1)}, u32[]{:S(2)}, u32[]{:S(2)}) collective-permute-start(bf16[768,768]{1,0:T(8,128)(2,1)S(1)} %collective-permute-done.11), channel_id=1, source_target_pairs={{0,1},{1,0},{2,3},{3,2},{4,5},{5,4},{6,7},{7,6},{8,9},{9,8},{10,11... | collective-permute-start | bytes 3538952 | tf_op jit(solution)/shard_map/ppermute | solution.py:76
  108.5 32.8 %collective-permute-start.14 = (bf16[768,768]{1,0:T(8,128)(2,1)S(1)}, bf16[768,768]{1,0:T(8,128)(2,1)S(1)}, u32[]{:S(2)}, u32[]{:S(2)}) collective-permute-start(bf16[768,768]{1,0:T(8,128)(2,1)S(1)} %collective-permute-done.12), channel_id=1, source_target_pairs={{0,1},{1,0},{2,3},{3,2},{4,5},{5,4},{6,7},{7,6},{8,9},{9,8},{10,11... | collective-permute-start | bytes 3538952 | tf_op jit(solution)/shard_map/ppermute | solution.py:76
  193.3 34.1 %collective-permute-start.19 = (bf16[768,192]{0,1:T(8,128)(2,1)}, bf16[768,192]{0,1:T(8,128)(2,1)}, u32[]{:S(2)}, u32[]{:S(2)}) collective-permute-start(bf16[768,192]{0,1:T(8,128)(2,1)} %convolution_convert_fusion.8), channel_id=1, source_target_pairs={{0,1},{1,0},{2,3},{3,2},{4,5},{5,4},{6,7},{7,6},{8,9},{9,8},{10,11... | collective-permute-start | bytes 884744 | tf_op jit(solution)/shard_map/ppermute | solution.py:76
  224.9 196.6 %all-gather.8.cloned.1.call-start = ((), (), s32[]{:S(2)}) async-start(), calls=%async_computation.11 | async-start | bytes 2949120 | tf_op jit(solution)/shard_map/all_gather | solution.py:277
  232.3 69.0 %collective-permute-start.25 = (bf16[768,768]{1,0:T(8,128)(2,1)}, bf16[768,768]{1,0:T(8,128)(2,1)}, u32[]{:S(2)}, u32[]{:S(2)}) collective-permute-start(bf16[768,768]{1,0:T(8,128)(2,1)} %convolution_convert_fusion), channel_id=1, source_target_pairs={{0,1},{1,0},{2,3},{3,2},{4,5},{5,4},{6,7},{7,6},{8,9},{9,8},{10,11... | collective-permute-start | bytes 3538952 | tf_op jit(solution)/shard_map/ppermute | solution.py:76
  232.4 63.6 %collective-permute-start.16 = (bf16[3,768,192]{1,2,0:T(8,128)(2,1)}, bf16[3,768,192]{1,2,0:T(8,128)(2,1)}, u32[]{:S(2)}, u32[]{:S(2)}) collective-permute-start(bf16[3,768,192]{1,2,0:T(8,128)(2,1)} %fusion.48), channel_id=1, source_target_pairs={{0,1},{1,0},{2,3},{3,2},{4,5},{5,4},{6,7},{7,6},{8,9},{9,8},{10,11... | collective-permute-start | bytes 2654216 | tf_op jit(solution)/shard_map/ppermute | solution.py:76
  291.7 37.2 %all-to-all-start.4 = ((bf16[8,96,512]{2,1,0:T(8,128)(2,1)}), bf16[8,96,512]{2,1,0:T(8,128)(2,1)}, u32[]{:S(2)}, u32[]{:S(2)}) async-start(bf16[8,96,512]{2,1,0:T(8,128)(2,1)} %bitcast.377), calls=%async_computation.4 | async-start | bytes 1572864 | tf_op jit(solution)/shard_map/all_to_all | solution.py:103
  300.7 38.1 %collective-permute-start.24 = (bf16[768,768]{1,0:T(8,128)(2,1)}, bf16[768,768]{1,0:T(8,128)(2,1)}, u32[]{:S(2)}, u32[]{:S(2)}) collective-permute-start(bf16[768,768]{1,0:T(8,128)(2,1)} %convolution_convert_fusion.1), channel_id=1, source_target_pairs={{0,1},{1,0},{2,3},{3,2},{4,5},{5,4},{6,7},{7,6},{8,9},{9,8},{10,11... | collective-permute-start | bytes 3538952 | tf_op jit(solution)/shard_map/ppermute | solution.py:76
  304.9 39.7 %collective-permute-start.26 = (bf16[768,768]{1,0:T(8,128)(2,1)}, bf16[768,768]{1,0:T(8,128)(2,1)}, u32[]{:S(2)}, u32[]{:S(2)}) collective-permute-start(bf16[768,768]{1,0:T(8,128)(2,1)} %add_convert_fusion.1), channel_id=1, source_target_pairs={{0,2},{1,3},{2,0},{3,1},{4,6},{5,7},{6,4},{7,5},{8,10},{9,11},{10,... | collective-permute-start | bytes 3538952 | tf_op jit(solution)/shard_map/ppermute | solution.py:76
  328.9 31.9 %all-to-all-start.6 = ((bf16[8,3,96,192]{2,3,1,0:T(8,128)(2,1)}), bf16[8,3,96,192]{2,3,1,0:T(8,128)(2,1)}, u32[]{:S(2)}, u32[]{:S(2)}) async-start(bf16[8,3,96,192]{2,3,1,0:T(8,128)(2,1)} %bitcast.368), calls=%async_computation.6 | async-start | bytes 2359296 | tf_op jit(solution)/shard_map/all_to_all | solution.py:103
  334.9 100.5 %all-gather.6.cloned.1.call-start = ((), (), s32[]{:S(2)}) async-start(), calls=%async_computation.10 | async-start | bytes 3932160 | tf_op jit(solution)/shard_map/all_gather | solution.py:219
  336.8 29.9 %collective-permute-start.22 = (bf16[768,768]{1,0:T(8,128)(2,1)}, bf16[768,768]{1,0:T(8,128)(2,1)}, u32[]{:S(2)}, u32[]{:S(2)}) collective-permute-start(bf16[768,768]{1,0:T(8,128)(2,1)} %convolution_convert_fusion.2), channel_id=1, source_target_pairs={{0,1},{1,0},{2,3},{3,2},{4,5},{5,4},{6,7},{7,6},{8,9},{9,8},{10,11... | collective-permute-start | bytes 3538952 | tf_op jit(solution)/shard_map/ppermute | solution.py:76
  360.8 37.9 %all-to-all-start.9 = ((bf16[8,96,768]{2,1,0:T(8,128)(2,1)}), bf16[8,96,768]{2,1,0:T(8,128)(2,1)S(1)}, u32[]{:S(2)}, u32[]{:S(2)}) async-start(bf16[8,96,768]{2,1,0:T(8,128)(2,1)} %bitcast.370), calls=%async_computation.9 | async-start | bytes 2359296 | tf_op jit(solution)/shard_map/all_to_all | solution.py:103
  368.8 28.4 %collective-permute-start.23 = (bf16[768,768]{1,0:T(8,128)(2,1)S(1)}, bf16[768,768]{1,0:T(8,128)(2,1)S(1)}, u32[]{:S(2)}, u32[]{:S(2)}) collective-permute-start(bf16[768,768]{1,0:T(8,128)(2,1)S(1)} %add_convert_fusion.3), channel_id=1, source_target_pairs={{0,2},{1,3},{2,0},{3,1},{4,6},{5,7},{6,4},{7,5},{8,10},{9,11},{10,... | collective-permute-start | bytes 3538952 | tf_op jit(solution)/shard_map/ppermute | solution.py:76
  398.6 34.6 %all-to-all-start.8 = ((bf16[8,96,768]{2,1,0:T(8,128)(2,1)}), bf16[8,96,768]{2,1,0:T(8,128)(2,1)}, u32[]{:S(2)}, u32[]{:S(2)}) async-start(bf16[8,96,768]{2,1,0:T(8,128)(2,1)} %bitcast.369), calls=%async_computation.8 | async-start | bytes 2359296 | tf_op jit(solution)/shard_map/all_to_all | solution.py:103
  (108 other events, 595.4 us)
Sparse Core Ops, SparseCore 0:
  232.4 26.7 all-gather.7
  337.3 29.0 all-gather.5

commit v2 on v1

v2 whole, which is shorter than its diff:
```python
import jax
import jax.numpy as jnp
from jax import lax
from jax.experimental import pallas as pl
from jax.experimental.pallas import tpu as pltpu
from jax.sharding import PartitionSpec as P

HD = 64
LT = 384
EPSILON = 1e-06
NEGATIVE = -1000000000.0
BF = jnp.bfloat16
F32 = jnp.float32


def layer_norm(values, gain, bias):
    mean = jnp.mean(values, axis=-1, keepdims=True)
    centred = values - mean
    variance = jnp.mean(centred * centred, axis=-1, keepdims=True)
    inverse = lax.rsqrt(variance + EPSILON)
    normed = centred * inverse
    return (normed * gain + bias, normed, inverse)


def key_mask(seg_row, count):
    length = seg_row.shape[0]
    places = jnp.arange(length, dtype=jnp.int32)
    usable = places < LT + count
    same = seg_row[:, None] == seg_row[None, :]
    return same & (usable[None, :] | (places[:, None] == places[None, :]))


VMEM_BYTES = 52 << 20
ROOT_HALF = 0.7071067811865476
DENSITY = 0.3989422804014327


def dot(a, b):
    return jnp.dot(a, b, preferred_element_type=F32)


def dot_nt(a, b):
    return lax.dot_general(a, b, (((1,), (1,)), ((), ())), preferred_element_type=F32)


def dot_tn(a, b):
    return lax.dot_general(a, b, (((0,), (0,)), ((), ())), preferred_element_type=F32)


def any_specs(count):
    return [pl.BlockSpec(memory_space=pl.ANY)] * count


def smem_spec():
    return [pl.BlockSpec(memory_space=pltpu.SMEM)]


def vmem_specs(count):
    return [pl.BlockSpec(memory_space=pltpu.VMEM)] * count


def call(body, outs, in_specs, out_specs, scratch, flops):
    return pl.pallas_call(
        body,
        out_shape=[jax.ShapeDtypeStruct(shape, kind) for shape, kind in outs],
        in_specs=in_specs,
        out_specs=out_specs,
        scratch_shapes=scratch,
        compiler_params=pltpu.CompilerParams(vmem_limit_bytes=VMEM_BYTES),
        cost_estimate=pl.CostEstimate(flops=flops, bytes_accessed=16 << 20, transcendentals=0),
    )


def attend_kernel(heads, sizes, side_ref, x_ref, z_ref, allow_ref, *rest):
    count = len(sizes)
    shards, rest = regroup(rest, sizes)
    zout_ref, helds, lses = rest[0], rest[1 : 1 + count], rest[1 + count : 1 + 2 * count]
    weights, sems = rest[1 + 2 * count :]
    started, _ = fetch_shards(shards, weights, side_ref[0], sems)
    length, width = x_ref.shape
    group = heads * HD
    block = 128
    lane = lax.broadcasted_iota(jnp.int32, (block, 128), 1)
    for i in range(count):
        for copy in started[i]:
            copy.wait()
        w_ref, held, lse_ref = weights.at[i], helds[i], lses[i]
        mixed = dot(x_ref[...], w_ref[...])
        held[:, group : 2 * group] = (mixed[:, group : 2 * group] * HD ** (-0.5)).astype(BF)
        held[:, 2 * group :] = mixed[:, 2 * group :].astype(BF)

        def rows(b, carry):
            at = pl.ds(pl.multiple_of(b * block, block), block)
            columns = jnp.zeros((block, 128), F32)
            allow = allow_ref[at, :] > 0.5
            for h in range(heads):
                q = held[at, group + h * HD : group + (h + 1) * HD]
                k = held[:, 2 * group + h * HD : 2 * group + (h + 1) * HD]
                v = held[:, 3 * group + h * HD : 3 * group + (h + 1) * HD]
                scores = jnp.where(allow, dot_nt(q, k), NEGATIVE)
                top = jnp.max(scores, axis=1, keepdims=True)
                raised = jnp.exp(scores - top)
                total = jnp.sum(raised, axis=1, keepdims=True)
                context = dot(raised.astype(BF), v) / total
                held[at, h * HD : (h + 1) * HD] = context.astype(BF)
                columns = jnp.where(lane == h, top + jnp.log(total), columns)
            lse_ref[:, at] = columns.T[:8, :]
            return carry

        lax.fori_loop(0, length // block, rows, 0)
        if i == 0:
            zout_ref[...] = z_ref[...] + dot_nt(held[:, :group], w_ref[:, :group])
        else:
            zout_ref[...] += dot_nt(held[:, :group], w_ref[:, :group])


def attend_call(heads, side, x, z, allow, shards):
    length, width = x.shape
    n = len(shards)
    sizes = [len(pieces) for pieces in shards]
    outs = [((length, width), F32)] + [((length, width), BF)] * n + [((8, length), F32)] * n
    got = call(
        lambda *refs: attend_kernel(heads, sizes, *refs),
        outs,
        smem_spec() + vmem_specs(3) + any_specs(sum(sizes)),
        vmem_specs(len(outs)),
        [pltpu.VMEM((n, width, width), BF), pltpu.SemaphoreType.DMA((sum(sizes),))],
        n * 2_000_000_000,
    )(side, x, z, allow, *sum(shards, []))
    return got[0], got[1 : 1 + n], got[1 + n :]


def attend_back_kernel(heads, sizes, side_ref, g_ref, gt_ref, xt_ref, acc_ref, allow_ref, *rest):
    count = len(sizes)
    shards, rest = regroup(rest, sizes)
    helds, lses = rest[:count], rest[count : 2 * count]
    accout_ref, terms = rest[2 * count], rest[2 * count + 1 : 3 * count + 1]
    gc_ref, grads, dq_ref, delta_ref, weights, sems = rest[3 * count + 1 :]
    started, _ = fetch_shards(shards, weights, side_ref[0], sems)
    length, width = g_ref.shape
    group = heads * HD
    block = 128
    lane = lax.broadcasted_iota(jnp.int32, (length, 128), 1)
    for i in range(count):
        for copy in started[i]:
            copy.wait()
        w_ref, held, lse_ref = weights.at[i], helds[i], lses[i]
        low = dot(g_ref[...], w_ref[:, :group]).astype(BF)
        gc_ref[...] = low
        product = low.astype(F32) * held[:, :group].astype(F32)
        columns = jnp.zeros((length, 128), F32)
        for h in range(heads):
            inner = jnp.sum(product[:, h * HD : (h + 1) * HD], axis=1, keepdims=True)
            columns = jnp.where(lane == h, inner, columns)
        delta_ref[...] = columns.T[:8, :]
        dq_ref[...] = jnp.zeros_like(dq_ref)
        grads[:, :group] = jnp.zeros((length, group), BF)

        def rows(b, carry):
            at = pl.ds(pl.multiple_of(b * block, block), block)
            allow = allow_ref[at, :] > 0.5
            for h in range(heads):
                q = held[:, group + h * HD : group + (h + 1) * HD]
                k = held[at, 2 * group + h * HD : 2 * group + (h + 1) * HD]
                v = held[at, 3 * group + h * HD : 3 * group + (h + 1) * HD]
                gc = gc_ref[:, h * HD : (h + 1) * HD]
                scores = jnp.where(allow, dot_nt(k, q), NEGATIVE)
                probs = jnp.exp(scores - lse_ref[h : h + 1, :])
                grad_probs = dot_nt(v, gc)
                grad_scores = (probs * (grad_probs - delta_ref[h : h + 1, :])).astype(BF)
                grads[at, 3 * group + h * HD : 3 * group + (h + 1) * HD] = dot(
                    probs.astype(BF), gc
                ).astype(BF)
                grads[at, 2 * group + h * HD : 2 * group + (h + 1) * HD] = dot(
                    grad_scores, q
                ).astype(BF)
                dq_ref[h * HD : (h + 1) * HD, :] += dot_tn(k, grad_scores)
            return carry

        lax.fori_loop(0, length // block, rows, 0)
        grads[:, group : 2 * group] = (dq_ref[...] * HD ** (-0.5)).T.astype(BF)
        if i == 0:
            accout_ref[...] = acc_ref[...] + dot_nt(grads[...], w_ref[...])
        else:
            accout_ref[...] += dot_nt(grads[...], w_ref[...])
        terms[i][...] = dot(xt_ref[...], grads[...]).astype(BF)
        terms[i][:, :group] = dot(gt_ref[...], held[:, :group]).astype(BF)


def attend_back_call(heads, side, g, gt, xt, acc, allow, shards, helds, lses):
    length, width = g.shape
    n = len(shards)
    sizes = [len(pieces) for pieces in shards]
    group = heads * HD
    outs = [((length, width), F32)] + [((width, width), BF)] * n
    got = call(
        lambda *refs: attend_back_kernel(heads, sizes, *refs),
        outs,
        smem_spec() + vmem_specs(5) + any_specs(sum(sizes)) + vmem_specs(2 * n),
        vmem_specs(len(outs)),
        [
            pltpu.VMEM((length, group), BF),
            pltpu.VMEM((length, width), BF),
            pltpu.VMEM((group, length), F32),
            pltpu.VMEM((8, length), F32),
            pltpu.VMEM((n, width, width), BF),
            pltpu.SemaphoreType.DMA((sum(sizes),)),
        ],
        n * 4_000_000_000,
    )(side, g, gt, xt, acc, allow, *sum(shards, []), *helds, *lses)
    return got[0], got[1:]


def erf(x):
    x = jnp.clip(x, -4.0, 4.0)
    s = x * x
    top = jnp.full_like(x, -2.72614225801306e-10)
    for c in (
        2.77068142495902e-08,
        -2.10102402082508e-06,
        -5.69250639462346e-05,
        -7.34990630326855e-04,
        -2.95459980854025e-03,
        -1.60960333262415e-02,
    ):
        top = top * s + c
    base = jnp.full_like(x, -1.45660718464996e-05)
    for c in (
        -2.13374055278905e-04,
        -1.68282697438203e-03,
        -7.37332916720468e-03,
        -1.42647390514189e-02,
    ):
        base = base * s + c
    return x * top / base


def norm_back(grad, values, gain):
    _, normed, inverse = layer_norm(values, gain, 0.0)
    scaled = grad * gain
    mean_grad = jnp.mean(scaled, axis=-1, keepdims=True)
    mean_proj = jnp.mean(scaled * normed, axis=-1, keepdims=True)
    return (
        inverse * (scaled - mean_grad - normed * mean_proj),
        jnp.sum(grad * normed, axis=0, keepdims=True),
        jnp.sum(grad, axis=0, keepdims=True),
    )


def regroup(flat, sizes):
    flat = list(flat)
    return [[flat.pop(0) for _ in range(size)] for size in sizes], flat


def fetch_shards(shards, target, side, sems, base=0):
    started = []
    for i, pieces in enumerate(shards):
        copies = []
        for j, piece in enumerate(pieces):
            rows = piece.shape[0]
            at = pl.ds(pl.multiple_of((side if j == 0 else 1 - side) * rows, 16), rows)
            place = target.at[i] if len(pieces) == 1 else target.at[i, at]
            copies.append(pltpu.make_async_copy(piece, place, sems.at[base]))
            copies[-1].start()
            base += 1
        started.append(copies)
    return started, base


def forward_kernel(
    parts, sizes, side_ref, z_ref, cot_ref, gm_ref, bm_ref, gf_ref, bf_ref, *rest
):
    up_shards, rest = regroup(rest, sizes)
    down_shards, rest = regroup(rest, sizes)
    slope_ref, terms = rest[0], rest[1 : parts + 1]
    out_ref, x1t_ref, gx2_ref, g_ref, vec_ref = rest[parts + 1 : parts + 6]
    ups, downs, actives, ffn_ref, x1_ref, gt_ref, sems = rest[parts + 6 :]
    up_started, base = fetch_shards(up_shards, ups, side_ref[1], sems)
    down_started, _ = fetch_shards(down_shards, downs, side_ref[2], sems, base)
    length, width = z_ref.shape
    block = 256
    vec_ref[...] = jnp.zeros_like(vec_ref)
    for b in range(length // block):
        at = slice(b * block, (b + 1) * block)
        hidden1, _, _ = layer_norm(z_ref[at, :], gm_ref[...], bm_ref[...])
        x1_ref[at, :] = hidden1.astype(BF)
        ffn_ref[at, :] = hidden1
        for k in range(parts):
            if b == 0:
                for copy in up_started[k]:
                    copy.wait()
            before = dot(x1_ref[at, :], ups[k])
            half = 0.5 + 0.5 * erf(before * ROOT_HALF)
            slope_ref[k, at, :] = (
                half + before * (DENSITY * jnp.exp(-0.5 * before * before))
            ).astype(BF)
            actives[k, at, :] = (before * half).astype(BF)
            if b == 0:
                for copy in down_started[k]:
                    copy.wait()
            ffn_ref[at, :] += dot(actives[k, at, :], downs[k])
        final, normed, inverse = layer_norm(ffn_ref[at, :], gf_ref[...], bf_ref[...])
        out_ref[at, :] = final.astype(BF)
        grad_in, gain_sum, bias_sum = norm_back(
            cot_ref[at, :].astype(F32), ffn_ref[at, :], gf_ref[...]
        )
        vec_ref[0:1, :] += gain_sum
        vec_ref[1:2, :] += bias_sum
        gx2_ref[at, :] = grad_in
        g_ref[at, :] = grad_in.astype(BF)
    gt_ref[...] = g_ref[...].T
    for k in range(parts):
        terms[k][...] = dot(gt_ref[...], actives[k]).astype(BF)
    x1t_ref[...] = x1_ref[...].T


def forward_call(side, z, cot, gm, bm, gf, bf, up, down):
    length, width = z.shape
    n = len(up)
    sizes = [len(pieces) for pieces in up]
    inner = up[0][0].shape[1]
    outs = (
        [((n, length, inner), BF)]
        + [((width, inner), BF)] * n
        + [
            ((length, width), BF),
            ((width, length), BF),
            ((length, width), F32),
            ((length, width), BF),
            ((8, width), F32),
        ]
    )
    got = call(
        lambda *refs: forward_kernel(n, sizes, *refs),
        outs,
        smem_spec() + vmem_specs(6) + any_specs(2 * sum(sizes)),
        vmem_specs(len(outs)),
        [
            pltpu.VMEM((n, width, inner), BF),
            pltpu.VMEM((n, inner, width), BF),
            pltpu.VMEM((n, length, inner), BF),
            pltpu.VMEM((length, width), F32),
            pltpu.VMEM((length, width), BF),
            pltpu.VMEM((width, length), BF),
            pltpu.SemaphoreType.DMA((2 * sum(sizes),)),
        ],
        8_000_000_000,
    )(side, z, cot, gm, bm, gf, bf, *sum(up, []), *sum(down, []))
    return got[0], got[1 : n + 1], got[n + 1 :]


def backward_kernel(
    parts, sizes, side_ref, z_ref, gx2_ref, g_ref, x1t_ref, gm_ref, *rest
):
    up_shards, rest = regroup(rest, sizes)
    down_shards, rest = regroup(rest, sizes)
    slope_any, *rest = rest
    terms = rest[:parts]
    gx1_ref, ga_ref, gat_ref, vec_ref, gb_ref, ups, downs, slopes, sems = rest[parts:]
    down_started, base = fetch_shards(down_shards, downs, side_ref[2], sems)
    up_started, base = fetch_shards(up_shards, ups, side_ref[1], sems, base)
    slope_copies = []
    for k in range(parts):
        slope_copies.append(
            pltpu.make_async_copy(slope_any.at[k], slopes.at[k], sems.at[base + k])
        )
        slope_copies[k].start()
    gx1_ref[...] = gx2_ref[...]
    for k in sorted(range(parts), key=lambda k: (1 - k % 2, k)):
        for copy in (*down_started[k], slope_copies[k], *up_started[k]):
            copy.wait()
        gb_ref[...] = (dot_nt(g_ref[...], downs[k]) * slopes[k].astype(F32)).astype(BF)
        terms[k][...] = dot(x1t_ref[...], gb_ref[...]).astype(BF)
        gx1_ref[...] += dot_nt(gb_ref[...], ups[k])
    grad_in, gain_sum, bias_sum = norm_back(gx1_ref[...], z_ref[...], gm_ref[...])
    vec_ref[...] = jnp.zeros_like(vec_ref)
    vec_ref[0:1, :] = gain_sum
    vec_ref[1:2, :] = bias_sum
    gx1_ref[...] = grad_in
    ga_ref[...] = grad_in.astype(BF)
    gat_ref[...] = ga_ref[...].T


def backward_call(side, z, gx2, g, x1t, gm, up, down, slope):
    length, width = z.shape
    n = len(up)
    sizes = [len(pieces) for pieces in up]
    inner = up[0][0].shape[1]
    outs = [((width, inner), BF)] * n + [
        ((length, width), F32),
        ((length, width), BF),
        ((width, length), BF),
        ((8, width), F32),
    ]
    got = call(
        lambda *refs: backward_kernel(n, sizes, *refs),
        outs,
        smem_spec() + vmem_specs(5) + any_specs(2 * sum(sizes) + 1),
        vmem_specs(len(outs)),
        [
            pltpu.VMEM((length, inner), BF),
            pltpu.VMEM((n, width, inner), BF),
            pltpu.VMEM((n, inner, width), BF),
            pltpu.VMEM((n, length, inner), BF),
            pltpu.SemaphoreType.DMA((2 * sum(sizes) + n,)),
        ],
        8_000_000_000,
    )(side, z, gx2, g, x1t, gm, *sum(up, []), *sum(down, []), slope)
    return got[:n], got[n:]


def pack_kernel(mix_ref, qkv_ref, out_ref):
    group = mix_ref.shape[0]
    out_ref[:, :group] = mix_ref[...].T
    for c in range(qkv_ref.shape[0]):
        out_ref[:, (c + 1) * group : (c + 2) * group] = qkv_ref[c]


def choose(index, count, step, source, store):
    for c in range(count):

        @pl.when(index == c)
        def _(c=c):
            store(source[:, c * step : (c + 1) * step])


def project_kernel(parts, mine_ref, feats_ref, w_ref, *rest):
    outs, full = rest[:parts], rest[parts]
    full[...] = dot(feats_ref[...], w_ref[...])
    step = outs[0].shape[1]
    for k, out in enumerate(outs):

        def store(value, out=out):
            out[...] = value.astype(out.dtype)

        choose(mine_ref[0] ^ k, parts, step, full, store)


def outgoing_kernel(parts, mine_ref, own_ref, near_ref, far_ref, box_ref, table_ref, pick_ref, out_ref, full, low):
    stored, chunk = own_ref.shape
    bins = table_ref.shape[1]
    places = lax.broadcasted_iota(jnp.int32, (stored, bins), 1)
    full[...] = jnp.zeros_like(full)
    for c in range(table_ref.shape[0]):
        full[...] += dot((box_ref[:, c : c + 1] == places).astype(BF), table_ref[c])

    def store(value):
        total = own_ref[...] + near_ref[...].astype(F32) + far_ref[...].astype(F32)
        low[...] = (total + value).astype(BF)

    choose(mine_ref[0], parts, chunk, full, store)
    slots = out_ref.shape[0]
    regions = lax.broadcasted_iota(jnp.int32, (slots, stored), 1)
    out_ref[...] = dot((pick_ref[...] == regions).astype(BF), low[...]).astype(BF)


def move_rows_kernel(pick_ref, rows_ref, out_ref):
    shape = (out_ref.shape[0], rows_ref.shape[0])
    places = lax.broadcasted_iota(jnp.int32, shape, 0)
    out_ref[...] = dot((pick_ref[...] == places).astype(BF), rows_ref[...]).astype(BF)


def take_rows_kernel(pick_ref, rows_ref, out_ref):
    shape = (out_ref.shape[0], rows_ref.shape[0])
    places = lax.broadcasted_iota(jnp.int32, shape, 1)
    out_ref[...] = dot((pick_ref[...] == places).astype(BF), rows_ref[...]).astype(BF)


def embed_kernel(parts, text_ref, placed_ref, type_ref, pos_ref, gain_ref, bias_ref, emb_ref, hid_ref, x_ref, xt_ref):
    text_len = text_ref.shape[0]
    chunk = placed_ref.shape[2]
    types = type_ref[...].astype(F32)
    pos = pos_ref[...].astype(F32)
    emb_ref[:text_len, :] = text_ref[...].astype(F32) + types[0:1, :] + pos[:text_len, :]
    for c in range(parts):
        at = slice(c * chunk, (c + 1) * chunk)
        emb_ref[text_len:, at] = placed_ref[c].astype(F32)
    emb_ref[text_len:, :] += types[1:2, :] + pos[text_len:, :]
    hidden, _, _ = layer_norm(emb_ref[...], gain_ref[...], bias_ref[...])
    hid_ref[...] = hidden
    x_ref[...] = hidden.astype(BF)
    xt_ref[...] = x_ref[...].T


def embed_back_kernel(parts, grad_ref, emb_ref, gain_ref, mid_ref, fin_ref, text_ref, reg_ref, rest_ref, vec):
    text_len = text_ref.shape[0]
    chunk = reg_ref.shape[2]
    grad_in, gain_sum, bias_sum = norm_back(grad_ref[...], emb_ref[...], gain_ref[...])
    low = grad_in.astype(BF)
    text_ref[...] = low[:text_len, :]
    vec[...] = jnp.zeros_like(vec)
    vec[0:1, :] = jnp.sum(grad_in[:text_len, :], axis=0, keepdims=True)
    vec[1:2, :] = jnp.sum(grad_in[text_len:, :], axis=0, keepdims=True)
    vec[2:3, :] = gain_sum
    vec[3:4, :] = bias_sum
    vec[4:6, :] = mid_ref[0:2, :]
    vec[6:8, :] = fin_ref[0:2, :]
    vectors = vec[...].astype(BF)
    for c in range(parts):
        at = slice(c * chunk, (c + 1) * chunk)
        reg_ref[c] = low[text_len:, at]
        rest_ref[c, :text_len, :] = low[:text_len, at]
        rest_ref[c, text_len:, :] = vectors[:, at]


def box_kernel(pick_ref, rows_ref, box_ref, chunk_ref, term_ref):
    move_rows_kernel(pick_ref, rows_ref, chunk_ref)
    bins = term_ref.shape[1]
    places = lax.broadcasted_iota(jnp.int32, (bins, chunk_ref.shape[0]), 0)
    for c in range(term_ref.shape[0]):
        term_ref[c] = dot((box_ref[c : c + 1, :] == places).astype(BF), chunk_ref[...])


def project_back_kernel(parts, chunks_ref, feats_ref, w_ref, grad_ref, term_ref, full):
    chunk = chunks_ref.shape[2]
    for c in range(parts):
        full[:, c * chunk : (c + 1) * chunk] = chunks_ref[c]
    grad_ref[...] = dot_nt(full[...], w_ref[...])
    term_ref[...] = dot(full[...].T, feats_ref[...]).astype(BF)


def spread_kernel(parts, chunks_ref, out_ref):
    chunk = chunks_ref.shape[2]
    for c in range(parts):
        out_ref[:, c * chunk : (c + 1) * chunk] = chunks_ref[c]


def small_call(body, args, outs, scratch=(), scalar=False, flops=500_000_000):
    specs = vmem_specs(len(args))
    if scalar:
        specs[0] = pl.BlockSpec(memory_space=pltpu.SMEM)
    got = call(body, outs, specs, vmem_specs(len(outs)), list(scratch), flops)(*args)
    return got[0] if len(outs) == 1 else got


def swap(value, axis, bit):
    count = lax.axis_size(axis)
    return lax.ppermute(value, axis, [(i, i ^ bit) for i in range(count)])


def bits_of(axis):
    count = lax.axis_size(axis)
    return [1 << i for i in range(count.bit_length() - 1)]


def tie(first, second):
    return lax.optimization_barrier((first, second))


def far_half(shard, bit):
    rows = shard.shape[0] // 2
    side = (lax.axis_index("dp") // bit) % 2
    return swap(lax.dynamic_slice_in_dim(shard, side * rows, rows, 0), "tensor", 2)


def gather_shards(shard, half, other):
    return [
        [shard],
        [swap(shard, "tensor", 1)],
        [half, other],
        [swap(half, "tensor", 1), swap(other, "tensor", 1)],
    ]


def fold(held, bit):
    moved = {
        k: swap(total(v).astype(BF), "tensor", bit) for k, v in held.items() if k & bit
    }
    return {k: v + [moved[k | bit]] for k, v in held.items() if not k & bit}


def total(summands):
    return sum(value.astype(F32) for value in summands)


def terms_of(terms):
    return {k: [term] for k, term in enumerate(terms)}


def sum_over_dp(term):
    bits = bits_of("dp")
    me = lax.axis_index("dp")
    rows, columns = term.shape
    held = term.reshape([2] * len(bits) + [rows >> len(bits), columns])
    for step, bit in enumerate(bits):
        axis = len(bits) - 1 - step
        side = (me // bit) % 2
        sent = lax.dynamic_index_in_dim(held, 1 - side, axis, keepdims=False)
        kept = lax.dynamic_index_in_dim(held, side, axis, keepdims=False)
        held = kept.astype(F32) + swap(sent.astype(BF), "dp", bit).astype(F32)
    return held


def local(
    text_embed,
    region_feats,
    box_coords,
    seg_ids,
    region_counts,
    send_index,
    recv_pos,
    w_proj,
    box_table,
    type_embed,
    pos_embed,
    gain_embed,
    bias_embed,
    w_qkv,
    w_mix,
    gain_mid,
    bias_mid,
    w_up,
    w_down,
    gain_final,
    bias_final,
    cotangent,
):
    parts = lax.axis_size("tensor")
    peers = lax.axis_size("dp")
    mine = lax.axis_index("tensor")
    mine_now = mine.reshape(1).astype(jnp.int32)
    dp_now = lax.axis_index("dp")
    sides = jnp.stack([dp_now % 2, dp_now % 2, (dp_now // 2) % 2]).astype(jnp.int32)
    row_count, text_len, width = text_embed.shape
    assert row_count == parts == 4
    length = seg_ids.shape[1]
    slots = length - text_len
    stored, depth = region_feats.shape
    capacity = send_index.shape[2]
    bins = box_table.shape[1]
    group = w_qkv.shape[2]
    heads = group // HD
    chunk = width // parts
    share = width // peers
    wire = peers * capacity

    def own(array):
        return lax.dynamic_index_in_dim(array, mine, 0, keepdims=False)

    def line(vector):
        return vector.reshape(1, width)

    held = small_call(
        lambda *refs: project_kernel(parts, *refs),
        [mine_now, region_feats, w_proj],
        [((stored, chunk), F32 if k == 0 else BF) for k in range(parts)],
        [pltpu.VMEM((stored, width), F32)],
        scalar=True,
    )
    near = swap(held[1], "tensor", 1)
    across = (held[2].astype(F32) + swap(held[3], "tensor", 1).astype(F32)).astype(BF)

    across, (w_mix, w_qkv) = tie(across, (w_mix, w_qkv))
    far = swap(across, "tensor", 2)
    packed = small_call(pack_kernel, [w_mix, w_qkv], [((width, width), BF)])
    far, packed = tie(far, packed)
    att_half = far_half(packed, 1)

    send_flat = send_index.reshape(-1)
    recv_flat = recv_pos.reshape(-1)
    recv_slot = jnp.where(
        recv_flat >= 0,
        (recv_flat // length) * slots + recv_flat % length - text_len,
        -1,
    )
    send_line, send_column = send_flat.reshape(1, wire), send_flat.reshape(wire, 1)
    recv_line, recv_column = recv_slot.reshape(1, wire), recv_slot.reshape(wire, 1)
    outgoing = small_call(
        lambda *refs: outgoing_kernel(parts, *refs),
        [mine_now, held[0], near, far, box_coords, box_table, send_column],
        [((wire, chunk), BF)],
        [pltpu.VMEM((stored, width), F32), pltpu.VMEM((stored, chunk), BF)],
        scalar=True,
    )
    outgoing, w_up = tie(outgoing, w_up)
    up_half = far_half(w_up, 1)
    incoming = lax.all_to_all(
        outgoing.reshape(peers, capacity, chunk), "dp", 0, 0, tiled=True
    ).reshape(wire, chunk)
    incoming, att_half = tie(incoming, att_half)
    att_other = swap(att_half, "dp", 1)
    placed = small_call(
        move_rows_kernel, [recv_line, incoming], [((row_count * slots, chunk), BF)]
    )
    placed = lax.all_to_all(placed.reshape(parts, slots, chunk), "tensor", 0, 0, tiled=True)
    placed, w_down = tie(placed, w_down)
    down_half = far_half(w_down, 2)

    embedded, hidden0, inputs0, inputs0_turned = small_call(
        lambda *refs: embed_kernel(parts, *refs),
        [own(text_embed), placed, type_embed, pos_embed, line(gain_embed), line(bias_embed)],
        [
            ((length, width), F32),
            ((length, width), F32),
            ((length, width), BF),
            ((width, length), BF),
        ],
    )
    allowed = key_mask(own(seg_ids), own(region_counts))
    allow = allowed.astype(F32)
    allow_turned = allowed.T.astype(F32)

    (hidden0, inputs0), (up_half, att_other) = tie((hidden0, inputs0), (up_half, att_other))
    up_other = swap(up_half, "dp", 1)
    att_shards = gather_shards(packed, att_half, att_other)
    z, near_helds, near_lses = attend_call(heads, sides, inputs0, hidden0, allow, att_shards[:2])
    z, (up_other, down_half) = tie(z, (up_other, down_half))
    down_other = swap(down_half, "dp", 2)
    up = gather_shards(w_up, up_half, up_other)
    z, far_helds, far_lses = attend_call(heads, sides, inputs0, z, allow, att_shards[2:])
    helds, lses = near_helds + far_helds, near_lses + far_lses
    z, down_other = tie(z, down_other)
    down = gather_shards(w_down, down_half, down_other)
    slopes, down_terms, (final, x1t, grad_x2, grad_ffn, final_vectors) = forward_call(
        sides,
        z,
        own(cotangent),
        line(gain_mid),
        line(bias_mid),
        line(gain_final),
        line(bias_final),
        up,
        down,
    )
    layer_output = lax.all_gather(final, "tensor", axis=0, tiled=False)
    sum_down = fold(terms_of(down_terms), 1)

    up_terms, (grad_x1, grad_attn, grad_attn_turned, mid_vectors) = backward_call(
        sides, z, grad_x2, grad_ffn, x1t, line(gain_mid), up, down, slopes
    )
    (grad_attn, grad_x1), sum_down = tie((grad_attn, grad_x1), sum_down)
    sum_down = fold(sum_down, 2)[0]
    sum_up = fold(terms_of(up_terms), 1)
    total0 = grad_x1
    att_terms = [None] * parts
    for at in (1, 0):
        picked = range(at, parts, 2)
        total0, terms = attend_back_call(
            heads,
            sides,
            grad_attn,
            grad_attn_turned,
            inputs0_turned,
            total0,
            allow_turned,
            [att_shards[k] for k in picked],
            [helds[k] for k in picked],
            [lses[k] for k in picked],
        )
        for k, term in zip(picked, terms, strict=True):
            att_terms[k] = term
        if at:
            total0, sum_up = tie(total0, sum_up)
            sum_up = fold(sum_up, 2)[0]
    total0, sum_down = tie(total0, sum_down)
    sum_att = fold(terms_of(att_terms), 1)

    text_own, regions_out, rest_out = small_call(
        lambda *refs: embed_back_kernel(parts, *refs),
        [total0, embedded, line(gain_embed), mid_vectors, final_vectors],
        [
            ((text_len, width), BF),
            ((parts, slots, chunk), BF),
            ((parts, text_len + 16, chunk), BF),
        ],
        [pltpu.VMEM((16, width), F32)],
    )
    regions_in = lax.all_to_all(regions_out, "tensor", 0, 0, tiled=True)
    regions_in, sum_att = tie(regions_in, sum_att)
    sum_att = fold(sum_att, 2)[0]
    returning = small_call(
        take_rows_kernel,
        [recv_column, regions_in.reshape(row_count * slots, chunk)],
        [((wire, chunk), BF)],
    )
    returned = lax.all_to_all(
        returning.reshape(peers, capacity, chunk), "dp", 0, 0, tiled=True
    ).reshape(wire, chunk)
    region_chunk, box_term = small_call(
        box_kernel,
        [send_line, returned, box_coords.T],
        [((stored, chunk), BF), ((box_table.shape[0], bins, chunk), F32)],
    )
    region_chunks = lax.all_gather(region_chunk, "tensor", axis=0, tiled=False)
    feat_grad, proj_term = small_call(
        lambda *refs: project_back_kernel(parts, *refs),
        [region_chunks, region_feats, w_proj],
        [((stored, depth), F32), ((width, depth), BF)],
        [pltpu.VMEM((stored, width), BF)],
    )

    rest_in = lax.all_to_all(rest_out, "tensor", 0, 0, tiled=True)
    text_grad = lax.all_gather(text_own, "tensor", axis=0, tiled=False).astype(F32)
    summed = jnp.sum(rest_in.astype(F32), axis=0)
    pos_term = jnp.concatenate(
        [summed[:text_len], jnp.sum(regions_in.astype(F32), axis=0)], axis=0
    )
    bin_share = bins // peers
    pos_share = length // peers
    bundle = jnp.concatenate(
        [
            pos_term.reshape(peers, pos_share, chunk),
            box_term.reshape(-1, peers, bin_share, chunk)
            .transpose(1, 0, 2, 3)
            .reshape(peers, -1, chunk),
            jnp.broadcast_to(summed[text_len:], (peers, 16, chunk)),
        ],
        axis=1,
    ).astype(BF)
    bundle = jnp.sum(
        lax.all_to_all(bundle, "dp", 0, 0, tiled=True).astype(F32), axis=0
    )
    bundle = lax.all_gather(bundle, "tensor", axis=0, tiled=False)
    bundle = small_call(
        lambda *refs: spread_kernel(parts, *refs), [bundle], [((bundle.shape[1], width), F32)]
    )
    grad_pos = bundle[:pos_share]
    grad_box = bundle[pos_share:-16].reshape(-1, bin_share, width)
    vectors = lax.dynamic_slice_in_dim(bundle[-16:], lax.axis_index("dp") * share, share, 1)

    grad_down = sum_over_dp(total(sum_down)).T
    grad_up = sum_over_dp(total(sum_up))
    grad_att = sum_over_dp(total(sum_att))
    grad_mix = grad_att[:, :group].T
    grad_qkv = grad_att[:, group:].reshape(share, 3, group).transpose(1, 0, 2)
    grad_proj = sum_over_dp(proj_term).T
    return (
        layer_output,
        text_grad,
        feat_grad,
        grad_proj,
        grad_box,
        vectors[:2],
        grad_pos,
        vectors[2],
        vectors[3],
        grad_qkv,
        grad_mix,
        vectors[4],
        vectors[5],
        grad_up,
        grad_down,
        vectors[6],
        vectors[7],
    )


def solution(mesh):
    return jax.shard_map(
        local,
        mesh=mesh,
        in_specs=(
            P("dp", None, None),
            P("dp", "tensor"),
            P("dp", None),
            P("dp", None),
            P("dp"),
            P("dp", None, None),
            P("dp", None, None),
            P("tensor", None),
            P(),
            P(),
            P(),
            P(),
            P(),
            P(None, None, "tensor"),
            P("tensor", None),
            P(),
            P(),
            P(None, "tensor"),
            P("tensor", None),
            P(),
            P(),
            P("dp", None, None),
        ),
        out_specs=(
            P("dp", None, None),
            P("dp", None, None),
            P("dp", "tensor"),
            P("tensor", "dp"),
            P(None, "dp", None),
            P(None, "dp"),
            P("dp", None),
            P("dp"),
            P("dp"),
            P(None, "dp", "tensor"),
            P("tensor", "dp"),
            P("dp"),
            P("dp"),
            P("dp", "tensor"),
            P("tensor", "dp"),
            P("dp"),
            P("dp"),
        ),
        check_vma=False,
    )
```

time: 453 us -> 375 us (0.83)
  Pallas kernels: 0 us -> 139 us
  matrix products: 130 us -> 0 us
  waiting for transfers between devices: 131 us -> 49.2 us
  blocking collectives: 14.4 us -> 26.7 us
  other arithmetic: 44.3 us -> 35.7 us
  starting transfers between devices: 60.8 us -> 53.9 us
    pallas_call x0 -> x16, Pallas kernels: none -> 139 us  [the longest x2 41.2 us: attend_back_call(): call(lambda *refs: attend_back_kernel(heads, sizes, *refs), outs, smem_sp...]
    dot_general x79 -> x0, matrix products: 124 us -> none  [the longest x4 26.8 us: local(): before = jnp.dot(inputs1, up_shards[k], preferred_element_type=F32)]
    ppermute x27 -> x39, waiting for transfers between devices: 81.5 us -> 34.5 us  [swap(): return lax.ppermute(value, axis, [(i, i ^ bit) for i in range(count)])]
    all_to_all x7 -> x3, waiting for transfers between devices: 34.1 us -> 2.5 us  [the longest x1 2.19 us: local(): rest_in = lax.all_to_all(rest_out, 'tensor', 0, 0, tiled=True)]
    all_to_all x7 -> x3, starting transfers between devices: 32.4 us -> 11.2 us  [the longest x1 4.33 us: local(): lax.all_to_all(bundle, 'dp', 0, 0, tiled=True).astype(F32)]
    ppermute x27 -> x39, starting transfers between devices: 14.8 us -> 29.1 us  [swap(): return lax.ppermute(value, axis, [(i, i ^ bit) for i in range(count)])]
    add x5 -> x13, other arithmetic: 1.23 us -> 14.4 us  [the longest x3 7.59 us: total(): return sum((value.astype(F32) for value in summands))]
    reduce_sum x16 -> x3, other arithmetic: 15.5 us -> 2.46 us  [the longest x1 1.26 us: local(): summed = jnp.sum(rest_in.astype(F32), axis=0)]
  transfers between devices with their start and end apart: 39 -> 47, of which waited for: 15 -> 16; matrix products, arithmetic and copies ran while one was open for 37% -> 17% of each run, Pallas kernels for 0% -> 31%
where the time goes in v2:
time: 375 us; the launch traced here: 369 us
  Pallas kernels  139 us (37%)
  starting transfers between devices  53.9 us (14%)
  waiting for transfers between devices  49.2 us (13%)
  local copies, waits for them, and re-layouts  47.7 us (13%)
  other arithmetic  35.7 us (10%)
  blocking collectives  26.7 us (7%)
  between operations  16.1 us (4%)
    pallas_call x2, Pallas kernels, attend_back_call(): call(lambda *refs: attend_back_kernel(heads, sizes, *refs), outs, smem_sp...  41.2 us
    pallas_call x2, Pallas kernels, attend_call(): call(lambda *refs: attend_kernel(heads, sizes, *refs), outs, smem_spec()...  37.9 us
    ppermute x39, waiting for transfers between devices, swap(): return lax.ppermute(value, axis, [(i, i ^ bit) for i in range(count)])  34.5 us
    ppermute x39, starting transfers between devices, swap(): return lax.ppermute(value, axis, [(i, i ^ bit) for i in range(count)])  29.1 us
    pallas_call x1, Pallas kernels, forward_call(): call(lambda *refs: forward_kernel(n, sizes, *refs), outs, smem_spec() + v...  20.7 us
    pallas_call x10, Pallas kernels, small_call(): call(body, outs, specs, vmem_specs(len(outs)), list(scratch), flops)(*args)  20.4 us
    all_gather x1, blocking collectives, local(): region_chunks = lax.all_gather(region_chunk, 'tensor', axis=0, tiled=False)  20.1 us
    pallas_call x1, Pallas kernels, backward_call(): call(lambda *refs: backward_kernel(n, sizes, *refs), outs, smem_spec() +...  19.2 us
  transfers between devices with their start and end apart: 47, of which 16 were waited for; matrix products, arithmetic and copies ran while one was open for 17% of the time, Pallas kernels for 31%

profile of v2, /device:TPU:0, one launch (start us, length us, event | category | flops | bytes accessed | tf_op | source)
XLA Modules:
  0.0 368.8 jit_solution(9614231207374613617)
XLA Ops:
  28.0 3.8 %shard_map.343 = bf16[768,192]{1,0:T(8,128)(2,1)} custom-call(s32[1]{0:T(128)} %bitcast.3.refs_0_, f32[384,192]{1,0:T(8,128)S(1)} %copy-done.8, bf16[384,192]{1,0:T(8,128)(2,1)} %collective-permute-done.refs_2_, bf16[384,192]{1,0:T(8,128)(2,1)} %collective-permute-done.2.refs_3_, s32[384,4]{1,0:T(8,128)S(1)} %copy-done.3, bf16[4,128,768]{2,1,0:T(8,128)(2,1)} %refs_5_.1, ...), custom_call_target="tpu_custom_call" | custom-call | flops 500000000 | bytes 16777216 | tf_op jit(solution)/shard_map/pallas_call | solution.py:532
  31.8 5.8 %all-to-all-start = ((bf16[8,96,192]{2,1,0:T(8,128)(2,1)}), bf16[8,96,192]{2,1,0:T(8,128)(2,1)S(1)}, u32[]{:S(2)}, u32[]{:S(2)}) async-start(bf16[8,96,192]{2,1,0:T(8,128)(2,1)} %bitcast.4), calls=%async_computation | async-start | bytes 786432 | tf_op jit(solution)/shard_map/all_to_all | solution.py:677
  42.1 6.5 %all-to-all-done = bf16[8,96,192]{2,1,0:T(8,128)(2,1)S(1)} async-done(((bf16[8,96,192]{2,1,0:T(8,128)(2,1)}), bf16[8,96,192]{2,1,0:T(8,128)(2,1)S(1)}, u32[]{:S(2)}, u32[]{:S(2)}) %all-to-all-start) | async-done | bytes 294944 | tf_op jit(solution)/shard_map/all_to_all | solution.py:677
  54.1 4.0 %all-to-all-start.1 = ((bf16[4,128,192]{1,2,0:T(8,128)(2,1)}), bf16[4,128,192]{1,2,0:T(8,128)(2,1)}, u32[]{:S(2)}, u32[]{:S(2)}) async-start(bf16[4,128,192]{1,2,0:T(8,128)(2,1)} %copy.170), calls=%async_computation.1 | async-start | bytes 393216 | tf_op jit(solution)/shard_map/all_to_all | solution.py:685
  72.5 19.0 %shard_map.346 = (f32[512,768]{1,0:T(8,128)}, bf16[512,768]{1,0:T(8,128)(2,1)S(1)}, bf16[512,768]{1,0:T(8,128)(2,1)S(1)}, f32[8,512]{1,0:T(8,128)S(1)}, f32[8,512]{1,0:T(8,128)S(1)}) custom-call(s32[3]{0:T(128)S(1)} %pad_add_fusion.refs_0_, bf16[512,768]{1,0:T(8,128)(2,1)} %copy-done.21, f32[512,768]{1,0:T(8,128)} %get-tuple-element.123.refs_2_, ...), custom_call_target="tpu_custom_call" | custom-call | flops 4000000000 | bytes 16777216 | tf_op jit(solution)/shard_map/pallas_call | solution.py:122
  95.8 18.9 %shard_map.347 = (f32[512,768]{1,0:T(8,128)}, bf16[512,768]{1,0:T(8,128)(2,1)}, bf16[512,768]{1,0:T(8,128)(2,1)}, f32[8,512]{1,0:T(8,128)S(1)}, f32[8,512]{1,0:T(8,128)S(1)}) custom-call(s32[3]{0:T(128)S(1)} %pad_add_fusion.refs_0_, bf16[512,768]{1,0:T(8,128)(2,1)} %copy-done.21, f32[512,768]{1,0:T(8,128)} %get-tuple-element.127.refs_2_, ...), custom_call_target="tpu_custom_call" | custom-call | flops 4000000000 | bytes 16777216 | tf_op jit(solution)/shard_map/pallas_call | solution.py:122
  118.8 20.7 %shard_map.348 = (bf16[4,512,768]{2,1,0:T(8,128)(2,1)}, bf16[768,768]{1,0:T(8,128)(2,1)}, bf16[768,768]{1,0:T(8,128)(2,1)}, bf16[768,768]{1,0:T(8,128)(2,1)}, bf...) custom-call(s32[3]{0:T(128)S(1)} %pad_add_fusion.refs_0_, ...), custom_call_target="tpu_custom_call" | custom-call | flops 8000000000 | bytes 16777216 | tf_op jit(solution)/shard_map/pallas_call | solution.py:333
  141.6 19.2 %shard_map.349 = (bf16[768,768]{1,0:T(8,128)(2,1)}, bf16[768,768]{1,0:T(8,128)(2,1)}, bf16[768,768]{1,0:T(8,128)(2,1)}, bf16[768,768]{1,0:T(8,128)(2,1)}, f32[51...) custom-call(s32[3]{0:T(128)S(1)} %pad_add_fusion.refs_0_, ...), custom_call_target="tpu_custom_call" | custom-call | flops 8000000000 | bytes 16777216 | tf_op jit(solution)/shard_map/pallas_call | solution.py:395
  165.6 20.5 %shard_map.350 = (f32[512,768]{1,0:T(8,128)}, bf16[768,768]{1,0:T(8,128)(2,1)}, bf16[768,768]{1,0:T(8,128)(2,1)}) custom-call(s32[3]{0:T(128)S(1)} %pad_add_fusion.refs_0_, bf16[512,768]{1,0:T(8,128)(2,1)S(1)} %copy-done.24, bf16[768,512]{1,0:T(8,128)(2,1)} %get-tuple-element.146.refs_2_, bf16[768,512]{1,0:T(8,128)(2,1)} %get-tuple-element.147.refs_3_, ...), custom_call_target="tpu_custom_call" | custom-call | flops 8000000000 | bytes 16777216 | tf_op jit(solution)/shard_map/pallas_call | solution.py:196
  189.8 20.7 %shard_map.351 = (f32[512,768]{1,0:T(8,128)}, bf16[768,768]{1,0:T(8,128)(2,1)}, bf16[768,768]{1,0:T(8,128)(2,1)}) custom-call(s32[3]{0:T(128)S(1)} %pad_add_fusion.refs_0_, bf16[512,768]{1,0:T(8,128)(2,1)S(1)} %copy-done.24, bf16[768,512]{1,0:T(8,128)(2,1)} %get-tuple-element.146.refs_2_, bf16[768,512]{1,0:T(8,128)(2,1)} %get-tuple-element.147.refs_3_, ...), custom_call_target="tpu_custom_call" | custom-call | flops 8000000000 | bytes 16777216 | tf_op jit(solution)/shard_map/pallas_call | solution.py:196
  214.0 4.0 %shard_map.352 = (bf16[384,768]{1,0:T(8,128)(2,1)}, bf16[4,128,192]{2,1,0:T(8,128)(2,1)S(1)}, bf16[4,400,192]{2,1,0:T(8,128)(2,1)S(1)}) custom-call(f32[512,768]{1,0:T(8,128)} %get-tuple-element.168.refs_0_, f32[512,768]{1,0:T(8,128)} %get-tuple-element.169.refs_1_, f32[1,768]{1,0:T(1,128)S(1)} %reshape.370.refs_4_.refs_2_, ...), custom_call_target="tpu_custom_call" | custom-call | flops 500000000 | bytes 16777216 | tf_op jit(solution)/shard_map/pallas_call | solution.py:532
  218.8 3.4 all-to-all-start.2
  222.1 3.8 %convert_add_fusion.1 = f32[768,768]{1,0:T(8,128)} fusion(bf16[768,768]{1,0:T(8,128)(2,1)} %collective-permute-done.32, bf16[768,768]{1,0:T(8,128)(2,1)} %collective-permute-done.20, bf16[768,768]{1,0:T(8,128)(2,1)} %get-tuple-element.188), kind=kLoop, calls=%fused_computation.1 | loop fusion | flops 2949120 | bytes 5898240 | tf_op jit(solution)/shard_map/add | solution.py:573
  227.4 3.5 all-to-all-start.4
  243.9 3.6 all-to-all-start.3
  254.9 4.4 %all-to-all-done.3 = bf16[8,96,192]{2,1,0:T(8,128)(2,1)S(1)} async-done(((bf16[8,96,192]{2,1,0:T(8,128)(2,1)}), bf16[8,96,192]{2,1,0:T(8,128)(2,1)S(1)}, u32[]{:S(2)}, u32[]{:S(2)}) %all-to-all-start.3) | async-done | bytes 294944 | tf_op jit(solution)/shard_map/all_to_all | solution.py:776
  261.2 4.3 %all-to-all-start.5 = ((bf16[8,144,192]{2,1,0:T(8,128)(2,1)}), bf16[8,144,192]{2,1,0:T(8,128)(2,1)}, u32[]{:S(2)}, u32[]{:S(2)}) async-start(bf16[8,144,192]{2,1,0:T(8,128)(2,1)} %pad_maximum_fusion), calls=%async_computation.5 | async-start | bytes 1179648 | tf_op jit(solution)/shard_map/all_to_all | solution.py:811
  265.5 20.1 %all-gather.2 = bf16[1536,192]{1,0:T(8,128)(2,1)S(1)} all-gather(bf16[384,192]{1,0:T(8,128)(2,1)S(1)} %get-tuple-element.179), channel_id=4, replica_groups=mesh['dp'=8,'tensor'=4] {'tensor'}, dimensions={0}, use_global_device_ids=true | all-gather | bytes 737280 | tf_op jit(solution)/shard_map/all_gather | solution.py:784
  294.9 9.9 %collective-permute-done.38 = bf16[96,768]{1,0:T(8,128)(2,1)S(1)} collective-permute-done((bf16[96,768]{1,0:T(8,128)(2,1)S(1)}, bf16[96,768]{1,0:T(8,128)(2,1)S(1)}, u32[]{:S(2)}, u32[]{:S(2)}) %collective-permute-start.38) | collective-permute-done | bytes 147488 | tf_op jit(solution)/shard_map/ppermute | solution.py:538
  307.9 3.6 collective-permute-done.26
  319.3 3.8 %collective-permute-done.27 = bf16[96,512]{1,0:T(8,128)(2,1)} collective-permute-done((bf16[96,512]{1,0:T(8,128)(2,1)}, bf16[96,512]{1,0:T(8,128)(2,1)}, u32[]{:S(2)}, u32[]{:S(2)}) %collective-permute-start.27) | collective-permute-done | bytes 98336 | tf_op jit(solution)/shard_map/ppermute | solution.py:538
  332.5 6.7 %all-gather.3 = f32[576,192]{1,0:T(8,128)S(1)} all-gather(f32[144,192]{1,0:T(8,128)S(1)} %convert_reduce_fusion.1), channel_id=5, replica_groups=mesh['dp'=8,'tensor'=4] {'tensor'}, dimensions={0}, use_global_device_ids=true | all-gather | bytes 552960 | tf_op jit(solution)/shard_map/all_gather | solution.py:813
  343.1 9.5 %collective-permute-done.31 = bf16[96,768]{0,1:T(8,128)(2,1)S(1)} collective-permute-done((bf16[96,768]{0,1:T(8,128)(2,1)S(1)}, bf16[96,768]{0,1:T(8,128)(2,1)S(1)}, u32[]{:S(2)}, u32[]{:S(2)}) %collective-permute-start.31) | collective-permute-done | bytes 147488 | tf_op jit(solution)/shard_map/ppermute | solution.py:538
  354.1 4.4 %convert.25 = f32[4,384,768]{2,1,0:T(8,128)} convert(bf16[4,384,768]{2,1,0:T(8,128)(2,1)} %bitcast.127) | non-fusion elementwise | flops 1179648 | bytes 7077888 | tf_op jit(solution)/shard_map/convert_element_type | solution.py:793
  (281 shorter events, 128.9 us)
Async XLA Ops:
  23.2 25.4 %collective-permute-start.3 = (bf16[384,768]{1,0:T(8,128)(2,1)}, bf16[384,768]{1,0:T(8,128)(2,1)}, u32[]{:S(2)}, u32[]{:S(2)}) collective-permute-start(bf16[384,768]{1,0:T(8,128)(2,1)} %constant_dynamic-slice_fusion.11), channel_id=1, source_target_pairs={{0,2},{1,3},{2,0},{3,1},{4,6},{5,7},{6,4},{7,5},{8,10},{9,11},{10,... | collective-permute-start | bytes 1769480 | tf_op jit(solution)/shard_map/ppermute | solution.py:538
  37.7 34.3 %collective-permute-start.6 = (bf16[768,768]{1,0:T(8,128)(2,1)}, bf16[768,768]{1,0:T(8,128)(2,1)}, u32[]{:S(2)}, u32[]{:S(2)}) collective-permute-start(bf16[768,768]{1,0:T(8,128)(2,1)} %copy-done.2), channel_id=1, source_target_pairs={{0,1},{1,0},{2,3},{3,2},{4,5},{5,4},{6,7},{7,6},{8,9},{9,8},{10,11... | collective-permute-start | bytes 3538952 | tf_op jit(solution)/shard_map/ppermute | solution.py:538
  41.6 28.0 %collective-permute-start.4 = (bf16[384,768]{1,0:T(8,128)(2,1)}, bf16[384,768]{1,0:T(8,128)(2,1)}, u32[]{:S(2)}, u32[]{:S(2)}) collective-permute-start(bf16[384,768]{1,0:T(8,128)(2,1)} %constant_dynamic-slice_fusion.10), channel_id=1, source_target_pairs={{0,2},{1,3},{2,0},{3,1},{4,6},{5,7},{6,4},{7,5},{8,10},{9,11},{10,... | collective-permute-start | bytes 1769480 | tf_op jit(solution)/shard_map/ppermute | solution.py:538
  58.1 296.0 %all-gather.7.cloned.1.call-start = ((), (), s32[]{:S(2)}) async-start(), calls=%async_computation.6 | async-start | bytes 3932160 | tf_op jit(solution)/shard_map/all_gather | solution.py:725
  61.8 53.2 %collective-permute-start.12 = (bf16[768,768]{1,0:T(8,128)(2,1)}, bf16[768,768]{1,0:T(8,128)(2,1)}, u32[]{:S(2)}, u32[]{:S(2)}) collective-permute-start(bf16[768,768]{1,0:T(8,128)(2,1)} %refs_6_), channel_id=1, source_target_pairs={{0,1},{1,0},{2,3},{3,2},{4,5},{5,4},{6,7},{7,6},{8,9},{9,8},{10,11... | collective-permute-start | bytes 3538952 | tf_op jit(solution)/shard_map/ppermute | solution.py:538
  65.8 27.5 %collective-permute-start.8 = (bf16[384,768]{1,0:T(8,128)(2,1)S(1)}, bf16[384,768]{1,0:T(8,128)(2,1)S(1)}, u32[]{:S(2)}, u32[]{:S(2)}) collective-permute-start(bf16[384,768]{1,0:T(8,128)(2,1)S(1)} %constant_dynamic-slice_fusion.8), channel_id=1, source_target_pairs={{0,2},{1,3},{2,0},{3,1},{4,6},{5,7},{6,4},{7,5},{8,10},{9,11},{10,... | collective-permute-start | bytes 1769480 | tf_op jit(solution)/shard_map/ppermute | solution.py:538
  69.6 23.7 %collective-permute-start.7 = (bf16[384,768]{1,0:T(8,128)(2,1)}, bf16[384,768]{1,0:T(8,128)(2,1)S(1)}, u32[]{:S(2)}, u32[]{:S(2)}) collective-permute-start(bf16[384,768]{1,0:T(8,128)(2,1)} %collective-permute-done.4.refs_9_.refs_8_), channel_id=1, source_target_pairs={{0,4},{4,0},{8,12},{12,8},{16,20},{20,16},{24,28},{28,24},{1,5},{5... | collective-permute-start | bytes 1769480 | tf_op jit(solution)/shard_map/ppermute | solution.py:538
  72.0 22.4 %collective-permute-start.9 = (bf16[384,768]{1,0:T(8,128)(2,1)}, bf16[384,768]{1,0:T(8,128)(2,1)S(1)}, u32[]{:S(2)}, u32[]{:S(2)}) collective-permute-start(bf16[384,768]{1,0:T(8,128)(2,1)} %collective-permute-done.3.refs_4_.refs_7_), channel_id=1, source_target_pairs={{0,1},{1,0},{2,3},{3,2},{4,5},{5,4},{6,7},{7,6},{8,9},{9,8},{10,11... | collective-permute-start | bytes 1769480 | tf_op jit(solution)/shard_map/ppermute | solution.py:538
  72.0 22.9 %collective-permute-start.10 = (bf16[384,768]{1,0:T(8,128)(2,1)}, bf16[384,768]{1,0:T(8,128)(2,1)S(1)}, u32[]{:S(2)}, u32[]{:S(2)}) collective-permute-start(bf16[384,768]{1,0:T(8,128)(2,1)} %collective-permute-done.5.refs_5_.refs_8_), channel_id=1, source_target_pairs={{0,1},{1,0},{2,3},{3,2},{4,5},{5,4},{6,7},{7,6},{8,9},{9,8},{10,11... | collective-permute-start | bytes 1769480 | tf_op jit(solution)/shard_map/ppermute | solution.py:538
  94.4 21.9 %collective-permute-start.15 = (bf16[768,768]{1,0:T(8,128)(2,1)S(1)}, bf16[768,768]{1,0:T(8,128)(2,1)S(1)}, u32[]{:S(2)}, u32[]{:S(2)}) collective-permute-start(bf16[768,768]{1,0:T(8,128)(2,1)S(1)} %copy-done.37), channel_id=1, source_target_pairs={{0,1},{1,0},{2,3},{3,2},{4,5},{5,4},{6,7},{7,6},{8,9},{9,8},{10,11... | collective-permute-start | bytes 3538952 | tf_op jit(solution)/shard_map/ppermute | solution.py:538
  94.4 21.9 %collective-permute-start.13 = (bf16[384,768]{1,0:T(8,128)(2,1)}, bf16[384,768]{1,0:T(8,128)(2,1)S(1)}, u32[]{:S(2)}, u32[]{:S(2)}) collective-permute-start(bf16[384,768]{1,0:T(8,128)(2,1)} %collective-permute-done.4.refs_9_.refs_8_), channel_id=1, source_target_pairs={{0,1},{1,0},{2,3},{3,2},{4,5},{5,4},{6,7},{7,6},{8,9},{9,8},{10,11... | collective-permute-start | bytes 1769480 | tf_op jit(solution)/shard_map/ppermute | solution.py:538
  94.9 21.9 %collective-permute-start.16 = (bf16[384,768]{1,0:T(8,128)(2,1)S(1)}, bf16[384,768]{1,0:T(8,128)(2,1)S(1)}, u32[]{:S(2)}, u32[]{:S(2)}) collective-permute-start(bf16[384,768]{1,0:T(8,128)(2,1)S(1)} %collective-permute-done.8.refs_15_.refs_14_), channel_id=1, source_target_pairs={{0,1},{1,0},{2,3},{3,2},{4,5},{5,4},{6,7},{7,6},{8,9},{9,8},{10,11... | collective-permute-start | bytes 1769480 | tf_op jit(solution)/shard_map/ppermute | solution.py:538
  160.8 25.3 %collective-permute-start.20 = (bf16[768,768]{1,0:T(8,128)(2,1)}, bf16[768,768]{1,0:T(8,128)(2,1)}, u32[]{:S(2)}, u32[]{:S(2)}) collective-permute-start(bf16[768,768]{1,0:T(8,128)(2,1)} %get-tuple-element.155), channel_id=1, source_target_pairs={{0,1},{1,0},{2,3},{3,2},{4,5},{5,4},{6,7},{7,6},{8,9},{9,8},{10,11... | collective-permute-start | bytes 3538952 | tf_op jit(solution)/shard_map/ppermute | solution.py:538
  160.9 25.2 %collective-permute-start.21 = (bf16[768,768]{1,0:T(8,128)(2,1)}, bf16[768,768]{1,0:T(8,128)(2,1)}, u32[]{:S(2)}, u32[]{:S(2)}) collective-permute-start(bf16[768,768]{1,0:T(8,128)(2,1)} %get-tuple-element.157), channel_id=1, source_target_pairs={{0,1},{1,0},{2,3},{3,2},{4,5},{5,4},{6,7},{7,6},{8,9},{9,8},{10,11... | collective-permute-start | bytes 3538952 | tf_op jit(solution)/shard_map/ppermute | solution.py:538
  164.0 46.5 %collective-permute-start.22 = (bf16[768,768]{1,0:T(8,128)(2,1)S(1)}, bf16[768,768]{1,0:T(8,128)(2,1)S(1)}, u32[]{:S(2)}, u32[]{:S(2)}) collective-permute-start(bf16[768,768]{1,0:T(8,128)(2,1)S(1)} %add_convert_fusion.2), channel_id=1, source_target_pairs={{0,2},{1,3},{2,0},{3,1},{4,6},{5,7},{6,4},{7,5},{8,10},{9,11},{10,... | collective-permute-start | bytes 3538952 | tf_op jit(solution)/shard_map/ppermute | solution.py:538
  188.8 33.4 %collective-permute-start.32 = (bf16[768,768]{1,0:T(8,128)(2,1)}, bf16[768,768]{1,0:T(8,128)(2,1)}, u32[]{:S(2)}, u32[]{:S(2)}) collective-permute-start(bf16[768,768]{1,0:T(8,128)(2,1)} %add_convert_fusion), channel_id=1, source_target_pairs={{0,2},{1,3},{2,0},{3,1},{4,6},{5,7},{6,4},{7,5},{8,10},{9,11},{10,... | collective-permute-start | bytes 3538952 | tf_op jit(solution)/shard_map/ppermute | solution.py:538
  189.3 45.3 %collective-permute-start.23 = (bf16[768,768]{1,0:T(8,128)(2,1)}, bf16[768,768]{1,0:T(8,128)(2,1)}, u32[]{:S(2)}, u32[]{:S(2)}) collective-permute-start(bf16[768,768]{1,0:T(8,128)(2,1)} %get-tuple-element.175), channel_id=1, source_target_pairs={{0,1},{1,0},{2,3},{3,2},{4,5},{5,4},{6,7},{7,6},{8,9},{9,8},{10,11... | collective-permute-start | bytes 3538952 | tf_op jit(solution)/shard_map/ppermute | solution.py:538
  189.3 45.3 %collective-permute-start.24 = (bf16[768,768]{1,0:T(8,128)(2,1)}, bf16[768,768]{1,0:T(8,128)(2,1)}, u32[]{:S(2)}, u32[]{:S(2)}) collective-permute-start(bf16[768,768]{1,0:T(8,128)(2,1)} %get-tuple-element.177), channel_id=1, source_target_pairs={{0,1},{1,0},{2,3},{3,2},{4,5},{5,4},{6,7},{7,6},{8,9},{9,8},{10,11... | collective-permute-start | bytes 3538952 | tf_op jit(solution)/shard_map/ppermute | solution.py:538
  213.4 35.6 %collective-permute-start.36 = (bf16[2,2,96,768]{3,2,0,1:T(8,128)(2,1)}, bf16[2,2,96,768]{3,2,0,1:T(8,128)(2,1)}, u32[]{:S(2)}, u32[]{:S(2)}) collective-permute-start(bf16[2,2,96,768]{3,2,0,1:T(8,128)(2,1)} %fusion.7), channel_id=1, source_target_pairs={{0,4},{4,0},{8,12},{12,8},{16,20},{20,16},{24,28},{28,24},{1,5},{5... | collective-permute-start | bytes 1769480 | tf_op jit(solution)/shard_map/ppermute | solution.py:538
  230.9 123.2 %all-gather.9.cloned.1.call-start = ((), (), s32[]{:S(2)}) async-start(), calls=%async_computation.7 | async-start | bytes 2949120 | tf_op jit(solution)/shard_map/all_gather | solution.py:793
  237.5 74.0 %collective-permute-start.28 = (bf16[768,768]{1,0:T(8,128)(2,1)}, bf16[768,768]{1,0:T(8,128)(2,1)}, u32[]{:S(2)}, u32[]{:S(2)}) collective-permute-start(bf16[768,768]{1,0:T(8,128)(2,1)} %add_convert_fusion.1), channel_id=1, source_target_pairs={{0,2},{1,3},{2,0},{3,1},{4,6},{5,7},{6,4},{7,5},{8,10},{9,11},{10,... | collective-permute-start | bytes 3538952 | tf_op jit(solution)/shard_map/ppermute | solution.py:538
  250.5 39.3 %collective-permute-start.37 = (bf16[2,96,768]{2,1,0:T(8,128)(2,1)S(1)}, bf16[2,96,768]{2,1,0:T(8,128)(2,1)}, u32[]{:S(2)}, u32[]{:S(2)}) collective-permute-start(bf16[2,96,768]{2,1,0:T(8,128)(2,1)S(1)} %fusion.19), channel_id=1, source_target_pairs={{0,8},{4,12},{8,0},{12,4},{16,24},{20,28},{24,16},{28,20},{1,9},{5... | collective-permute-start | bytes 884744 | tf_op jit(solution)/shard_map/ppermute | solution.py:538
  254.5 37.4 %collective-permute-start.34 = (bf16[2,96,768]{2,1,0:T(8,128)(2,1)}, bf16[2,96,768]{2,1,0:T(8,128)(2,1)}, u32[]{:S(2)}, u32[]{:S(2)}) collective-permute-start(bf16[2,96,768]{2,1,0:T(8,128)(2,1)} %fusion.18), channel_id=1, source_target_pairs={{0,8},{4,12},{8,0},{12,4},{16,24},{20,28},{24,16},{28,20},{1,9},{5... | collective-permute-start | bytes 884744 | tf_op jit(solution)/shard_map/ppermute | solution.py:538
  261.2 63.5 %all-to-all-start.5 = ((bf16[8,144,192]{2,1,0:T(8,128)(2,1)}), bf16[8,144,192]{2,1,0:T(8,128)(2,1)}, u32[]{:S(2)}, u32[]{:S(2)}) async-start(bf16[8,144,192]{2,1,0:T(8,128)(2,1)} %pad_maximum_fusion), calls=%async_computation.5 | async-start | bytes 1179648 | tf_op jit(solution)/shard_map/all_to_all | solution.py:811
  (76 other events, 786.5 us)
Sparse Core Ops, SparseCore 0:
  140.5 27.4 all-gather.6
  234.7 35.5 all-gather.8

commit v3 on v2

--- a/solution.py
+++ b/solution.py
@@ -79,7 +79,7 @@
     started, _ = fetch_shards(shards, weights, side_ref[0], sems)
     length, width = x_ref.shape
     group = heads * HD
-    block = 128
+    block = length
     lane = lax.broadcasted_iota(jnp.int32, (block, 128), 1)
     for i in range(count):
         for copy in started[i]:
@@ -107,7 +107,8 @@
             lse_ref[:, at] = columns.T[:8, :]
             return carry
 
-        lax.fori_loop(0, length // block, rows, 0)
+        for b in range(length // block):
+            rows(b, 0)
         if i == 0:
             zout_ref[...] = z_ref[...] + dot_nt(held[:, :group], w_ref[:, :group])
         else:
@@ -135,11 +136,11 @@
     shards, rest = regroup(rest, sizes)
     helds, lses = rest[:count], rest[count : 2 * count]
     accout_ref, terms = rest[2 * count], rest[2 * count + 1 : 3 * count + 1]
-    gc_ref, grads, dq_ref, delta_ref, weights, sems = rest[3 * count + 1 :]
+    gc_ref, grads, dq_ref, delta_ref, weights, full_ref, sems = rest[3 * count + 1 :]
     started, _ = fetch_shards(shards, weights, side_ref[0], sems)
     length, width = g_ref.shape
     group = heads * HD
-    block = 128
+    block = length
     lane = lax.broadcasted_iota(jnp.int32, (length, 128), 1)
     for i in range(count):
         for copy in started[i]:
@@ -177,22 +178,24 @@
                 dq_ref[h * HD : (h + 1) * HD, :] += dot_tn(k, grad_scores)
             return carry
 
-        lax.fori_loop(0, length // block, rows, 0)
+        for b in range(length // block):
+            rows(b, 0)
         grads[:, group : 2 * group] = (dq_ref[...] * HD ** (-0.5)).T.astype(BF)
         if i == 0:
             accout_ref[...] = acc_ref[...] + dot_nt(grads[...], w_ref[...])
         else:
             accout_ref[...] += dot_nt(grads[...], w_ref[...])
-        terms[i][...] = dot(xt_ref[...], grads[...]).astype(BF)
-        terms[i][:, :group] = dot(gt_ref[...], held[:, :group]).astype(BF)
-
-
-def attend_back_call(heads, side, g, gt, xt, acc, allow, shards, helds, lses):
+        full_ref[...] = dot(xt_ref[...], grads[...]).astype(BF)
+        full_ref[:, :group] = dot(gt_ref[...], held[:, :group]).astype(BF)
+        store_blocks(terms[i], full_ref, side_ref[3])
+
+
+def attend_back_call(heads, peers, side, g, gt, xt, acc, allow, shards, helds, lses):
     length, width = g.shape
     n = len(shards)
     sizes = [len(pieces) for pieces in shards]
     group = heads * HD
-    outs = [((length, width), F32)] + [((width, width), BF)] * n
+    outs = [((length, width), F32)] + [(blocks_shape(peers, width, width), BF)] * n
     got = call(
         lambda *refs: attend_back_kernel(heads, sizes, *refs),
         outs,
@@ -204,6 +207,7 @@
             pltpu.VMEM((group, length), F32),
             pltpu.VMEM((8, length), F32),
             pltpu.VMEM((n, width, width), BF),
+            pltpu.VMEM((width, width), BF),
             pltpu.SemaphoreType.DMA((sum(sizes),)),
         ],
         n * 4_000_000_000,
@@ -272,11 +276,21 @@
 ):
     up_shards, rest = regroup(rest, sizes)
     down_shards, rest = regroup(rest, sizes)
-    slope_ref, terms = rest[0], rest[1 : parts + 1]
+    slope_any, terms = rest[0], rest[1 : parts + 1]
     out_ref, x1t_ref, gx2_ref, g_ref, vec_ref = rest[parts + 1 : parts + 6]
-    ups, downs, actives, ffn_ref, x1_ref, gt_ref, sems = rest[parts + 6 :]
-    up_started, base = fetch_shards(up_shards, ups, side_ref[1], sems)
-    down_started, _ = fetch_shards(down_shards, downs, side_ref[2], sems, base)
+    ups, downs, actives, ffn_ref, x1_ref, gt_ref, slope_ref, held, sems = rest[parts + 6 :]
+    up_started, down_started, base = [], [], 0
+    for k in range(parts):
+        copies, base = fetch_shards([up_shards[k]], ups.at[k : k + 1], side_ref[1], sems, base)
+        up_started += copies
+        copies, base = fetch_shards([down_shards[k]], downs.at[k : k + 1], side_ref[2], sems, base)
+        down_started += copies
+    leaving = []
+
+    def leave(source, target):
+        leaving.append(pltpu.make_async_copy(source, target, sems.at[base + len(leaving)]))
+        leaving[-1].start()
+
     length, width = z_ref.shape
     block = 256
     vec_ref[...] = jnp.zeros_like(vec_ref)
@@ -299,6 +313,8 @@
                 for copy in down_started[k]:
                     copy.wait()
             ffn_ref[at, :] += dot(actives[k, at, :], downs[k])
+            if at.stop == length:
+                leave(slope_ref.at[k], slope_any.at[k])
         final, normed, inverse = layer_norm(ffn_ref[at, :], gf_ref[...], bf_ref[...])
         out_ref[at, :] = final.astype(BF)
         grad_in, gain_sum, bias_sum = norm_back(
@@ -309,19 +325,23 @@
         gx2_ref[at, :] = grad_in
         g_ref[at, :] = grad_in.astype(BF)
     gt_ref[...] = g_ref[...].T
-    for k in range(parts):
-        terms[k][...] = dot(gt_ref[...], actives[k]).astype(BF)
+    for k in sorted(range(parts), key=lambda k: (1 - k % 2, k)):
+        store_blocks(held.at[k], dot(gt_ref[...], actives[k]).astype(BF), side_ref[3])
+        leave(held.at[k], terms[k])
     x1t_ref[...] = x1_ref[...].T
-
-
-def forward_call(side, z, cot, gm, bm, gf, bf, up, down):
+    for copy in leaving:
+        copy.wait()
+
+
+def forward_call(peers, side, z, cot, gm, bm, gf, bf, up, down):
     length, width = z.shape
     n = len(up)
     sizes = [len(pieces) for pieces in up]
     inner = up[0][0].shape[1]
+    shape = blocks_shape(peers, width, inner)
     outs = (
         [((n, length, inner), BF)]
-        + [((width, inner), BF)] * n
+        + [(shape, BF)] * n
         + [
             ((length, width), BF),
             ((width, length), BF),
@@ -334,7 +354,7 @@
         lambda *refs: forward_kernel(n, sizes, *refs),
         outs,
         smem_spec() + vmem_specs(6) + any_specs(2 * sum(sizes)),
-        vmem_specs(len(outs)),
+        any_specs(n + 1) + vmem_specs(5),
         [
             pltpu.VMEM((n, width, inner), BF),
             pltpu.VMEM((n, inner, width), BF),
@@ -342,7 +362,9 @@
             pltpu.VMEM((length, width), F32),
             pltpu.VMEM((length, width), BF),
             pltpu.VMEM((width, length), BF),
-            pltpu.SemaphoreType.DMA((2 * sum(sizes),)),
+            pltpu.VMEM((n, length, inner), BF),
+            pltpu.VMEM((n, *shape), BF),
+            pltpu.SemaphoreType.DMA((2 * sum(sizes) + 2 * n,)),
         ],
         8_000_000_000,
     )(side, z, cot, gm, bm, gf, bf, *sum(up, []), *sum(down, []))
@@ -356,21 +378,26 @@
     down_shards, rest = regroup(rest, sizes)
     slope_any, *rest = rest
     terms = rest[:parts]
-    gx1_ref, ga_ref, gat_ref, vec_ref, gb_ref, ups, downs, slopes, sems = rest[parts:]
-    down_started, base = fetch_shards(down_shards, downs, side_ref[2], sems)
-    up_started, base = fetch_shards(up_shards, ups, side_ref[1], sems, base)
-    slope_copies = []
-    for k in range(parts):
-        slope_copies.append(
-            pltpu.make_async_copy(slope_any.at[k], slopes.at[k], sems.at[base + k])
-        )
-        slope_copies[k].start()
+    gx1_ref, ga_ref, gat_ref, vec_ref, gb_ref, ups, downs, slopes, held, sems = rest[parts:]
+    order = sorted(range(parts), key=lambda k: (1 - k % 2, k))
+    started, base = {}, 0
+    for k in order:
+        first, base = fetch_shards([down_shards[k]], downs.at[k : k + 1], side_ref[2], sems, base)
+        slope = pltpu.make_async_copy(slope_any.at[k], slopes.at[k], sems.at[base])
+        slope.start()
+        second, base = fetch_shards([up_shards[k]], ups.at[k : k + 1], side_ref[1], sems, base + 1)
+        started[k] = first[0] + [slope], second[0]
+    leaving = []
     gx1_ref[...] = gx2_ref[...]
-    for k in sorted(range(parts), key=lambda k: (1 - k % 2, k)):
-        for copy in (*down_started[k], slope_copies[k], *up_started[k]):
+    for k in order:
+        for copy in started[k][0]:
             copy.wait()
         gb_ref[...] = (dot_nt(g_ref[...], downs[k]) * slopes[k].astype(F32)).astype(BF)
-        terms[k][...] = dot(x1t_ref[...], gb_ref[...]).astype(BF)
+        store_blocks(held.at[k], dot(x1t_ref[...], gb_ref[...]).astype(BF), side_ref[3])
+        leaving.append(pltpu.make_async_copy(held.at[k], terms[k], sems.at[base + len(leaving)]))
+        leaving[-1].start()
+        for copy in started[k][1]:
+            copy.wait()
         gx1_ref[...] += dot_nt(gb_ref[...], ups[k])
     grad_in, gain_sum, bias_sum = norm_back(gx1_ref[...], z_ref[...], gm_ref[...])
     vec_ref[...] = jnp.zeros_like(vec_ref)
@@ -379,14 +406,17 @@
     gx1_ref[...] = grad_in
     ga_ref[...] = grad_in.astype(BF)
     gat_ref[...] = ga_ref[...].T
-
-
-def backward_call(side, z, gx2, g, x1t, gm, up, down, slope):
+    for copy in leaving:
+        copy.wait()
+
+
+def backward_call(peers, side, z, gx2, g, x1t, gm, up, down, slope):
     length, width = z.shape
     n = len(up)
     sizes = [len(pieces) for pieces in up]
     inner = up[0][0].shape[1]
-    outs = [((width, inner), BF)] * n + [
+    shape = blocks_shape(peers, width, inner)
+    outs = [(shape, BF)] * n + [
         ((length, width), F32),
         ((length, width), BF),
         ((width, length), BF),
@@ -396,13 +426,14 @@
         lambda *refs: backward_kernel(n, sizes, *refs),
         outs,
         smem_spec() + vmem_specs(5) + any_specs(2 * sum(sizes) + 1),
-        vmem_specs(len(outs)),
+        any_specs(n) + vmem_specs(4),
         [
             pltpu.VMEM((length, inner), BF),
             pltpu.VMEM((n, width, inner), BF),
             pltpu.VMEM((n, inner, width), BF),
             pltpu.VMEM((n, length, inner), BF),
-            pltpu.SemaphoreType.DMA((2 * sum(sizes) + n,)),
+            pltpu.VMEM((n, *shape), BF),
+            pltpu.SemaphoreType.DMA((2 * sum(sizes) + 2 * n,)),
         ],
         8_000_000_000,
     )(side, z, gx2, g, x1t, gm, *sum(up, []), *sum(down, []), slope)
@@ -416,6 +447,23 @@
         out_ref[:, (c + 1) * group : (c + 2) * group] = qkv_ref[c]
 
 
+def store_blocks(ref, value, me):
+    if len(ref.shape) == 2:
+        ref[...] = value[...]
+        return
+    count, share, _ = ref.shape
+    bits = count.bit_length() - 1
+    for p in range(count):
+        apart = p ^ me
+        place = sum(((apart >> i) & 1) << (bits - 1 - i) for i in range(bits))
+        ref[place] = value[p * share : (p + 1) * share, :]
+
+
+def blocks_shape(peers, width, columns):
+    share = width // peers
+    return (peers, share, columns) if share % 16 == 0 else (width, columns)
+
+
 def choose(index, count, step, source, store):
     for c in range(count):
 
@@ -441,12 +489,18 @@
     bins = table_ref.shape[1]
     places = lax.broadcasted_iota(jnp.int32, (stored, bins), 1)
     full[...] = jnp.zeros_like(full)
+    spare = low.shape[1] - chunk
+    lane = lax.broadcasted_iota(jnp.int32, (stored, spare), 1)
+    codes = jnp.zeros((stored, spare), F32)
     for c in range(table_ref.shape[0]):
-        full[...] += dot((box_ref[:, c : c + 1] == places).astype(BF), table_ref[c])
+        corner = box_ref[:, c : c + 1]
+        full[...] += dot((corner == places).astype(BF), table_ref[c])
+        codes = jnp.where(lane == c, corner.astype(F32) + 1.0, codes)
+    low[:, chunk:] = codes.astype(BF)
 
     def store(value):
         total = own_ref[...] + near_ref[...].astype(F32) + far_ref[...].astype(F32)
-        low[...] = (total + value).astype(BF)
+        low[:, :chunk] = (total + value).astype(BF)
 
     choose(mine_ref[0], parts, chunk, full, store)
     slots = out_ref.shape[0]
@@ -454,10 +508,25 @@
     out_ref[...] = dot((pick_ref[...] == regions).astype(BF), low[...]).astype(BF)
 
 
+def place_kernel(pick_ref, rows_ref, out_ref):
+    places = lax.broadcasted_iota(jnp.int32, (out_ref.shape[0], rows_ref.shape[0]), 0)
+    chosen = (pick_ref[...] == places).astype(BF)
+    out_ref[...] = dot(chosen, rows_ref[:, : out_ref.shape[1]]).astype(BF)
+
+
+def place_feats_kernel(chunk, pick_ref, rows_ref, feats_ref, out_ref, codes_ref):
+    places = lax.broadcasted_iota(jnp.int32, (out_ref.shape[0], feats_ref.shape[0]), 0)
+    chosen = (pick_ref[...] == places).astype(BF)
+    out_ref[...] = dot(chosen, feats_ref[...]).astype(BF)
+    last = rows_ref.shape[1] - 128
+    first = chunk - last
+    codes_ref[...] = dot(chosen, rows_ref[:, last:]).T[first : first + 8, :]
+
+
 def move_rows_kernel(pick_ref, rows_ref, out_ref):
     shape = (out_ref.shape[0], rows_ref.shape[0])
     places = lax.broadcasted_iota(jnp.int32, shape, 0)
-    out_ref[...] = dot((pick_ref[...] == places).astype(BF), rows_ref[...]).astype(BF)
+    out_ref[...] = dot((pick_ref[...] == places).astype(BF), rows_ref[...])
 
 
 def take_rows_kernel(pick_ref, rows_ref, out_ref):
@@ -482,12 +551,12 @@
     xt_ref[...] = x_ref[...].T
 
 
-def embed_back_kernel(parts, grad_ref, emb_ref, gain_ref, mid_ref, fin_ref, text_ref, reg_ref, rest_ref, vec):
+def embed_back_kernel(grad_ref, emb_ref, gain_ref, mid_ref, fin_ref, text_ref, reg_ref, vec):
     text_len = text_ref.shape[0]
-    chunk = reg_ref.shape[2]
+    slots = emb_ref.shape[0] - text_len
     grad_in, gain_sum, bias_sum = norm_back(grad_ref[...], emb_ref[...], gain_ref[...])
-    low = grad_in.astype(BF)
-    text_ref[...] = low[:text_len, :]
+    text_ref[...] = grad_in[:text_len, :].astype(BF)
+    reg_ref[:slots, :] = grad_in[text_len:, :].astype(BF)
     vec[...] = jnp.zeros_like(vec)
     vec[0:1, :] = jnp.sum(grad_in[:text_len, :], axis=0, keepdims=True)
     vec[1:2, :] = jnp.sum(grad_in[text_len:, :], axis=0, keepdims=True)
@@ -495,28 +564,58 @@
     vec[3:4, :] = bias_sum
     vec[4:6, :] = mid_ref[0:2, :]
     vec[6:8, :] = fin_ref[0:2, :]
-    vectors = vec[...].astype(BF)
-    for c in range(parts):
-        at = slice(c * chunk, (c + 1) * chunk)
-        reg_ref[c] = low[text_len:, at]
-        rest_ref[c, :text_len, :] = low[:text_len, at]
-        rest_ref[c, text_len:, :] = vectors[:, at]
-
-
-def box_kernel(pick_ref, rows_ref, box_ref, chunk_ref, term_ref):
-    move_rows_kernel(pick_ref, rows_ref, chunk_ref)
-    bins = term_ref.shape[1]
-    places = lax.broadcasted_iota(jnp.int32, (bins, chunk_ref.shape[0]), 0)
-    for c in range(term_ref.shape[0]):
-        term_ref[c] = dot((box_ref[c : c + 1, :] == places).astype(BF), chunk_ref[...])
-
-
-def project_back_kernel(parts, chunks_ref, feats_ref, w_ref, grad_ref, term_ref, full):
-    chunk = chunks_ref.shape[2]
-    for c in range(parts):
-        full[:, c * chunk : (c + 1) * chunk] = chunks_ref[c]
-    grad_ref[...] = dot_nt(full[...], w_ref[...])
-    term_ref[...] = dot(full[...].T, feats_ref[...]).astype(BF)
+    reg_ref[slots:, :] = vec[...].astype(BF)
+
+
+def return_kernel(parts, mine_ref, pick_ref, feats_ref, codes_ref, w_ref, *rest):
+    pieces = rest[:parts]
+    wire_ref, proj_ref, box_ref, rest_ref, rows, columns, sums, full_ref = rest[parts:]
+    slots = rows.shape[0] // parts
+    chunk = columns.shape[1]
+    for k in range(parts):
+        rows[k * slots : (k + 1) * slots, :] = pieces[k][:slots, :]
+    low = dot_nt(rows[...], w_ref[...]).astype(BF)
+    places = lax.broadcasted_iota(jnp.int32, (wire_ref.shape[0], rows.shape[0]), 1)
+    wire_ref[...] = dot((pick_ref[...] == places).astype(BF), low).astype(BF)
+    full_ref[...] = dot(rows[...].T, feats_ref[...]).astype(BF)
+    store_blocks(proj_ref, full_ref, mine_ref[1])
+    sums[...] = pieces[0][...].astype(F32)
+    for k in range(1, parts):
+        sums[...] += pieces[k][...].astype(F32)
+
+    def store_rows(value):
+        columns[...] = value
+
+    def store_rest(value):
+        rest_ref[...] = value
+
+    choose(mine_ref[0], parts, chunk, rows, store_rows)
+    choose(mine_ref[0], parts, chunk, sums, store_rest)
+    bins = box_ref.shape[1]
+    codes = lax.broadcasted_iota(jnp.int32, (bins, rows.shape[0]), 0).astype(F32) + 1.0
+    for c in range(box_ref.shape[0]):
+        box_ref[c] = dot((codes_ref[c : c + 1, :] == codes).astype(BF), columns[...])
+
+
+def text_kernel(parts, mine_ref, *rest):
+    pieces, (out_ref, pos_ref, sums) = rest[:parts], rest[parts:]
+    sums[...] = pieces[0][...].astype(F32)
+    out_ref[mine_ref[0]] = sums[...]
+    for k in range(1, parts):
+        value = pieces[k][...].astype(F32)
+        out_ref[mine_ref[0] ^ k] = value
+        sums[...] += value
+
+    def store(value):
+        pos_ref[...] = value
+
+    choose(mine_ref[0], parts, pos_ref.shape[1], sums, store)
+
+
+def line_up_kernel(parts, mine_ref, *rest):
+    pieces, out_ref = rest[:parts], rest[parts]
+    for k in range(parts):
+        out_ref[mine_ref[0] ^ k] = pieces[k][...]
 
 
 def spread_kernel(parts, chunks_ref, out_ref):
@@ -562,33 +661,26 @@
     ]
 
 
-def fold(held, bit):
-    moved = {
-        k: swap(total(v).astype(BF), "tensor", bit) for k, v in held.items() if k & bit
-    }
-    return {k: v + [moved[k | bit]] for k, v in held.items() if not k & bit}
+def pair_sum(terms):
+    here = [terms[0], swap(terms[1], "tensor", 1)]
+    return here, total([terms[2], swap(terms[3], "tensor", 1)]).astype(BF)
 
 
 def total(summands):
     return sum(value.astype(F32) for value in summands)
 
 
-def terms_of(terms):
-    return {k: [term] for k, term in enumerate(terms)}
-
-
-def sum_over_dp(term):
+def sum_over_dp(values):
     bits = bits_of("dp")
-    me = lax.axis_index("dp")
-    rows, columns = term.shape
-    held = term.reshape([2] * len(bits) + [rows >> len(bits), columns])
-    for step, bit in enumerate(bits):
-        axis = len(bits) - 1 - step
-        side = (me // bit) % 2
-        sent = lax.dynamic_index_in_dim(held, 1 - side, axis, keepdims=False)
-        kept = lax.dynamic_index_in_dim(held, side, axis, keepdims=False)
-        held = kept.astype(F32) + swap(sent.astype(BF), "dp", bit).astype(F32)
-    return held
+    if values[0].ndim == 2:
+        term = total(values).astype(BF)
+        term = term.reshape(1 << len(bits), -1, term.shape[1])
+        return jnp.sum(lax.all_to_all(term, "dp", 0, 0, tiled=True).astype(F32), axis=0)
+    for bit in bits:
+        half = values[0].shape[0] // 2
+        sent = total([v[half:] for v in values]).astype(BF)
+        values = [v[:half] for v in values] + [swap(sent, "dp", bit)]
+    return total(values)[0]
 
 
 def local(
@@ -618,9 +710,9 @@
     parts = lax.axis_size("tensor")
     peers = lax.axis_size("dp")
     mine = lax.axis_index("tensor")
-    mine_now = mine.reshape(1).astype(jnp.int32)
     dp_now = lax.axis_index("dp")
-    sides = jnp.stack([dp_now % 2, dp_now % 2, (dp_now // 2) % 2]).astype(jnp.int32)
+    mine_now = jnp.stack([mine, dp_now]).astype(jnp.int32)
+    sides = jnp.stack([dp_now % 2, dp_now % 2, (dp_now // 2) % 2, dp_now]).astype(jnp.int32)
     row_count, text_len, width = text_embed.shape
     assert row_count == parts == 4
     length = seg_ids.shape[1]
@@ -632,6 +724,7 @@
     heads = group // HD
     chunk = width // parts
     share = width // peers
+    broad = -(-(chunk + 8) // 128) * 128
     wire = peers * capacity
 
     def own(array):
@@ -663,24 +756,26 @@
         (recv_flat // length) * slots + recv_flat % length - text_len,
         -1,
     )
+    recv_near = jnp.where(recv_flat >= 0, (recv_slot // slots ^ mine) * slots + recv_slot % slots, -1)
+    near_line, near_column = recv_near.reshape(1, wire), recv_near.reshape(wire, 1)
     send_line, send_column = send_flat.reshape(1, wire), send_flat.reshape(wire, 1)
-    recv_line, recv_column = recv_slot.reshape(1, wire), recv_slot.reshape(wire, 1)
+    recv_line = recv_slot.reshape(1, wire)
     outgoing = small_call(
         lambda *refs: outgoing_kernel(parts, *refs),
         [mine_now, held[0], near, far, box_coords, box_table, send_column],
-        [((wire, chunk), BF)],
-        [pltpu.VMEM((stored, width), F32), pltpu.VMEM((stored, chunk), BF)],
+        [((wire, broad), BF)],
+        [pltpu.VMEM((stored, width), F32), pltpu.VMEM((stored, broad), BF)],
         scalar=True,
     )
     outgoing, w_up = tie(outgoing, w_up)
     up_half = far_half(w_up, 1)
     incoming = lax.all_to_all(
-        outgoing.reshape(peers, capacity, chunk), "dp", 0, 0, tiled=True
-    ).reshape(wire, chunk)
+        outgoing.reshape(peers, capacity, broad), "dp", 0, 0, tiled=True
+    ).reshape(wire, broad)
     incoming, att_half = tie(incoming, att_half)
     att_other = swap(att_half, "dp", 1)
     placed = small_call(
-        move_rows_kernel, [recv_line, incoming], [((row_count * slots, chunk), BF)]
+        place_kernel, [recv_line, incoming], [((row_count * slots, chunk), BF)]
     )
     placed = lax.all_to_all(placed.reshape(parts, slots, chunk), "tensor", 0, 0, tiled=True)
     placed, w_down = tie(placed, w_down)
@@ -696,6 +791,11 @@
             ((width, length), BF),
         ],
     )
+    (hidden0, inputs0), feats = tie((hidden0, inputs0), region_feats)
+    feats_wire = small_call(take_rows_kernel, [send_column, feats], [((wire, depth), BF)])
+    feats_wire = lax.all_to_all(
+        feats_wire.reshape(peers, capacity, depth), "dp", 0, 0, tiled=True
+    ).reshape(wire, depth)
     allowed = key_mask(own(seg_ids), own(region_counts))
     allow = allowed.astype(F32)
     allow_turned = allowed.T.astype(F32)
@@ -712,6 +812,7 @@
     z, down_other = tie(z, down_other)
     down = gather_shards(w_down, down_half, down_other)
     slopes, down_terms, (final, x1t, grad_x2, grad_ffn, final_vectors) = forward_call(
+        peers,
         sides,
         z,
         own(cotangent),
@@ -722,21 +823,29 @@
         up,
         down,
     )
-    layer_output = lax.all_gather(final, "tensor", axis=0, tiled=False)
-    sum_down = fold(terms_of(down_terms), 1)
+    down_here, down_across = pair_sum(down_terms)
+    final_far = swap(final, "tensor", 2)
 
     up_terms, (grad_x1, grad_attn, grad_attn_turned, mid_vectors) = backward_call(
-        sides, z, grad_x2, grad_ffn, x1t, line(gain_mid), up, down, slopes
-    )
-    (grad_attn, grad_x1), sum_down = tie((grad_attn, grad_x1), sum_down)
-    sum_down = fold(sum_down, 2)[0]
-    sum_up = fold(terms_of(up_terms), 1)
+        peers, sides, z, grad_x2, grad_ffn, x1t, line(gain_mid), up, down, slopes
+    )
+    (grad_attn, grad_x1), (down_across, final_far, feats_wire) = tie(
+        (grad_attn, grad_x1), (down_across, final_far, feats_wire)
+    )
+    down_far = swap(down_across, "tensor", 2)
+    up_here, up_across = pair_sum(up_terms)
+    slot_feats, slot_codes = small_call(
+        lambda *refs: place_feats_kernel(chunk, *refs),
+        [near_line, incoming, feats_wire],
+        [((row_count * slots, depth), BF), ((8, row_count * slots), F32)],
+    )
     total0 = grad_x1
     att_terms = [None] * parts
     for at in (1, 0):
         picked = range(at, parts, 2)
         total0, terms = attend_back_call(
             heads,
+            peers,
             sides,
             grad_attn,
             grad_attn_turned,
@@ -750,51 +859,60 @@
         for k, term in zip(picked, terms, strict=True):
             att_terms[k] = term
         if at:
-            total0, sum_up = tie(total0, sum_up)
-            sum_up = fold(sum_up, 2)[0]
-    total0, sum_down = tie(total0, sum_down)
-    sum_att = fold(terms_of(att_terms), 1)
-
-    text_own, regions_out, rest_out = small_call(
-        lambda *refs: embed_back_kernel(parts, *refs),
+            total0, (up_across, slot_feats) = tie(total0, (up_across, slot_feats))
+            up_far = swap(up_across, "tensor", 2)
+    total0, down_far = tie(total0, down_far)
+    att_here, att_across = pair_sum(att_terms)
+
+    def neighbours(piece, far):
+        return [piece, swap(piece, "tensor", 1), far, swap(far, "tensor", 1)]
+
+    text_own, regions_own = small_call(
+        embed_back_kernel,
         [total0, embedded, line(gain_embed), mid_vectors, final_vectors],
+        [((text_len, width), BF), ((slots + 16, width), BF)],
+        [pltpu.VMEM((16, width), F32)],
+    )
+    regions_far = swap(regions_own, "tensor", 2)
+    regions_far, (text_own, att_across) = tie(regions_far, (text_own, att_across))
+    att_far = swap(att_across, "tensor", 2)
+    text_far = swap(text_own, "tensor", 2)
+    feats_back, proj_term, box_term, rest_sum = small_call(
+        lambda *refs: return_kernel(parts, *refs),
+        [mine_now, near_column, slot_feats, slot_codes, w_proj]
+        + neighbours(regions_own, regions_far),
         [
-            ((text_len, width), BF),
-            ((parts, slots, chunk), BF),
-            ((parts, text_len + 16, chunk), BF),
+            ((wire, depth), BF),
+            (blocks_shape(peers, width, depth), BF),
+            ((box_table.shape[0], bins, chunk), F32),
+            ((slots + 16, chunk), F32),
         ],
-        [pltpu.VMEM((16, width), F32)],
-    )
-    regions_in = lax.all_to_all(regions_out, "tensor", 0, 0, tiled=True)
-    regions_in, sum_att = tie(regions_in, sum_att)
-    sum_att = fold(sum_att, 2)[0]
-    returning = small_call(
-        take_rows_kernel,
-        [recv_column, regions_in.reshape(row_count * slots, chunk)],
-        [((wire, chunk), BF)],
-    )
-    returned = lax.all_to_all(
-        returning.reshape(peers, capacity, chunk), "dp", 0, 0, tiled=True
-    ).reshape(wire, chunk)
-    region_chunk, box_term = small_call(
-        box_kernel,
-        [send_line, returned, box_coords.T],
-        [((stored, chunk), BF), ((box_table.shape[0], bins, chunk), F32)],
-    )
-    region_chunks = lax.all_gather(region_chunk, "tensor", axis=0, tiled=False)
-    feat_grad, proj_term = small_call(
-        lambda *refs: project_back_kernel(parts, *refs),
-        [region_chunks, region_feats, w_proj],
-        [((stored, depth), F32), ((width, depth), BF)],
-        [pltpu.VMEM((stored, width), BF)],
-    )
-
-    rest_in = lax.all_to_all(rest_out, "tensor", 0, 0, tiled=True)
-    text_grad = lax.all_gather(text_own, "tensor", axis=0, tiled=False).astype(F32)
-    summed = jnp.sum(rest_in.astype(F32), axis=0)
-    pos_term = jnp.concatenate(
-        [summed[:text_len], jnp.sum(regions_in.astype(F32), axis=0)], axis=0
-    )
+        [
+            pltpu.VMEM((row_count * slots, width), BF),
+            pltpu.VMEM((row_count * slots, chunk), BF),
+            pltpu.VMEM((slots + 16, width), F32),
+            pltpu.VMEM((width, depth), BF),
+        ],
+        scalar=True,
+    )
+    feats_back = lax.all_to_all(
+        feats_back.reshape(peers, capacity, depth), "dp", 0, 0, tiled=True
+    ).reshape(wire, depth)
+    feat_grad = small_call(move_rows_kernel, [send_line, feats_back], [((stored, depth), F32)])
+    text_grad, text_sum = small_call(
+        lambda *refs: text_kernel(parts, *refs),
+        [mine_now] + neighbours(text_own, text_far),
+        [((parts, text_len, width), F32), ((text_len, chunk), F32)],
+        [pltpu.VMEM((text_len, width), F32)],
+        scalar=True,
+    )
+    layer_output = small_call(
+        lambda *refs: line_up_kernel(parts, *refs),
+        [mine_now] + neighbours(final, final_far),
+        [((parts, length, width), BF)],
+        scalar=True,
+    )
+    pos_term = jnp.concatenate([text_sum, rest_sum[:slots]], axis=0)
     bin_share = bins // peers
     pos_share = length // peers
     bundle = jnp.concatenate(
@@ -803,7 +921,7 @@
             box_term.reshape(-1, peers, bin_share, chunk)
             .transpose(1, 0, 2, 3)
             .reshape(peers, -1, chunk),
-            jnp.broadcast_to(summed[text_len:], (peers, 16, chunk)),
+            jnp.broadcast_to(rest_sum[slots:], (peers, 16, chunk)),
         ],
         axis=1,
     ).astype(BF)
@@ -818,12 +936,12 @@
     grad_box = bundle[pos_share:-16].reshape(-1, bin_share, width)
     vectors = lax.dynamic_slice_in_dim(bundle[-16:], lax.axis_index("dp") * share, share, 1)
 
-    grad_down = sum_over_dp(total(sum_down)).T
-    grad_up = sum_over_dp(total(sum_up))
-    grad_att = sum_over_dp(total(sum_att))
+    grad_down = sum_over_dp(down_here + [down_far]).T
+    grad_up = sum_over_dp(up_here + [up_far])
+    grad_att = sum_over_dp(att_here + [att_far])
     grad_mix = grad_att[:, :group].T
     grad_qkv = grad_att[:, group:].reshape(share, 3, group).transpose(1, 0, 2)
-    grad_proj = sum_over_dp(proj_term).T
+    grad_proj = sum_over_dp([proj_term]).T
     return (
         layer_output,
         text_grad,

time: 375 us -> 350 us (0.933)
  blocking collectives: 26.7 us -> 6.69 us
  waiting for transfers between devices: 49.2 us -> 65.4 us
  Pallas kernels: 139 us -> 125 us
  between operations: 16.1 us -> 2.35 us
  starting transfers between devices: 53.9 us -> 66.2 us
  local copies, waits for them, and re-layouts: 47.7 us -> 40.9 us
    ppermute x39 -> x48, waiting for transfers between devices: 34.5 us -> 57.7 us  [swap(): return lax.ppermute(value, axis, [(i, i ^ bit) for i in range(count)])]
    all_gather x1 -> x0, blocking collectives: 20.1 us -> none  [local(): region_chunks = lax.all_gather(region_chunk, 'tensor', axis=0, tiled=False)]
    pallas_call x2, Pallas kernels: 37.9 us -> 21.5 us  [attend_call(): call(lambda *refs: attend_kernel(heads, sizes, *refs), outs, smem_spec()...]
    add x13 -> x0, other arithmetic: 14.4 us -> none  [the longest x3 7.59 us: total(): return sum((value.astype(F32) for value in summands))]
    all_to_all x4 -> x3, waiting for transfers between devices: 13.4 us -> 0.01 us  [the longest x1 0.01 us: local(): lax.all_to_all(feats_wire.reshape(peers, capacity, depth), 'dp', 0, 0, ti...]
    pallas_call x10 -> x13, Pallas kernels: 20.4 us -> 33.1 us  [small_call(): call(body, outs, specs, vmem_specs(len(outs)), list(scratch), flops)(*args)]
    convert_element_type x4 -> x14, other arithmetic: 12 us -> 23.9 us  [the longest x11 16.5 us: sum_over_dp(): sent = total([v[half:] for v in values]).astype(BF)]
    ppermute x39 -> x48, starting transfers between devices: 29.1 us -> 39.1 us  [swap(): return lax.ppermute(value, axis, [(i, i ^ bit) for i in range(count)])]
  transfers between devices with their start and end apart: 47 -> 53, of which waited for: 16 -> 15; matrix products, arithmetic and copies ran while one was open for 17% -> 16% of each run, Pallas kernels for 31% -> 28%
where the time goes in v3:
time: 350 us; the launch traced here: 343 us
  Pallas kernels  125 us (36%)
  starting transfers between devices  66.2 us (19%)
  waiting for transfers between devices  65.4 us (19%)
  local copies, waits for them, and re-layouts  40.9 us (12%)
  other arithmetic  36.6 us (10%)
  blocking collectives  6.69 us (2%)
    ppermute x48, waiting for transfers between devices, swap(): return lax.ppermute(value, axis, [(i, i ^ bit) for i in range(count)])  57.7 us
    ppermute x48, starting transfers between devices, swap(): return lax.ppermute(value, axis, [(i, i ^ bit) for i in range(count)])  39.1 us
    pallas_call x13, Pallas kernels, small_call(): call(body, outs, specs, vmem_specs(len(outs)), list(scratch), flops)(*args)  33.1 us
    pallas_call x2, Pallas kernels, attend_back_call(): call(lambda *refs: attend_back_kernel(heads, sizes, *refs), outs, smem_sp...  31.8 us
    pallas_call x1, Pallas kernels, forward_call(): call(lambda *refs: forward_kernel(n, sizes, *refs), outs, smem_spec() + v...  21.8 us
    pallas_call x2, Pallas kernels, attend_call(): call(lambda *refs: attend_kernel(heads, sizes, *refs), outs, smem_spec()...  21.5 us
    unnamed x151, local copies, waits for them, and re-layouts  19.7 us
    pallas_call x1, Pallas kernels, backward_call(): call(lambda *refs: backward_kernel(n, sizes, *refs), outs, smem_spec() +...  17 us
  transfers between devices with their start and end apart: 53, of which 15 were waited for; matrix products, arithmetic and copies ran while one was open for 16% of the time, Pallas kernels for 28%

profile of v3, /device:TPU:0, one launch (start us, length us, event | category | flops | bytes accessed | tf_op | source)
XLA Modules:
  0.0 343.4 jit_solution(4200731610603488194)
XLA Ops:
  22.1 5.9 %all-to-all-start = ((bf16[8,96,256]{2,1,0:T(8,128)(2,1)}), bf16[8,96,256]{2,1,0:T(8,128)(2,1)}, u32[]{:S(2)}, u32[]{:S(2)}) async-start(bf16[8,96,256]{2,1,0:T(8,128)(2,1)} %bitcast.53), calls=%async_computation | async-start | bytes 786432 | tf_op jit(solution)/shard_map/all_to_all | solution.py:772
  36.0 10.4 %collective-permute-done.3.refs_4_.refs_7_ = bf16[384,768]{1,0:T(8,128)(2,1)} collective-permute-done((bf16[384,768]{1,0:T(8,128)(2,1)}, bf16[384,768]{1,0:T(8,128)(2,1)}, u32[]{:S(2)}, u32[]{:S(2)}) %collective-permute-start.3) | collective-permute-done | bytes 589856 | tf_op jit(solution)/shard_map/ppermute | solution.py:637
  54.2 4.2 %all-to-all-start.1 = ((bf16[4,128,192]{1,2,0:T(8,128)(2,1)}), bf16[4,128,192]{1,2,0:T(8,128)(2,1)}, u32[]{:S(2)}, u32[]{:S(2)}) async-start(bf16[4,128,192]{1,2,0:T(8,128)(2,1)} %copy.59), calls=%async_computation.1 | async-start | bytes 393216 | tf_op jit(solution)/shard_map/all_to_all | solution.py:780
  74.5 10.8 %shard_map.346 = (f32[512,768]{1,0:T(8,128)}, bf16[512,768]{1,0:T(8,128)(2,1)S(1)}, bf16[512,768]{1,0:T(8,128)(2,1)S(1)}, f32[8,512]{1,0:T(8,128)S(1)}, f32[8,512]{1,0:T(8,128)S(1)}) custom-call(s32[4]{0:T(128)S(1)} %copy-done.14, bf16[512,768]{1,0:T(8,128)(2,1)} %copy-done.27, f32[512,768]{1,0:T(8,128)} %get-tuple-element.124.refs_2_, ...), custom_call_target="tpu_custom_call" | custom-call | flops 4000000000 | bytes 16777216 | tf_op jit(solution)/shard_map/pallas_call | solution.py:123
  91.8 10.7 %shard_map.347 = (f32[512,768]{1,0:T(8,128)}, bf16[512,768]{1,0:T(8,128)(2,1)}, bf16[512,768]{1,0:T(8,128)(2,1)}, f32[8,512]{1,0:T(8,128)S(1)}, f32[8,512]{1,0:T(8,128)S(1)}) custom-call(s32[4]{0:T(128)S(1)} %copy-done.14, bf16[512,768]{1,0:T(8,128)(2,1)} %copy-done.27, f32[512,768]{1,0:T(8,128)} %get-tuple-element.128.refs_2_, ...), custom_call_target="tpu_custom_call" | custom-call | flops 4000000000 | bytes 16777216 | tf_op jit(solution)/shard_map/pallas_call | solution.py:123
  108.1 21.8 %shard_map.348 = (bf16[4,512,768]{2,1,0:T(8,128)(2,1)}, bf16[8,96,768]{2,1,0:T(8,128)(2,1)}, bf16[8,96,768]{2,1,0:T(8,128)(2,1)}, bf16[8,96,768]{2,1,0:T(8,128)(...) custom-call(s32[4]{0:T(128)S(1)} %copy-done.14, ...), custom_call_target="tpu_custom_call" | custom-call | flops 8000000000 | bytes 16777216 | tf_op jit(solution)/shard_map/pallas_call | solution.py:353
  132.5 5.9 %all-to-all-start.2 = ((bf16[8,96,512]{2,1,0:T(8,128)(2,1)}), bf16[8,96,512]{2,1,0:T(8,128)(2,1)}, u32[]{:S(2)}, u32[]{:S(2)}) async-start(bf16[8,96,512]{2,1,0:T(8,128)(2,1)} %bitcast.11), calls=%async_computation.2 | async-start | bytes 1572864 | tf_op jit(solution)/shard_map/all_to_all | solution.py:796
  140.1 17.0 %shard_map.349 = (bf16[8,96,768]{2,1,0:T(8,128)(2,1)}, bf16[8,96,768]{2,1,0:T(8,128)(2,1)}, bf16[8,96,768]{2,1,0:T(8,128)(2,1)}, bf16[8,96,768]{2,1,0:T(8,128)(2...) custom-call(s32[4]{0:T(128)S(1)} %copy-done.15, ...), custom_call_target="tpu_custom_call" | custom-call | flops 8000000000 | bytes 16777216 | tf_op jit(solution)/shard_map/pallas_call | solution.py:425
  160.9 15.8 %shard_map.352 = (f32[512,768]{1,0:T(8,128)}, bf16[8,96,768]{2,1,0:T(8,128)(2,1)}, bf16[8,96,768]{2,1,0:T(8,128)(2,1)}) custom-call(s32[4]{0:T(128)S(1)} %copy-done.15, bf16[512,768]{1,0:T(8,128)(2,1)S(1)} %copy-done.30, bf16[768,512]{1,0:T(8,128)(2,1)} %get-tuple-element.147.refs_2_, bf16[768,512]{1,0:T(8,128)(2,1)} %get-tuple-element.148.refs_3_, ...), custom_call_target="tpu_custom_call" | custom-call | flops 8000000000 | bytes 16777216 | tf_op jit(solution)/shard_map/pallas_call | solution.py:199
  184.0 16.0 %shard_map.354 = (f32[512,768]{1,0:T(8,128)}, bf16[8,96,768]{2,1,0:T(8,128)(2,1)}, bf16[8,96,768]{2,1,0:T(8,128)(2,1)}) custom-call(s32[4]{0:T(128)S(1)} %copy-done.15, bf16[512,768]{1,0:T(8,128)(2,1)S(1)} %copy-done.31, bf16[768,512]{1,0:T(8,128)(2,1)} %get-tuple-element.147.refs_2_, bf16[768,512]{1,0:T(8,128)(2,1)} %get-tuple-element.148.refs_3_, ...), custom_call_target="tpu_custom_call" | custom-call | flops 8000000000 | bytes 16777216 | tf_op jit(solution)/shard_map/pallas_call | solution.py:199
  200.2 3.9 %shard_map.355 = (bf16[384,768]{1,0:T(8,128)(2,1)}, bf16[144,768]{1,0:T(8,128)(2,1)S(1)}) custom-call(f32[512,768]{1,0:T(8,128)} %get-tuple-element.166.grad_ref, f32[512,768]{1,0:T(8,128)} %get-tuple-element.167.emb_ref, f32[1,768]{1,0:T(1,128)S(1)} %reshape.516.refs_4_.gain_ref, f32[8,768]{1,0:T(8,128)S(1)} %get-tuple-element.168.mid_ref, ...), custom_call_target="tpu_custom_call" | custom-call | flops 500000000 | bytes 16777216 | tf_op jit(solution)/shard_map/pallas_call | solution.py:631
  210.2 4.1 %collective-permute-done.40 = bf16[8,96,768]{2,1,0:T(8,128)(2,1)S(1)} collective-permute-done((bf16[8,96,768]{2,1,0:T(8,128)(2,1)S(1)}, bf16[8,96,768]{2,1,0:T(8,128)(2,1)S(1)}, u32[]{:S(2)}, u32[]{:S(2)}) %collective-permute-start.40) | collective-permute-done | bytes 1179680 | tf_op jit(solution)/shard_map/ppermute | solution.py:637
  227.5 4.1 %shard_map.357 = (bf16[768,512]{1,0:T(8,128)(2,1)}, bf16[8,96,512]{2,1,0:T(8,128)(2,1)}, f32[4,128,192]{2,1,0:T(8,128)S(1)}, f32[144,192]{1,0:T(8,128)S(1)}) custom-call(s32[2]{0:T(128)S(1)} %pad_add_fusion.refs_0_, s32[768,1]{1,0:T(8,128)S(1)} %fusion.13.refs_1_, bf16[512,512]{1,0:T(8,128)(2,1)} %copy-done.8, f32[8,512]{1,0:T(8,128)S(1)} %get-tuple-element.177.refs_3_, ...), custom_call_target="tpu_custom_call" | custom-call | flops 500000000 | bytes 16777216 | tf_op jit(solution)/shard_map/pallas_call | solution.py:631
  232.8 4.8 %all-to-all-start.3 = ((bf16[8,96,512]{2,1,0:T(8,128)(2,1)}), bf16[8,96,512]{2,1,0:T(8,128)(2,1)S(1)}, u32[]{:S(2)}, u32[]{:S(2)}) async-start(bf16[8,96,512]{2,1,0:T(8,128)(2,1)} %bitcast.13), calls=%async_computation.3 | async-start | bytes 1572864 | tf_op jit(solution)/shard_map/all_to_all | solution.py:898
  241.1 6.7 %collective-permute-done.41 = bf16[4,96,768]{2,1,0:T(8,128)(2,1)} collective-permute-done((bf16[4,96,768]{2,1,0:T(8,128)(2,1)}, bf16[4,96,768]{2,1,0:T(8,128)(2,1)}, u32[]{:S(2)}, u32[]{:S(2)}) %collective-permute-start.41) | collective-permute-done | bytes 589856 | tf_op jit(solution)/shard_map/ppermute | solution.py:637
  250.0 8.7 %collective-permute-done.31 = bf16[4,96,512]{2,1,0:T(8,128)(2,1)S(1)} collective-permute-done((bf16[4,96,512]{2,1,0:T(8,128)(2,1)S(1)}, bf16[4,96,512]{2,1,0:T(8,128)(2,1)S(1)}, u32[]{:S(2)}, u32[]{:S(2)}) %collective-permute-start.31) | collective-permute-done | bytes 393248 | tf_op jit(solution)/shard_map/ppermute | solution.py:637
  261.4 5.4 %collective-permute-done.27.refs_3_ = bf16[384,768]{1,0:T(8,128)(2,1)} collective-permute-done((bf16[384,768]{1,0:T(8,128)(2,1)}, bf16[384,768]{1,0:T(8,128)(2,1)}, u32[]{:S(2)}, u32[]{:S(2)}) %collective-permute-start.27) | collective-permute-done | bytes 589856 | tf_op jit(solution)/shard_map/ppermute | solution.py:637
  272.9 5.6 %collective-permute-done.47 = bf16[1,96,768]{2,1,0:T(8,128)(2,1)S(1)} collective-permute-done((bf16[1,96,768]{2,1,0:T(8,128)(2,1)S(1)}, bf16[1,96,768]{2,1,0:T(8,128)(2,1)S(1)}, u32[]{:S(2)}, u32[]{:S(2)}) %collective-permute-start.47) | collective-permute-done | bytes 147488 | tf_op jit(solution)/shard_map/ppermute | solution.py:637
  280.9 3.6 %collective-permute-done.32 = bf16[2,96,512]{2,1,0:T(8,128)(2,1)S(1)} collective-permute-done((bf16[2,96,512]{2,1,0:T(8,128)(2,1)S(1)}, bf16[2,96,512]{2,1,0:T(8,128)(2,1)S(1)}, u32[]{:S(2)}, u32[]{:S(2)}) %collective-permute-start.32) | collective-permute-done | bytes 196640 | tf_op jit(solution)/shard_map/ppermute | solution.py:637
  292.8 4.4 %shard_map.356 = (f32[4,384,768]{2,1,0:T(8,128)}, f32[384,192]{1,0:T(8,128)S(1)}) custom-call(s32[2]{0:T(128)S(1)} %pad_add_fusion.refs_0_, bf16[384,768]{1,0:T(8,128)(2,1)} %get-tuple-element.174.refs_1_, bf16[384,768]{1,0:T(8,128)(2,1)S(1)} %collective-permute-done.26.refs_2_, bf16[384,768]{1,0:T(8,128)(2,1)} %collective-permute-done.27.refs_3_, ...), custom_call_target="tpu_custom_call" | custom-call | flops 500000000 | bytes 16777216 | tf_op jit(solution)/shard_map/pallas_call | solution.py:631
  298.2 6.3 %all-to-all-start.4 = ((bf16[8,144,192]{2,1,0:T(8,128)(2,1)}), bf16[8,144,192]{2,1,0:T(8,128)(2,1)S(1)}, u32[]{:S(2)}, u32[]{:S(2)}) async-start(bf16[8,144,192]{2,1,0:T(8,128)(2,1)} %pad_maximum_fusion), calls=%async_computation.4 | async-start | bytes 1179648 | tf_op jit(solution)/shard_map/all_to_all | solution.py:929
  313.1 6.0 %all-to-all-done.4 = bf16[8,144,192]{2,1,0:T(8,128)(2,1)S(1)} async-done(((bf16[8,144,192]{2,1,0:T(8,128)(2,1)}), bf16[8,144,192]{2,1,0:T(8,128)(2,1)S(1)}, u32[]{:S(2)}, u32[]{:S(2)}) %all-to-all-start.4) | async-done | bytes 442400 | tf_op jit(solution)/shard_map/all_to_all | solution.py:929
  319.2 6.7 %all-gather = f32[576,192]{1,0:T(8,128)S(1)} all-gather(f32[144,192]{1,0:T(8,128)S(1)} %convert_reduce_fusion), channel_id=2, replica_groups=mesh['dp'=8,'tensor'=4] {'tensor'}, dimensions={0}, use_global_device_ids=true | all-gather | bytes 552960 | tf_op jit(solution)/shard_map/all_gather | solution.py:931
  330.0 8.2 %collective-permute-done.38 = bf16[1,96,768]{2,1,0:T(8,128)(2,1)S(1)} collective-permute-done((bf16[1,96,768]{2,1,0:T(8,128)(2,1)S(1)}, bf16[1,96,768]{2,1,0:T(8,128)(2,1)S(1)}, u32[]{:S(2)}, u32[]{:S(2)}) %collective-permute-start.38) | collective-permute-done | bytes 147488 | tf_op jit(solution)/shard_map/ppermute | solution.py:637
  (315 shorter events, 144.1 us)
Async XLA Ops:
  22.1 24.3 %all-to-all-start = ((bf16[8,96,256]{2,1,0:T(8,128)(2,1)}), bf16[8,96,256]{2,1,0:T(8,128)(2,1)}, u32[]{:S(2)}, u32[]{:S(2)}) async-start(bf16[8,96,256]{2,1,0:T(8,128)(2,1)} %bitcast.53), calls=%async_computation | async-start | bytes 786432 | tf_op jit(solution)/shard_map/all_to_all | solution.py:772
  30.6 43.4 %collective-permute-start.6 = (bf16[768,768]{1,0:T(8,128)(2,1)}, bf16[768,768]{1,0:T(8,128)(2,1)}, u32[]{:S(2)}, u32[]{:S(2)}) collective-permute-start(bf16[768,768]{1,0:T(8,128)(2,1)} %copy-done.2), channel_id=1, source_target_pairs={{0,1},{1,0},{2,3},{3,2},{4,5},{5,4},{6,7},{7,6},{8,9},{9,8},{10,11... | collective-permute-start | bytes 3538952 | tf_op jit(solution)/shard_map/ppermute | solution.py:637
  34.5 37.6 %collective-permute-start.4 = (bf16[384,768]{1,0:T(8,128)(2,1)}, bf16[384,768]{1,0:T(8,128)(2,1)}, u32[]{:S(2)}, u32[]{:S(2)}) collective-permute-start(bf16[384,768]{1,0:T(8,128)(2,1)} %constant_dynamic-slice_fusion.3), channel_id=1, source_target_pairs={{0,2},{1,3},{2,0},{3,1},{4,6},{5,7},{6,4},{7,5},{8,10},{9,11},{10,... | collective-permute-start | bytes 1769480 | tf_op jit(solution)/shard_map/ppermute | solution.py:637
  46.4 25.7 %collective-permute-start.5 = (bf16[384,768]{1,0:T(8,128)(2,1)}, bf16[384,768]{1,0:T(8,128)(2,1)}, u32[]{:S(2)}, u32[]{:S(2)}) collective-permute-start(bf16[384,768]{1,0:T(8,128)(2,1)} %collective-permute-done.3.refs_4_.refs_7_), channel_id=1, source_target_pairs={{0,4},{4,0},{8,12},{12,8},{16,20},{20,16},{24,28},{28,24},{1,5},{5... | collective-permute-start | bytes 1769480 | tf_op jit(solution)/shard_map/ppermute | solution.py:637
  61.5 42.4 %collective-permute-start.12 = (bf16[768,768]{1,0:T(8,128)(2,1)}, bf16[768,768]{1,0:T(8,128)(2,1)}, u32[]{:S(2)}, u32[]{:S(2)}) collective-permute-start(bf16[768,768]{1,0:T(8,128)(2,1)} %refs_6_), channel_id=1, source_target_pairs={{0,1},{1,0},{2,3},{3,2},{4,5},{5,4},{6,7},{7,6},{8,9},{9,8},{10,11... | collective-permute-start | bytes 3538952 | tf_op jit(solution)/shard_map/ppermute | solution.py:637
  130.9 26.3 %collective-permute-start.19 = (bf16[8,96,768]{2,1,0:T(8,128)(2,1)}, bf16[8,96,768]{2,1,0:T(8,128)(2,1)}, u32[]{:S(2)}, u32[]{:S(2)}) collective-permute-start(bf16[8,96,768]{2,1,0:T(8,128)(2,1)} %get-tuple-element.143), channel_id=1, source_target_pairs={{0,1},{1,0},{2,3},{3,2},{4,5},{5,4},{6,7},{7,6},{8,9},{9,8},{10,11... | collective-permute-start | bytes 3538952 | tf_op jit(solution)/shard_map/ppermute | solution.py:637
  132.5 27.6 %all-to-all-start.2 = ((bf16[8,96,512]{2,1,0:T(8,128)(2,1)}), bf16[8,96,512]{2,1,0:T(8,128)(2,1)}, u32[]{:S(2)}, u32[]{:S(2)}) async-start(bf16[8,96,512]{2,1,0:T(8,128)(2,1)} %bitcast.11), calls=%async_computation.2 | async-start | bytes 1572864 | tf_op jit(solution)/shard_map/all_to_all | solution.py:796
  138.3 21.7 %collective-permute-start.20 = (bf16[512,768]{1,0:T(8,128)(2,1)S(1)}, bf16[512,768]{1,0:T(8,128)(2,1)}, u32[]{:S(2)}, u32[]{:S(2)}) collective-permute-start(bf16[512,768]{1,0:T(8,128)(2,1)S(1)} %copy-done.4), channel_id=1, source_target_pairs={{0,2},{1,3},{2,0},{3,1},{4,6},{5,7},{6,4},{7,5},{8,10},{9,11},{10,... | collective-permute-start | bytes 2359304 | tf_op jit(solution)/shard_map/ppermute | solution.py:637
  157.1 20.7 %collective-permute-start.22 = (bf16[8,96,768]{2,1,0:T(8,128)(2,1)}, bf16[8,96,768]{2,1,0:T(8,128)(2,1)}, u32[]{:S(2)}, u32[]{:S(2)}) collective-permute-start(bf16[8,96,768]{2,1,0:T(8,128)(2,1)} %get-tuple-element.156), channel_id=1, source_target_pairs={{0,1},{1,0},{2,3},{3,2},{4,5},{5,4},{6,7},{7,6},{8,9},{9,8},{10,11... | collective-permute-start | bytes 3538952 | tf_op jit(solution)/shard_map/ppermute | solution.py:637
  160.0 40.0 %collective-permute-start.23 = (bf16[8,96,768]{2,1,0:T(8,128)(2,1)}, bf16[8,96,768]{2,1,0:T(8,128)(2,1)}, u32[]{:S(2)}, u32[]{:S(2)}) collective-permute-start(bf16[8,96,768]{2,1,0:T(8,128)(2,1)} %add_convert_fusion.2), channel_id=1, source_target_pairs={{0,2},{1,3},{2,0},{3,1},{4,6},{5,7},{6,4},{7,5},{8,10},{9,11},{10,... | collective-permute-start | bytes 3538952 | tf_op jit(solution)/shard_map/ppermute | solution.py:637
  176.8 27.3 %collective-permute-start.25 = (bf16[8,96,768]{2,1,0:T(8,128)(2,1)}, bf16[8,96,768]{2,1,0:T(8,128)(2,1)}, u32[]{:S(2)}, u32[]{:S(2)}) collective-permute-start(bf16[8,96,768]{2,1,0:T(8,128)(2,1)} %get-tuple-element.173), channel_id=1, source_target_pairs={{0,1},{1,0},{2,3},{3,2},{4,5},{5,4},{6,7},{7,6},{8,9},{9,8},{10,11... | collective-permute-start | bytes 3538952 | tf_op jit(solution)/shard_map/ppermute | solution.py:637
  177.2 30.0 %collective-permute-start.44 = (bf16[8,96,768]{2,1,0:T(8,128)(2,1)}, bf16[8,96,768]{2,1,0:T(8,128)(2,1)S(1)}, u32[]{:S(2)}, u32[]{:S(2)}) collective-permute-start(bf16[8,96,768]{2,1,0:T(8,128)(2,1)} %get-tuple-element.191), channel_id=1, source_target_pairs={{0,1},{1,0},{2,3},{3,2},{4,5},{5,4},{6,7},{7,6},{8,9},{9,8},{10,11... | collective-permute-start | bytes 3538952 | tf_op jit(solution)/shard_map/ppermute | solution.py:637
  177.7 32.5 %collective-permute-start.39 = (bf16[8,96,768]{2,1,0:T(8,128)(2,1)}, bf16[8,96,768]{2,1,0:T(8,128)(2,1)S(1)}, u32[]{:S(2)}, u32[]{:S(2)}) collective-permute-start(bf16[8,96,768]{2,1,0:T(8,128)(2,1)} %get-tuple-element.188), channel_id=1, source_target_pairs={{0,1},{1,0},{2,3},{3,2},{4,5},{5,4},{6,7},{7,6},{8,9},{9,8},{10,11... | collective-permute-start | bytes 3538952 | tf_op jit(solution)/shard_map/ppermute | solution.py:637
  182.7 31.6 %collective-permute-start.40 = (bf16[8,96,768]{2,1,0:T(8,128)(2,1)S(1)}, bf16[8,96,768]{2,1,0:T(8,128)(2,1)S(1)}, u32[]{:S(2)}, u32[]{:S(2)}) collective-permute-start(bf16[8,96,768]{2,1,0:T(8,128)(2,1)S(1)} %add_convert_fusion.1), channel_id=1, source_target_pairs={{0,2},{1,3},{2,0},{3,1},{4,6},{5,7},{6,4},{7,5},{8,10},{9,11},{10,... | collective-permute-start | bytes 3538952 | tf_op jit(solution)/shard_map/ppermute | solution.py:637
  214.3 23.3 %collective-permute-start.45 = (bf16[4,96,768]{2,1,0:T(8,128)(2,1)}, bf16[4,96,768]{2,1,0:T(8,128)(2,1)}, u32[]{:S(2)}, u32[]{:S(2)}) collective-permute-start(bf16[4,96,768]{2,1,0:T(8,128)(2,1)} %add_convert_fusion.3), channel_id=1, source_target_pairs={{0,4},{4,0},{8,12},{12,8},{16,20},{20,16},{24,28},{28,24},{1,5},{5... | collective-permute-start | bytes 1769480 | tf_op jit(solution)/shard_map/ppermute | solution.py:637
  218.6 29.2 %collective-permute-start.41 = (bf16[4,96,768]{2,1,0:T(8,128)(2,1)}, bf16[4,96,768]{2,1,0:T(8,128)(2,1)}, u32[]{:S(2)}, u32[]{:S(2)}) collective-permute-start(bf16[4,96,768]{2,1,0:T(8,128)(2,1)} %add_convert_fusion.4), channel_id=1, source_target_pairs={{0,4},{4,0},{8,12},{12,8},{16,20},{20,16},{24,28},{28,24},{1,5},{5... | collective-permute-start | bytes 1769480 | tf_op jit(solution)/shard_map/ppermute | solution.py:637
  221.4 67.6 %collective-permute-start.34 = (bf16[8,96,768]{2,1,0:T(8,128)(2,1)}, bf16[8,96,768]{2,1,0:T(8,128)(2,1)}, u32[]{:S(2)}, u32[]{:S(2)}) collective-permute-start(bf16[8,96,768]{2,1,0:T(8,128)(2,1)} %get-tuple-element.185), channel_id=1, source_target_pairs={{0,1},{1,0},{2,3},{3,2},{4,5},{5,4},{6,7},{7,6},{8,9},{9,8},{10,11... | collective-permute-start | bytes 3538952 | tf_op jit(solution)/shard_map/ppermute | solution.py:637
  225.5 63.6 %collective-permute-start.35 = (bf16[8,96,768]{2,1,0:T(8,128)(2,1)}, bf16[8,96,768]{2,1,0:T(8,128)(2,1)}, u32[]{:S(2)}, u32[]{:S(2)}) collective-permute-start(bf16[8,96,768]{2,1,0:T(8,128)(2,1)} %add_convert_fusion), channel_id=1, source_target_pairs={{0,2},{1,3},{2,0},{3,1},{4,6},{5,7},{6,4},{7,5},{8,10},{9,11},{10,... | collective-permute-start | bytes 3538952 | tf_op jit(solution)/shard_map/ppermute | solution.py:637
  225.9 41.0 %collective-permute-start.27 = (bf16[384,768]{1,0:T(8,128)(2,1)}, bf16[384,768]{1,0:T(8,128)(2,1)}, u32[]{:S(2)}, u32[]{:S(2)}) collective-permute-start(bf16[384,768]{1,0:T(8,128)(2,1)} %get-tuple-element.174.refs_1_), channel_id=1, source_target_pairs={{0,2},{1,3},{2,0},{3,1},{4,6},{5,7},{6,4},{7,5},{8,10},{9,11},{10,... | collective-permute-start | bytes 1769480 | tf_op jit(solution)/shard_map/ppermute | solution.py:637
  232.8 65.4 %all-to-all-start.3 = ((bf16[8,96,512]{2,1,0:T(8,128)(2,1)}), bf16[8,96,512]{2,1,0:T(8,128)(2,1)S(1)}, u32[]{:S(2)}, u32[]{:S(2)}) async-start(bf16[8,96,512]{2,1,0:T(8,128)(2,1)} %bitcast.13), calls=%async_computation.3 | async-start | bytes 1572864 | tf_op jit(solution)/shard_map/all_to_all | solution.py:898
  237.6 21.1 %collective-permute-start.31 = (bf16[4,96,512]{2,1,0:T(8,128)(2,1)S(1)}, bf16[4,96,512]{2,1,0:T(8,128)(2,1)S(1)}, u32[]{:S(2)}, u32[]{:S(2)}) collective-permute-start(bf16[4,96,512]{2,1,0:T(8,128)(2,1)S(1)} %slice.296), channel_id=1, source_target_pairs={{0,4},{4,0},{8,12},{12,8},{16,20},{20,16},{24,28},{28,24},{1,5},{5... | collective-permute-start | bytes 1179656 | tf_op jit(solution)/shard_map/ppermute | solution.py:637
  266.8 25.1 %collective-permute-start.26 = (bf16[384,768]{1,0:T(8,128)(2,1)}, bf16[384,768]{1,0:T(8,128)(2,1)S(1)}, u32[]{:S(2)}, u32[]{:S(2)}) collective-permute-start(bf16[384,768]{1,0:T(8,128)(2,1)} %get-tuple-element.174.refs_1_), channel_id=1, source_target_pairs={{0,1},{1,0},{2,3},{3,2},{4,5},{5,4},{6,7},{7,6},{8,9},{9,8},{10,11... | collective-permute-start | bytes 1769480 | tf_op jit(solution)/shard_map/ppermute | solution.py:637
  266.8 25.1 %collective-permute-start.28 = (bf16[384,768]{1,0:T(8,128)(2,1)}, bf16[384,768]{1,0:T(8,128)(2,1)S(1)}, u32[]{:S(2)}, u32[]{:S(2)}) collective-permute-start(bf16[384,768]{1,0:T(8,128)(2,1)} %collective-permute-done.27.refs_3_), channel_id=1, source_target_pairs={{0,1},{1,0},{2,3},{3,2},{4,5},{5,4},{6,7},{7,6},{8,9},{9,8},{10,11... | collective-permute-start | bytes 1769480 | tf_op jit(solution)/shard_map/ppermute | solution.py:637
  298.2 20.9 %all-to-all-start.4 = ((bf16[8,144,192]{2,1,0:T(8,128)(2,1)}), bf16[8,144,192]{2,1,0:T(8,128)(2,1)S(1)}, u32[]{:S(2)}, u32[]{:S(2)}) async-start(bf16[8,144,192]{2,1,0:T(8,128)(2,1)} %pad_maximum_fusion), calls=%async_computation.4 | async-start | bytes 1179648 | tf_op jit(solution)/shard_map/all_to_all | solution.py:929
  (103 other events, 965.6 us)
